TPU v7x, 32 devices: a whole 2x2x4 slice. The times are simulated.
32 devices in a mesh: rep: 16 (over z, x, core), fsdp: 2 (over y).
Axes of the slice: x: 2, y: 2, z: 4, core: 2. Of those that a mesh axis runs over, the one named last changes fastest.
Arguments:
- hidden_in: bfloat16 [8192, 1024], P(('rep', 'fsdp')), may hold values from -6 to 6
- routes: int32 [8192, 8], P(('rep', 'fsdp')), may hold values from 0 to 15, all different within a row; in each aligned block of 256 rows (0 to 255, 256 to 511, ...) at most 160 rows name the same one
- w_qkv: bfloat16 [1024, 2048], P('fsdp'), may hold values from -0.1875 to 0.1875
- w_out: bfloat16 [1024, 1024], P('fsdp'), may hold values from -2 to 2
- w_router: bfloat16 [1024, 16], P('fsdp'), may hold values from -0.09375 to 0.09375
- attn_gain: bfloat16 [1024], P('fsdp'), may hold values from 0.5 to 1.5
- ffn_gain: bfloat16 [1024], P('fsdp'), may hold values from 0.5 to 1.5
- w_gate_up: bfloat16 [16, 1024, 1024], P('fsdp'), may hold values from -0.1875 to 0.1875
- w_down: bfloat16 [16, 1024, 512], P('fsdp'), may hold values from -2 to 2
- cotangent: bfloat16 [8192, 1024], P(('rep', 'fsdp')), may hold values from -6 to 6
Outputs:
- layer_out: bfloat16 [8192, 1024], P(('rep', 'fsdp'))
- grad_in: float32 [8192, 1024], P(('rep', 'fsdp'))
- grad_w_qkv: float32 [1024, 2048], P('fsdp')
- grad_w_out: float32 [1024, 1024], P('fsdp')
- grad_w_router: float32 [1024, 16], P('fsdp')
- grad_attn_gain: float32 [1024], P('fsdp')
- grad_ffn_gain: float32 [1024], P('fsdp')
- grad_w_gate_up: float32 [16, 1024, 1024], P('fsdp')
- grad_w_down: float32 [16, 1024, 512], P('fsdp')
Inputs may be any that keep to these rules, and one draw needn't show every extreme that they name: `routes`: each row names 8 different experts. Within the 256 rows of one device no expert is named by more than 160 rows, and in every draw some expert is named by exactly 160 rows of some device.
All inputs are finite; a program needn't handle non-finite values.
Results may differ from a plain program's by a relative error of at most 0.023.
Values may be sent and summed in bfloat16 or wider, within the bound.
No kernel may reach another device: no remote copies, remote signals or barrier semaphores. Data moves between devices by JAX's collectives and lax.ppermute only.
A program may use at most 448 MiB of HBM per device.

v0:
```python
from functools import partial

import jax
import jax.numpy as jnp
from jax import lax
from jax.sharding import PartitionSpec as P

D = 1024
HEADS = 16
KV_HEADS = 8
HEAD_DIM = 64
F = 512
TOP = 8
EXPERTS = 16
BLOCK = 256
CAP = 160


norm_eps = 1e-06
masked_score = -1e30
weight_forms = ("ecd,edf->ecf", "ecf,edf->ecd", "ecd,ecf->edf")


def shifted(value, axis, steps):
    count = lax.axis_size(axis)
    initial, last = (max(0, -steps), min(count, count - steps))
    return lax.ppermute(value, axis, [(source, source + steps) for source in range(initial, last)])


def normalize(input_rows):
    scale_inv = lax.rsqrt(jnp.mean(input_rows * input_rows, -1, keepdims=True) + norm_eps)
    return (input_rows * scale_inv, scale_inv)


def norm_back(normed, scale_inv, grad_normed):
    return scale_inv * (grad_normed - normed * jnp.mean(grad_normed * normed, -1, keepdims=True))


def rotate(values):
    middle = values.shape[-1] // 2
    return jnp.concatenate([-values[..., middle:], values[..., :middle]], -1)


def rotate_back(values):
    middle = values.shape[-1] // 2
    return jnp.concatenate([values[..., middle:], -values[..., :middle]], -1)


def rotary_tables(places, head_width):
    middle = head_width // 2
    place_values = places.astype(jnp.float32)
    frequency = 10000.0 ** (-(2.0 * jnp.arange(middle, dtype=jnp.float32)) / head_width)
    angles = place_values[:, None] * frequency[None, :]
    cosine_table = jnp.concatenate([jnp.cos(angles), jnp.cos(angles)], -1)
    sine_table = jnp.concatenate([jnp.sin(angles), jnp.sin(angles)], -1)
    return (cosine_table[:, None, :], sine_table[:, None, :])


def slot_tables(route_rows):
    length = route_rows.shape[0]
    assigned = route_rows.reshape(-1)
    one_hot = (assigned[:, None] == jnp.arange(EXPERTS, dtype=jnp.int32)[None, :]).astype(jnp.int32)
    earlier = jnp.cumsum(one_hot, 0) - one_hot
    position = jnp.sum(earlier * one_hot, 1)
    target = assigned * CAP + position
    slot_owner = (
        jnp.full((EXPERTS * CAP,), length * TOP, jnp.int32)
        .at[target]
        .set(jnp.arange(length * TOP, dtype=jnp.int32))
    )
    return (target, slot_owner)


def attend_group(pieces, allowed, score_scale):
    query_group, key_group, value_group = pieces
    scores = (
        jnp.einsum("qrd,kd->rqk", query_group, key_group, preferred_element_type=jnp.float32)
        * score_scale
    )
    scores = jnp.where(allowed[None], scores, masked_score)
    largest = jnp.max(scores, -1, keepdims=True)
    exponent = jnp.exp(scores - largest)
    totals = jnp.sum(exponent, -1, keepdims=True)
    attn_probs = (exponent / totals).astype(jnp.bfloat16)
    output = jnp.einsum("rqk,kd->qrd", attn_probs, value_group, preferred_element_type=jnp.float32)
    return (output, (largest + jnp.log(totals))[..., 0])


def attend_back(pieces, allowed, score_scale):
    query_group, key_group, value_group, grad_group, log_total = pieces
    scores = (
        jnp.einsum("qrd,kd->rqk", query_group, key_group, preferred_element_type=jnp.float32)
        * score_scale
    )
    scores = jnp.where(allowed[None], scores, masked_score)
    attn_probs = jnp.exp(scores - log_total[..., None])
    probs_low = attn_probs.astype(jnp.bfloat16)
    grad_value = jnp.einsum(
        "rqk,qrd->kd", probs_low, grad_group, preferred_element_type=jnp.float32
    )
    grad_probs = jnp.einsum(
        "qrd,kd->rqk", grad_group, value_group, preferred_element_type=jnp.float32
    )
    grad_scores = (
        attn_probs * (grad_probs - jnp.sum(attn_probs * grad_probs, -1, keepdims=True))
    ).astype(jnp.bfloat16)
    grad_query = (
        jnp.einsum("rqk,kd->qrd", grad_scores, key_group, preferred_element_type=jnp.float32)
        * score_scale
    )
    grad_key = (
        jnp.einsum("rqk,qrd->kd", grad_scores, query_group, preferred_element_type=jnp.float32)
        * score_scale
    )
    return (grad_query, grad_key, grad_value)


def expert_out(slot_rows, gate_up_w, down_w, forms):
    gate_up = jnp.einsum(forms[0], slot_rows, gate_up_w, preferred_element_type=jnp.float32)
    hidden_width = down_w.shape[-1]
    hidden = (jax.nn.silu(gate_up[..., :hidden_width]) * gate_up[..., hidden_width:]).astype(
        jnp.bfloat16
    )
    return jnp.einsum(forms[1], hidden, down_w, preferred_element_type=jnp.float32).astype(
        jnp.bfloat16
    )


def expert_back(slot_rows, grad_rows, gate_up_w, down_w, forms):
    gate_up = jnp.einsum(forms[0], slot_rows, gate_up_w, preferred_element_type=jnp.float32)
    hidden_width = down_w.shape[-1]
    gate_part = gate_up[..., :hidden_width]
    up_part = gate_up[..., hidden_width:]
    sigmoid_g = jax.nn.sigmoid(gate_part)
    silu_g = gate_part * sigmoid_g
    hidden = (silu_g * up_part).astype(jnp.bfloat16)
    grad_hidden = jnp.einsum(forms[0], grad_rows, down_w, preferred_element_type=jnp.float32)
    grad_gate_up = jnp.concatenate(
        [
            grad_hidden * up_part * sigmoid_g * (1.0 + gate_part * (1.0 - sigmoid_g)),
            grad_hidden * silu_g,
        ],
        -1,
    ).astype(jnp.bfloat16)
    grad_slots = jnp.einsum(forms[1], grad_gate_up, gate_up_w, preferred_element_type=jnp.float32)
    return (grad_slots, grad_gate_up, hidden)


def body(
    hidden_in, routes, w_qkv, w_out, w_router, attn_gain, ffn_gain, w_gate_up, w_down, cotangent
):
    length = hidden_in.shape[0]
    groups = HEADS // KV_HEADS
    query_width = HEADS * HEAD_DIM
    key_width = KV_HEADS * HEAD_DIM
    score_scale = HEAD_DIM ** (-0.5)
    parity = lax.axis_index("fsdp") % 2
    local_rows = jnp.arange(length, dtype=jnp.int32)
    places = parity * length + local_rows
    query_block = places // BLOCK
    earlier_block = jnp.where(parity == 1, local_rows // BLOCK, 4 * length)
    key_block = jnp.concatenate([earlier_block, query_block], 0)
    allowed = key_block[None, :] <= query_block[:, None]
    cosine_table, sine_table = rotary_tables(places, HEAD_DIM)
    full_qkv, full_out, full_router, gain_attn, gain_ffn = (
        lax.all_gather(w_qkv, "fsdp", axis=0, tiled=True),
        lax.all_gather(w_out, "fsdp", axis=0, tiled=True),
        lax.all_gather(w_router, "fsdp", axis=0, tiled=True),
        lax.all_gather(attn_gain, "fsdp", axis=0, tiled=True),
        lax.all_gather(ffn_gain, "fsdp", axis=0, tiled=True),
    )
    input_rows = hidden_in.astype(jnp.float32)
    normed_one, inverse_one = normalize(input_rows)
    input_one = (normed_one * gain_attn).astype(jnp.bfloat16)
    qkv_proj = jnp.dot(input_one, full_qkv, preferred_element_type=jnp.float32)
    query_raw = qkv_proj[:, :query_width].reshape(length, HEADS, HEAD_DIM)
    key_raw = qkv_proj[:, query_width : query_width + key_width].reshape(length, KV_HEADS, HEAD_DIM)
    queries = (query_raw * cosine_table + rotate(query_raw) * sine_table).astype(jnp.bfloat16)
    key_flat = (
        (key_raw * cosine_table + rotate(key_raw) * sine_table)
        .astype(jnp.bfloat16)
        .reshape(length, key_width)
    )
    value_flat = qkv_proj[:, query_width + key_width :].astype(jnp.bfloat16)
    key_prev, value_prev = shifted((key_flat, value_flat), "fsdp", 1)
    all_keys = jnp.concatenate([key_prev, key_flat], 0).reshape(2 * length, KV_HEADS, HEAD_DIM)
    all_values = jnp.concatenate([value_prev, value_flat], 0).reshape(
        2 * length, KV_HEADS, HEAD_DIM
    )
    query_groups = jnp.transpose(queries.reshape(length, KV_HEADS, groups, HEAD_DIM), (1, 0, 2, 3))
    key_groups = jnp.transpose(all_keys, (1, 0, 2))
    value_groups = jnp.transpose(all_values, (1, 0, 2))
    attended, log_totals = lax.map(
        partial(attend_group, allowed=allowed, score_scale=score_scale),
        (query_groups, key_groups, value_groups),
    )
    attended = (
        jnp.transpose(attended, (1, 0, 2, 3)).reshape(length, query_width).astype(jnp.bfloat16)
    )
    residual = input_rows + jnp.dot(attended, full_out, preferred_element_type=jnp.float32)
    normed_two, inverse_two = normalize(residual)
    input_two = (normed_two * gain_ffn).astype(jnp.bfloat16)
    logits = jnp.dot(input_two, full_router, preferred_element_type=jnp.float32)
    router = jax.nn.softmax(logits, -1)
    gate_vals = jnp.take_along_axis(router, routes, 1)
    target, slot_owner = slot_tables(routes)
    token_of = slot_owner // TOP
    padded = jnp.concatenate([input_two, jnp.zeros((1, D), jnp.bfloat16)], 0)
    slotted = padded[token_of].reshape(EXPERTS, CAP, D)
    pieces = lax.all_gather((w_gate_up, w_down), "fsdp", axis=0, tiled=True)
    piece_rows = slotted
    expert_rows = expert_out(piece_rows, pieces[0], pieces[1], weight_forms)
    picked = (
        expert_rows.reshape(EXPERTS * CAP, D)[target].reshape(length, TOP, D).astype(jnp.float32)
    )
    mixture = jnp.sum(gate_vals[:, :, None] * picked, 1)
    layer_out = (residual + mixture).astype(jnp.bfloat16)
    back_qkv, back_out, back_router, back_attn_gain, back_ffn_gain = (
        lax.all_gather(w_qkv, "fsdp", axis=0, tiled=True),
        lax.all_gather(w_out, "fsdp", axis=0, tiled=True),
        lax.all_gather(w_router, "fsdp", axis=0, tiled=True),
        lax.all_gather(attn_gain, "fsdp", axis=0, tiled=True),
        lax.all_gather(ffn_gain, "fsdp", axis=0, tiled=True),
    )
    grad_out = cotangent.astype(jnp.float32)
    grad_gates = jnp.sum(grad_out[:, None, :] * picked, -1)
    gate_flat = jnp.concatenate([gate_vals.reshape(-1), jnp.zeros((1,), jnp.float32)], 0)
    grad_pad = jnp.concatenate([grad_out, jnp.zeros((1, D), jnp.float32)], 0)
    grad_expert = (
        (gate_flat[slot_owner][:, None] * grad_pad[token_of])
        .astype(jnp.bfloat16)
        .reshape(EXPERTS, CAP, D)
    )
    pieces = lax.all_gather((w_gate_up, w_down), "fsdp", axis=0, tiled=True)
    piece_rows = slotted
    piece_grads = grad_expert
    grad_slotted, grad_gate_up, hidden = expert_back(
        piece_rows, piece_grads, pieces[0], pieces[1], weight_forms
    )
    piece_rows = slotted
    piece_grads = grad_expert
    expert_terms = lax.psum_scatter(
        jnp.concatenate(
            [
                jnp.einsum(
                    weight_forms[2], piece_rows, grad_gate_up, preferred_element_type=jnp.float32
                ),
                jnp.einsum(
                    weight_forms[2], piece_grads, hidden, preferred_element_type=jnp.float32
                ),
            ],
            -1,
        ).astype(jnp.bfloat16),
        "fsdp",
        scatter_dimension=0,
        tiled=True,
    ).astype(jnp.float32)
    grad_gu_own = expert_terms[..., : 2 * F]
    grad_down_own = expert_terms[..., 2 * F :]
    grad_slot_rows = grad_slotted.reshape(EXPERTS * CAP, D)[target].reshape(length, TOP, D)
    expert_ids = jnp.arange(EXPERTS, dtype=jnp.int32)[None, None, :]
    grad_router = jnp.sum(
        grad_gates[:, :, None] * (routes[:, :, None] == expert_ids).astype(jnp.float32), 1
    )
    grad_logits = (
        router * (grad_router - jnp.sum(router * grad_router, -1, keepdims=True))
    ).astype(jnp.bfloat16)
    grad_input_two = jnp.sum(grad_slot_rows, 1) + jnp.dot(
        grad_logits, back_router.T, preferred_element_type=jnp.float32
    )
    grad_w_router = jnp.dot(input_two.T, grad_logits, preferred_element_type=jnp.float32)
    grad_ffn_gain = jnp.sum(grad_input_two * normed_two, 0)
    grad_residual = grad_out + norm_back(normed_two, inverse_two, grad_input_two * back_ffn_gain)
    grad_attn = grad_residual.astype(jnp.bfloat16)
    grad_w_out = jnp.dot(attended.T, grad_attn, preferred_element_type=jnp.float32)
    grad_attended = jnp.dot(grad_attn, back_out.T, preferred_element_type=jnp.float32).astype(
        jnp.bfloat16
    )
    grad_groups = jnp.transpose(
        grad_attended.reshape(length, KV_HEADS, groups, HEAD_DIM), (1, 0, 2, 3)
    )
    grad_query, grad_key, grad_value = lax.map(
        partial(attend_back, allowed=allowed, score_scale=score_scale),
        (query_groups, key_groups, value_groups, grad_groups, log_totals),
    )
    grad_query = jnp.transpose(grad_query, (1, 0, 2, 3)).reshape(length, HEADS, HEAD_DIM)
    grad_key = jnp.transpose(grad_key, (1, 0, 2)).reshape(2 * length, key_width)
    grad_value = jnp.transpose(grad_value, (1, 0, 2)).reshape(2 * length, key_width)
    key_later, value_later = (
        shifted(grad_key[:length].astype(jnp.bfloat16), "fsdp", -1).astype(jnp.float32),
        shifted(grad_value[:length].astype(jnp.bfloat16), "fsdp", -1).astype(jnp.float32),
    )
    grad_key = (grad_key[length:] + key_later).reshape(length, KV_HEADS, HEAD_DIM)
    grad_value = grad_value[length:] + value_later
    query_back = grad_query * cosine_table + rotate_back(grad_query * sine_table)
    key_back = grad_key * cosine_table + rotate_back(grad_key * sine_table)
    grad_qkv = jnp.concatenate(
        [query_back.reshape(length, query_width), key_back.reshape(length, key_width), grad_value],
        -1,
    ).astype(jnp.bfloat16)
    grad_w_qkv = jnp.dot(input_one.T, grad_qkv, preferred_element_type=jnp.float32)
    grad_input_one = jnp.dot(grad_qkv, back_qkv.T, preferred_element_type=jnp.float32)
    grad_attn_gain = jnp.sum(grad_input_one * normed_one, 0)
    grad_in = grad_residual + norm_back(normed_one, inverse_one, grad_input_one * back_attn_gain)
    owned_qkv, owned_out, owned_router, owned_attn_gain, owned_ffn_gain = (
        lax.psum_scatter(
            grad_w_qkv.astype(jnp.bfloat16), "fsdp", scatter_dimension=0, tiled=True
        ).astype(jnp.float32),
        lax.psum_scatter(
            grad_w_out.astype(jnp.bfloat16), "fsdp", scatter_dimension=0, tiled=True
        ).astype(jnp.float32),
        lax.psum_scatter(
            grad_w_router.astype(jnp.bfloat16), "fsdp", scatter_dimension=0, tiled=True
        ).astype(jnp.float32),
        lax.psum_scatter(
            grad_attn_gain.astype(jnp.bfloat16), "fsdp", scatter_dimension=0, tiled=True
        ).astype(jnp.float32),
        lax.psum_scatter(
            grad_ffn_gain.astype(jnp.bfloat16), "fsdp", scatter_dimension=0, tiled=True
        ).astype(jnp.float32),
    )
    summed = (
        lax.psum(owned_qkv.astype(jnp.bfloat16), "rep").astype(jnp.float32),
        lax.psum(owned_out.astype(jnp.bfloat16), "rep").astype(jnp.float32),
        lax.psum(owned_router.astype(jnp.bfloat16), "rep").astype(jnp.float32),
        lax.psum(owned_attn_gain.astype(jnp.bfloat16), "rep").astype(jnp.float32),
        lax.psum(owned_ffn_gain.astype(jnp.bfloat16), "rep").astype(jnp.float32),
        lax.psum(grad_gu_own.astype(jnp.bfloat16), "rep").astype(jnp.float32),
        lax.psum(grad_down_own.astype(jnp.bfloat16), "rep").astype(jnp.float32),
    )
    return (
        layer_out,
        grad_in,
        summed[0],
        summed[1],
        summed[2],
        summed[3],
        summed[4],
        summed[5],
        summed[6],
    )


def solution(mesh):
    in_specs = (
        P(("rep", "fsdp"), None),
        P(("rep", "fsdp"), None),
        P("fsdp", None),
        P("fsdp", None),
        P("fsdp", None),
        P("fsdp"),
        P("fsdp"),
        P("fsdp", None, None),
        P("fsdp", None, None),
        P(("rep", "fsdp"), None),
    )
    out_specs = (
        P(("rep", "fsdp"), None),
        P(("rep", "fsdp"), None),
        P("fsdp", None),
        P("fsdp", None),
        P("fsdp", None),
        P("fsdp"),
        P("fsdp"),
        P("fsdp", None, None),
        P("fsdp", None, None),
    )
    return jax.shard_map(body, mesh=mesh, in_specs=in_specs, out_specs=out_specs, check_vma=False)
```

profile of v0, /device:TPU:0, one launch (start us, length us, event | category | flops | bytes accessed | tf_op | source)
XLA Modules:
  0.0 1995.1 jit_solution(15569543793549782783)
XLA Ops:
  50.0 19.5 all-gather.7.cloned.1.call-done
  88.1 20.1 %collective-permute-done = bf16[256,512]{1,0:T(8,128)(2,1)} collective-permute-done((bf16[256,512]{1,0:T(8,128)(2,1)}, bf16[256,512]{1,0:T(8,128)(2,1)}, u32[]{:S(2)}, u32[]{:S(2)}) %collective-permute-start) | collective-permute-done | bytes 262176 | tf_op jit(solution)/shard_map/ppermute | solution.py:27
  111.6 12.7 while.30
  138.6 16.8 gather_fusion.5
  156.6 13.6 gather_fusion.2
  170.3 335.3 %all-gather.11.cloned.1.call-done = bf16[16,1024,1024]{2,1,0:T(8,128)(2,1)} async-done(((bf16[8,1024,1024]{2,1,0:T(8,128)(2,1)}), bf16[16,1024,1024]{2,1,0:T(8,128)(2,1)}) %all-gather.11.cloned.1.call-update) | async-done | bytes 33554448 | tf_op jit(solution)/shard_map/all_gather | solution.py:210
  505.5 23.0 %fusion.98 = f32[16,160,1024]{2,1,0:T(8,128)} fusion(bf16[16,160,1024]{2,1,0:T(8,128)(2,1)} %bitcast.262, bf16[16,1024,1024]{2,1,0:T(8,128)(2,1)} %all-gather.11.cloned.1.call-done), kind=kOutput, calls=%fused_computation.210 | convolution fusion | flops 5368709120 | bytes 49283072 | tf_op jit(solution)/shard_map/ecd,edf->ecf/dot_general | solution.py:119
  528.5 177.3 %all-gather.13.cloned.1.call-done = bf16[16,1024,512]{2,1,0:T(8,128)(2,1)} async-done(((bf16[8,1024,512]{2,1,0:T(8,128)(2,1)}), bf16[16,1024,512]{2,1,0:T(8,128)(2,1)}) %all-gather.13.cloned.1.call-update) | async-done | bytes 16777232 | tf_op jit(solution)/shard_map/all_gather | solution.py:210
  705.8 17.3 multiply_convert_fusion.3
  734.3 17.7 convolution_convert_fusion
  752.0 35.6 %pad_maximum_fusion = bf16[16,1024,1536]{1,2,0:T(8,128)(2,1)} fusion(bf16[16,1024,512]{1,2,0:T(8,128)(2,1)} %convolution_convert_fusion.1, bf16[16,1024,1024]{1,2,0:T(8,128)(2,1)} %convolution_convert_fusion), kind=kLoop, calls=%fused_computation.69 | loop fusion | flops 100663296 | bytes 100663296 | tf_op jit(solution)/shard_map/concatenate | solution.py:243
  789.8 21.4 %fusion.52 = f32[16,160,1024]{2,1,0:T(8,128)} fusion(bf16[16,1024,1024]{2,1,0:T(8,128)(2,1)} %all-gather.11.cloned.1.call-done, bf16[16,160,512]{2,1,0:T(8,128)(2,1)} %get-tuple-element.264, bf16[16,160,512]{2,1,0:T(8,128)(2,1)} %get-tuple-element.263), kind=kOutput, calls=%fused_computation.85 | convolution fusion | flops 5379194880 | bytes 49283072 | tf_op jit(solution)/shard_map/ecf,edf->ecd/dot_general | solution.py:145
  811.2 15.9 gather_fusion.4
  837.7 14.5 gather_fusion.1
  871.1 58.2 %while.31 = (s32[]{:T(128)}, f32[8,256,2,64]{1,3,2,0:T(8,128)S(1)}, f32[8,512,64]{1,2,0:T(8,128)}, f32[8,512,64]{1,2,0:T(8,128)}, bf16[8,512,64]{1,2,0:T(8,128)(...) while((s32[]{:T(128)}, f32[8,256,2,64]{1,3,2,0:T(8,128)S(1)}, ...), condition=%wide.region_20.21_spmd.clone.clone, body=%wide.region_18.20_spmd.clone.sunk.clone | while | flops 170327552 | bytes 8996985 | solution.py:282
  938.6 22.9 %collective-permute-done.2 = bf16[256,512]{0,1:T(8,128)(2,1)S(1)} collective-permute-done((bf16[256,512]{0,1:T(8,128)(2,1)S(1)}, bf16[256,512]{0,1:T(8,128)(2,1)S(1)}, u32[]{:S(2)}, u32[]{:S(2)}) %collective-permute-start.2) | collective-permute-done | bytes 262176 | tf_op jit(solution)/shard_map/ppermute | solution.py:27
  966.4 381.6 %reduce-scatter.11.cloned.1.call-done = bf16[8,1024,1536]{1,2,0:T(8,128)(2,1)} async-done(((bf16[16,1024,1536]{1,2,0:T(8,128)(2,1)}), bf16[8,1024,1536]{1,2,0:T(8,128)(2,1)}) %reduce-scatter.11.cloned.1.call-update) | async-done | bytes 25165840 | tf_op jit(solution)/shard_map/reduce_scatter | solution.py:242
  1348.0 14.0 slice.132
  1369.8 12.8 reduce-scatter.7.cloned.1.call-done
  1382.5 57.3 %reduce-scatter.5.cloned.1.call-done = bf16[512,2048]{1,0:T(8,128)(2,1)} async-done(((bf16[1024,2048]{1,0:T(8,128)(2,1)}), bf16[512,2048]{1,0:T(8,128)(2,1)}) %reduce-scatter.5.cloned.1.call-update) | async-done | bytes 2097168 | tf_op jit(solution)/shard_map/reduce_scatter | solution.py:306
  1452.5 64.1 %all-reduce.4 = (bf16[512,16]{0,1:T(8,128)(2,1)S(1)}, bf16[512]{0:T(512)(128)(2,1)S(1)}, bf16[512]{0:T(512)(128)(2,1)S(1)}) all-reduce(bf16[512,16]{0,1:T(8,128)(2,1)} %reduce-scatter.9.cloned.1.call-done, bf16[512]{0:T(512)(128)(2,1)S(1)} %dynamic-slice.1, ...), channel_id=1, replica_groups=mesh['rep'=16,'fsdp'=2] {'rep'}, use_global_device_ids=true, to_apply=%region_27.28 | all-reduce | flops 9216 | bytes 36864 | tf_op jit(solution)/shard_map/psum | solution.py:325
  1519.6 426.8 %all-reduce.9.cloned.1.call-done = (bf16[8,1024,1024]{1,2,0:T(8,128)(2,1)}, bf16[8,1024,512]{1,2,0:T(8,128)(2,1)}, bf16[512,2048]{1,0:T(8,128)(2,1)}, bf16[512,1024]{1,0:T(8,128)(2,1)}) async-done(((bf16[8,1024,1024]{1,2,0:T(8,128)(2,1)}, bf16[8,1024,512]{1,2,0:T(8,128)(2,1)}, bf16[512,2048]{1,0:T(8,128)(2,1)}, bf16[512,1024]{1,0:T(8,128)(2,1)}), (bf16[8,1024,1024]{1,2,0:T(8,128)(2,1)}, ...) | async-done | bytes 28311568 | tf_op jit(solution)/shard_map/psum | solution.py:328
  1952.1 23.7 %copy.155 = f32[8,1024,1024]{2,1,0:T(8,128)} copy(bf16[8,1024,1024]{1,2,0:T(8,128)(2,1)} %get-tuple-element.253) | data formatting | bytes 50331648
  1975.9 12.6 copy.156
  (369 shorter events, 235.0 us)
Async XLA Ops:
  7.2 62.3 %all-gather.7.cloned.1.call-start = ((), (), s32[]{:S(2)}) async-start(), calls=%async_computation.4 | async-start | bytes 6291456 | tf_op jit(solution)/shard_map/all_gather | solution.py:166
  7.9 116.5 %all-gather.9.cloned.1.call-start = ((), (), s32[]{:S(2)}) async-start(), calls=%async_computation.5 | async-start | bytes 3145728 | tf_op jit(solution)/shard_map/all_gather | solution.py:167
  8.7 496.8 %all-gather.11.cloned.1.call-start = ((), (), s32[]{:S(2)}) async-start(), calls=%async_computation.6 | async-start | bytes 50331648 | tf_op jit(solution)/shard_map/all_gather | solution.py:210
  9.4 696.4 %all-gather.13.cloned.1.call-start = ((), (), s32[]{:S(2)}) async-start(), calls=%async_computation.7 | async-start | bytes 25165824 | tf_op jit(solution)/shard_map/all_gather | solution.py:210
  10.0 1338.0 %reduce-scatter.11.cloned.1.call-start = ((), (), s32[]{:S(2)}) async-start(), calls=%async_computation.11 | async-start | bytes 75497472 | tf_op jit(solution)/shard_map/reduce_scatter | solution.py:242
  16.1 71.8 %copy-start.21 = (f32[256,64]{0,1:T(8,128)}, f32[256,64]{0,1:T(8,128)S(1)}, u32[]{:S(2)}) copy-start(f32[256,64]{0,1:T(8,128)S(1)} %pad_maximum_fusion.10) | copy-start | bytes 196612
  21.4 48.1 %copy-start.49 = (f32[2,1,512]{2,1,0:T(1,128)}, f32[2,1,512]{2,1,0:T(1,128)S(1)}, u32[]{:S(2)}) copy-start(f32[2,1,512]{2,1,0:T(1,128)S(1)} %convert_element_type.201) | copy-start | bytes 12292
  26.8 101.5 %copy-start.40 = (f32[2,1,512]{2,1,0:T(1,128)}, f32[2,1,512]{2,1,0:T(1,128)S(1)}, u32[]{:S(2)}) copy-start(f32[2,1,512]{2,1,0:T(1,128)S(1)} %convert_element_type.202) | copy-start | bytes 12292
  49.7 88.6 %copy-start.31 = (bf16[1024,16]{0,1:T(8,128)(2,1)}, bf16[1024,16]{0,1:T(8,128)(2,1)S(1)}, u32[]{:S(2)}) copy-start(bf16[1024,16]{0,1:T(8,128)(2,1)S(1)} %all_gather.32) | copy-start | bytes 98308
  49.7 38.2 %copy-start.19 = (f32[256,64]{0,1:T(8,128)}, f32[256,64]{0,1:T(8,128)S(1)}, u32[]{:S(2)}) copy-start(f32[256,64]{0,1:T(8,128)S(1)} %pad_maximum_fusion.11) | copy-start | bytes 196612
  50.0 26.7 %copy-start.53 = (f32[256]{0:T(256)}, f32[256]{0:T(256)S(1)}, u32[]{:S(2)}) copy-start(f32[256]{0:T(256)S(1)} %add_rsqrt_fusion.1) | copy-start | bytes 3076
  82.5 27.0 %collective-permute-start.1 = (bf16[256,512]{1,0:T(8,128)(2,1)}, bf16[256,512]{1,0:T(8,128)(2,1)}, u32[]{:S(2)}, u32[]{:S(2)}) collective-permute-start(bf16[256,512]{1,0:T(8,128)(2,1)} %add_convert_fusion.1), channel_id=1, source_target_pairs={{0,1},{2,3},{4,5},{6,7},{8,9},{10,11},{12,13},{14,15},{16,17},{18,... | collective-permute-start | bytes 786440 | tf_op jit(solution)/shard_map/ppermute | solution.py:27
  85.4 22.8 %collective-permute-start = (bf16[256,512]{1,0:T(8,128)(2,1)}, bf16[256,512]{1,0:T(8,128)(2,1)}, u32[]{:S(2)}, u32[]{:S(2)}) collective-permute-start(bf16[256,512]{1,0:T(8,128)(2,1)} %slice.153), channel_id=1, source_target_pairs={{0,1},{2,3},{4,5},{6,7},{8,9},{10,11},{12,13},{14,15},{16,17},{18,... | collective-permute-start | bytes 786440 | tf_op jit(solution)/shard_map/ppermute | solution.py:27
  787.7 594.9 %reduce-scatter.7.cloned.1.call-start = ((), (), s32[]{:S(2)}) async-start(), calls=%async_computation.9 | async-start | bytes 3145728 | tf_op jit(solution)/shard_map/reduce_scatter | solution.py:309
  871.1 568.8 %reduce-scatter.5.cloned.1.call-start = ((), (), s32[]{:S(2)}) async-start(), calls=%async_computation.8 | async-start | bytes 6291456 | tf_op jit(solution)/shard_map/reduce_scatter | solution.py:306
  871.1 65.7 %copy-start.20 = (f32[256,64]{0,1:T(8,128)S(1)}, f32[256,64]{0,1:T(8,128)}, u32[]{:S(2)}) copy-start(f32[256,64]{0,1:T(8,128)} %copy-done.19) | copy-start | bytes 196612
  934.2 27.6 %collective-permute-start.3 = (bf16[256,512]{0,1:T(8,128)(2,1)S(1)}, bf16[256,512]{0,1:T(8,128)(2,1)S(1)}, u32[]{:S(2)}, u32[]{:S(2)}) collective-permute-start(bf16[256,512]{0,1:T(8,128)(2,1)S(1)} %bitcast.283), channel_id=1, source_target_pairs={{1,0},{3,2},{5,4},{7,6},{9,8},{11,10},{13,12},{15,14},{17,16},{19,... | collective-permute-start | bytes 786440 | tf_op jit(solution)/shard_map/ppermute | solution.py:27
  935.5 26.0 %collective-permute-start.2 = (bf16[256,512]{0,1:T(8,128)(2,1)S(1)}, bf16[256,512]{0,1:T(8,128)(2,1)S(1)}, u32[]{:S(2)}, u32[]{:S(2)}) collective-permute-start(bf16[256,512]{0,1:T(8,128)(2,1)S(1)} %bitcast.284), channel_id=1, source_target_pairs={{1,0},{3,2},{5,4},{7,6},{9,8},{11,10},{13,12},{15,14},{17,16},{19,... | collective-permute-start | bytes 786440 | tf_op jit(solution)/shard_map/ppermute | solution.py:27
  937.1 24.8 %copy-start.8 = (bf16[256,1024]{1,0:T(8,128)(2,1)S(1)}, bf16[256,1024]{1,0:T(8,128)(2,1)}, u32[]{:S(2)}) copy-start(bf16[256,1024]{1,0:T(8,128)(2,1)} %param.14) | copy-start | bytes 1572868
  937.1 24.8 %copy-start.50 = (f32[2,1,512]{2,1,0:T(1,128)S(1)}, f32[2,1,512]{2,1,0:T(1,128)}, u32[]{:S(2)}) copy-start(f32[2,1,512]{2,1,0:T(1,128)} %copy-done.49) | copy-start | bytes 12292
  937.1 24.8 %copy-start.54 = (f32[256]{0:T(256)S(1)}, f32[256]{0:T(256)}, u32[]{:S(2)}) copy-start(f32[256]{0:T(256)} %copy-done.53) | copy-start | bytes 3076
  938.6 23.3 %copy-start.27 = (bf16[256,1024]{0,1:T(8,128)(2,1)}, bf16[256,1024]{0,1:T(8,128)(2,1)S(1)}, u32[]{:S(2)}) copy-start(bf16[256,1024]{0,1:T(8,128)(2,1)S(1)} %fusion.68) | copy-start | bytes 1572868
  965.5 487.0 %reduce-scatter.9.cloned.1.call-start = ((), (), s32[]{:S(2)}) async-start(), calls=%async_computation.10 | async-start | bytes 49152 | tf_op jit(solution)/shard_map/reduce_scatter | solution.py:312
  966.3 980.0 %all-reduce.9.cloned.1.call-start = ((), (), s32[]{:S(2)}) async-start(), calls=%async_computation.12 | async-start | bytes 56623104 | tf_op jit(solution)/shard_map/psum | solution.py:328
  (48 other events, 326.9 us)
Sparse Core Ops, SparseCore 0:
  9.6 59.8 all-gather.6
  71.0 42.0 all-gather.8
  114.6 390.8 all-gather.10
  506.9 198.8 all-gather.12
  787.8 560.1 reduce-scatter.10
  1350.7 31.8 reduce-scatter.6
  1385.5 54.2 reduce-scatter.4
  1442.6 9.8 reduce-scatter.8
  1458.4 487.9 all-reduce.8
where the time goes:
time: 2000 us
  waiting for transfers between devices  1460 us (73%)
  matrix products  176 us (9%)
  local copies, waits for them, and re-layouts  172 us (9%)
  blocking collectives  83.3 us (4%)
  other arithmetic  81 us (4%)
    all_gather x2, waiting for transfers between devices, body(): pieces = lax.all_gather((w_gate_up, w_down), 'fsdp', axis=0, tiled=True)  513 us
    psum x1, waiting for transfers between devices, body(): lax.psum(grad_gu_own.astype(jnp.bfloat16), 'rep').astype(jnp.float32)  427 us
    reduce_scatter x1, waiting for transfers between devices, body(): lax.psum_scatter(jnp.concatenate([jnp.einsum(weight_forms[2], piece_rows,...  382 us
    psum x1, blocking collectives, body(): lax.psum(owned_router.astype(jnp.bfloat16), 'rep').astype(jnp.float32)  64.1 us
    reduce_scatter x1, waiting for transfers between devices, body(): lax.psum_scatter(grad_w_qkv.astype(jnp.bfloat16), 'fsdp', scatter_dimensi...  57.3 us
    ppermute x4, waiting for transfers between devices, shifted(): lax.ppermute(value, axis, [(source, source + steps) for source in range(i...  43 us
    unnamed x124, local copies, waits for them, and re-layouts  41.8 us
  transfers between devices with their start and end apart: 13, of which 10 were waited for; matrix products, arithmetic and copies ran while one was open for 15% of the time, Pallas kernels for 0%

commit v1 on v0

v1 whole, which is shorter than its diff:
```python
import math
from functools import partial

import jax
import jax.numpy as jnp
from jax import lax
from jax.sharding import Mesh, PartitionSpec as P

D = 1024
HEADS = 16
KV_HEADS = 8
HEAD_DIM = 64
F = 512
TOP = 8
EXPERTS = 16
BLOCK = 256


norm_eps = 1e-06
masked_score = -1e30

def turn(value, axes, steps, sizes):
    count = math.prod(sizes)
    pairs = []
    for source in range(count):
        place, rest = [], source
        for size in reversed(sizes):
            place.append(rest % size)
            rest //= size
        place.reverse()
        target = 0
        for at, size, step in zip(place, sizes, steps):
            target = target * size + (at + step) % size
        pairs.append((source, target))
    return lax.ppermute(value, axes, pairs)


def normalize(input_rows):
    scale_inv = lax.rsqrt(jnp.mean(input_rows * input_rows, -1, keepdims=True) + norm_eps)
    return (input_rows * scale_inv, scale_inv)


def norm_back(normed, scale_inv, grad_normed):
    return scale_inv * (grad_normed - normed * jnp.mean(grad_normed * normed, -1, keepdims=True))


def rotate(values):
    middle = values.shape[-1] // 2
    return jnp.concatenate([-values[..., middle:], values[..., :middle]], -1)


def rotate_back(values):
    middle = values.shape[-1] // 2
    return jnp.concatenate([values[..., middle:], -values[..., :middle]], -1)


def rotary_tables(places, head_width):
    middle = head_width // 2
    place_values = places.astype(jnp.float32)
    frequency = 10000.0 ** (-(2.0 * jnp.arange(middle, dtype=jnp.float32)) / head_width)
    angles = place_values[:, None] * frequency[None, :]
    cosine_table = jnp.concatenate([jnp.cos(angles), jnp.cos(angles)], -1)
    sine_table = jnp.concatenate([jnp.sin(angles), jnp.sin(angles)], -1)
    return (cosine_table[:, None, :], sine_table[:, None, :])


def attend_group(pieces, allowed, score_scale):
    query_group, key_group, value_group = pieces
    scores = (
        jnp.einsum("qrd,kd->rqk", query_group, key_group, preferred_element_type=jnp.float32)
        * score_scale
    )
    scores = jnp.where(allowed[None], scores, masked_score)
    largest = jnp.max(scores, -1, keepdims=True)
    exponent = jnp.exp(scores - largest)
    totals = jnp.sum(exponent, -1, keepdims=True)
    attn_probs = (exponent / totals).astype(jnp.bfloat16)
    output = jnp.einsum("rqk,kd->qrd", attn_probs, value_group, preferred_element_type=jnp.float32)
    return (output, (largest + jnp.log(totals))[..., 0])


def attend_back(pieces, allowed, score_scale):
    query_group, key_group, value_group, grad_group, log_total = pieces
    scores = (
        jnp.einsum("qrd,kd->rqk", query_group, key_group, preferred_element_type=jnp.float32)
        * score_scale
    )
    scores = jnp.where(allowed[None], scores, masked_score)
    attn_probs = jnp.exp(scores - log_total[..., None])
    probs_low = attn_probs.astype(jnp.bfloat16)
    grad_value = jnp.einsum(
        "rqk,qrd->kd", probs_low, grad_group, preferred_element_type=jnp.float32
    )
    grad_probs = jnp.einsum(
        "qrd,kd->rqk", grad_group, value_group, preferred_element_type=jnp.float32
    )
    grad_scores = (
        attn_probs * (grad_probs - jnp.sum(attn_probs * grad_probs, -1, keepdims=True))
    ).astype(jnp.bfloat16)
    grad_query = (
        jnp.einsum("rqk,kd->qrd", grad_scores, key_group, preferred_element_type=jnp.float32)
        * score_scale
    )
    grad_key = (
        jnp.einsum("rqk,qrd->kd", grad_scores, query_group, preferred_element_type=jnp.float32)
        * score_scale
    )
    return (grad_query, grad_key, grad_value)


def line_sum(value, axis):
    count = lax.axis_size(axis)
    if count == 1:
        return value
    if count % 2:
        return lax.psum(value, axis)
    middle = count // 2
    total = value
    for step in range(middle - 1):
        total = total + lax.ppermute(total, axis, [(step, step + 1), (count - 1 - step, count - 2 - step)])
    total = total + lax.ppermute(total, axis, [(middle - 1, middle), (middle, middle - 1)])
    place = lax.axis_index(axis)
    for step in range(middle - 1):
        low = middle - 2 - step
        passed = lax.ppermute(total, axis, [(low + 1, low), (count - 2 - low, count - 1 - low)])
        total = jnp.where((place == low) | (place == count - 1 - low), passed, total)
    return total


def own_part(value, axis, index, parts):
    size = value.shape[axis] // parts
    return lax.dynamic_slice_in_dim(value, index * size, size, axis)


def body(
    hidden_in, routes, w_qkv, w_out, w_router, attn_gain, ffn_gain, w_gate_up, w_down, cotangent
):
    length = hidden_in.shape[0]
    groups = HEADS // KV_HEADS
    query_width = HEADS * HEAD_DIM
    key_width = KV_HEADS * HEAD_DIM
    score_scale = HEAD_DIM ** (-0.5)
    shards, side, cores = lax.axis_size("fsdp"), lax.axis_size("side"), lax.axis_size("core")
    shard, side_at, core_at = lax.axis_index("fsdp"), lax.axis_index("side"), lax.axis_index("core")
    near = [(a, s) for a in range(side) for s in range(shards)]
    bf16, f32 = jnp.bfloat16, jnp.float32

    def dot(left, right, dims=((1,), (0,))):
        return lax.dot_general(left, right, (dims, ((), ())), preferred_element_type=f32)

    def fetch(piece):
        out = [[piece]]
        part = own_part(piece, 0, core_at, cores)
        for step in range(1, shards):
            first = turn(part, "fsdp", (step,), (shards,))
            parts = [first]
            for core in range(1, cores):
                parts.append(turn(first, "core", (core,), (cores,)))
            out.append(parts)
        return out

    def spread(rows):
        first = [rows if (a, s) == (0, 0) else turn(rows, ("side", "fsdp"), (a, s), (side, shards)) for a, s in near]
        first = jnp.stack(first)
        out = [first]
        for core in range(1, cores):
            out.append(turn(first, "core", (core,), (cores,)))
        return jnp.concatenate(out, 0)

    def collect(blocks):
        count = len(near)
        total = blocks[:count]
        for core in range(1, cores):
            total = total.astype(f32) + turn(blocks[core * count : (core + 1) * count], "core", (-core % cores,), (cores,)).astype(f32)
        total = total.astype(blocks.dtype)
        out = total[0].astype(f32)
        for i, (a, s) in enumerate(near):
            if (a, s) != (0, 0):
                out = out + turn(total[i], ("side", "fsdp"), (-a % side, -s % shards), (side, shards)).astype(f32)
        return out

    def row_blocks(values, axis):
        width = values.shape[axis] // shards
        out = [[lax.dynamic_slice_in_dim(values, shard * width, width, axis)]]
        for step in range(1, shards):
            base = (shard - step) % shards * width
            parts = []
            for core in range(cores):
                at = base + (core_at - core) % cores * (width // cores)
                parts.append(lax.dynamic_slice_in_dim(values, at, width // cores, axis))
            out.append(parts)
        return out

    def rows_dot(values, pieces):
        total = None
        for parts, weights in zip(row_blocks(values, 1), pieces):
            for part, weight in zip(parts, weights):
                term = dot(part, weight)
                total = term if total is None else total + term
        return total

    def rows_back(grads, pieces, width):
        full = jnp.zeros((grads.shape[0], width), f32)
        block = width // shards
        for step, weights in enumerate(pieces):
            base = (shard - step) % shards * block
            for core, weight in enumerate(weights):
                at = base + ((core_at - core) % cores * (block // cores) if step else 0)
                full = lax.dynamic_update_slice_in_dim(full, dot(grads, weight, ((1,), (1,))), at, 1)
        return full

    def gathered(piece):
        return lax.all_gather(piece, "fsdp", axis=0, tiled=True)

    def owned_sum(partial_sum):
        value = partial_sum.astype(bf16)
        half = own_part(value, 1, core_at, cores)
        for core in range(1, cores):
            other = own_part(value, 1, (core_at + core) % cores, cores)
            half = half + turn(other, "core", (core,), (cores,))
        total = own_part(half, 0, shard, shards)
        for step in range(1, shards):
            other = own_part(half, 0, (shard + step) % shards, shards)
            total = total + turn(other, "fsdp", (step,), (shards,))
        if side > 1:
            mine = own_part(total, 1, side_at, side)
            for step in range(1, side):
                mine = mine + turn(own_part(total, 1, (side_at + step) % side, side), "side", (step,), (side,))
            mine = line_sum(mine, "line")
            full = jnp.zeros(total.shape, bf16)
            width = mine.shape[1]
            full = lax.dynamic_update_slice_in_dim(full, mine, side_at * width, 1)
            for step in range(1, side):
                full = lax.dynamic_update_slice_in_dim(full, turn(mine, "side", (step,), (side,)), (side_at - step) % side * width, 1)
        else:
            full = line_sum(total, "line")
        width = full.shape[1]
        out = jnp.zeros((full.shape[0], width * cores), f32)
        out = lax.dynamic_update_slice_in_dim(out, full.astype(f32), core_at * width, 1)
        for core in range(1, cores):
            out = lax.dynamic_update_slice_in_dim(out, turn(full, "core", (core,), (cores,)).astype(f32), (core_at - core) % cores * width, 1)
        return out

    parity = shard % 2
    local_rows = jnp.arange(length, dtype=jnp.int32)
    places = parity * length + local_rows
    query_block = places // BLOCK
    earlier_block = jnp.where(parity == 1, local_rows // BLOCK, 4 * length)
    key_block = jnp.concatenate([earlier_block, query_block], 0)
    allowed = key_block[None, :] <= query_block[:, None]
    cosine_table, sine_table = rotary_tables(places, HEAD_DIM)
    small = gathered(jnp.concatenate([w_router, attn_gain[:, None], ffn_gain[:, None]], 1))
    full_router, gain_attn, gain_ffn = small[:, :EXPERTS], small[:, EXPERTS], small[:, EXPERTS + 1]
    qkv_pieces = fetch(w_qkv)
    out_pieces = fetch(w_out)
    grads_near = spread(cotangent).reshape(-1, D)
    routes_near = spread(routes).reshape(-1, TOP)
    later = [(i, i + 1) for i in range(0, shards, 2)]
    before = [(i + 1, i) for i in range(0, shards, 2)]

    input_rows = hidden_in.astype(f32)
    normed_one, inverse_one = normalize(input_rows)
    input_one = (normed_one * gain_attn).astype(bf16)
    qkv_proj = rows_dot(input_one, qkv_pieces)
    query_raw = qkv_proj[:, :query_width].reshape(length, HEADS, HEAD_DIM)
    key_raw = qkv_proj[:, query_width : query_width + key_width].reshape(length, KV_HEADS, HEAD_DIM)
    queries = (query_raw * cosine_table + rotate(query_raw) * sine_table).astype(bf16)
    key_flat = (
        (key_raw * cosine_table + rotate(key_raw) * sine_table).astype(bf16).reshape(length, key_width)
    )
    value_flat = qkv_proj[:, query_width + key_width :].astype(bf16)
    both = jnp.concatenate([key_flat, value_flat], 1)
    both = jnp.concatenate([lax.ppermute(both, "fsdp", later), both], 0)
    all_keys = both[:, :key_width].reshape(2 * length, KV_HEADS, HEAD_DIM)
    all_values = both[:, key_width:].reshape(2 * length, KV_HEADS, HEAD_DIM)
    query_groups = jnp.transpose(queries.reshape(length, KV_HEADS, groups, HEAD_DIM), (1, 0, 2, 3))
    key_groups = jnp.transpose(all_keys, (1, 0, 2))
    value_groups = jnp.transpose(all_values, (1, 0, 2))
    attended, log_totals = lax.map(
        partial(attend_group, allowed=allowed, score_scale=score_scale),
        (query_groups, key_groups, value_groups),
    )
    attended = jnp.transpose(attended, (1, 0, 2, 3)).reshape(length, query_width).astype(bf16)
    residual = input_rows + rows_dot(attended, out_pieces)
    normed_two, inverse_two = normalize(residual)
    input_two = (normed_two * gain_ffn).astype(bf16)

    def gates(rows, named):
        router = jax.nn.softmax(dot(rows, full_router), -1)
        routed = jnp.any(named[:, :, None] == jnp.arange(EXPERTS, dtype=jnp.int32), 1)
        return (router, jnp.where(routed, router, 0.0), routed)

    router, _, routed = gates(input_two, routes)
    rows_near = spread(input_two).reshape(-1, D)
    _, gates_near, _ = gates(rows_near, routes_near)

    local_experts = w_gate_up.shape[0]
    count = local_experts // (side * cores)
    mine_at = (side_at * cores + core_at) * count
    own_gate_up = lax.dynamic_slice_in_dim(w_gate_up, mine_at, count, 0)
    own_down = lax.dynamic_slice_in_dim(w_down, mine_at, count, 0)
    first_expert = shard * local_experts + mine_at
    own_gates = lax.dynamic_slice_in_dim(gates_near, first_expert, count, 1)
    grad_slots = jnp.zeros(rows_near.shape, f32)
    mixed = jnp.zeros(rows_near.shape, f32)
    gate_up_sums, down_sums, gate_grads = [], [], []
    for e in range(count):
        gate_up = dot(rows_near, own_gate_up[e])
        gate_part, up_part = gate_up[:, :F], gate_up[:, F:]
        sigmoid_g = jax.nn.sigmoid(gate_part)
        silu_g = gate_part * sigmoid_g
        hidden = silu_g * up_part
        gate = own_gates[:, e : e + 1]
        hidden_gated = (gate * hidden).astype(bf16)
        raw = dot(grads_near, own_down[e])
        gate_grads.append(jnp.sum(raw * hidden, 1))
        grad_hidden = gate * raw
        grad_gate_up = jnp.concatenate(
            [
                grad_hidden * up_part * sigmoid_g * (1.0 + gate_part * (1.0 - sigmoid_g)),
                grad_hidden * silu_g,
            ],
            -1,
        ).astype(bf16)
        gate_up_sums.append(line_sum(dot(rows_near, grad_gate_up, ((0,), (0,))).astype(bf16), "line"))
        down_sums.append(line_sum(dot(grads_near, hidden_gated, ((0,), (0,))).astype(bf16), "line"))
        mixed = mixed + dot(hidden_gated, own_down[e], ((1,), (1,)))
        grad_slots = grad_slots + dot(grad_gate_up, own_gate_up[e], ((1,), (1,)))
    blocks = len(near) * cores
    gate_grads = jnp.stack(gate_grads).reshape(count, blocks, length)
    gate_wide = jnp.zeros((blocks, EXPERTS, length), f32)
    gate_wide = lax.dynamic_update_slice_in_dim(gate_wide, jnp.transpose(gate_grads, (1, 0, 2)), first_expert, 1)
    grad_router = jnp.where(routed, collect(gate_wide).T, 0.0)
    grad_slot_sum = collect(grad_slots.astype(bf16).reshape(blocks, length, D))
    mixture = collect(mixed.astype(bf16).reshape(blocks, length, D))
    layer_out = (residual + mixture).astype(bf16)

    def assemble(sums):
        width = sums[0].shape[-1]
        own = jnp.stack(sums)
        out = jnp.zeros((local_experts, D, width), f32)
        for a in range(side):
            theirs = own if a == 0 else turn(own, "side", (a,), (side,))
            for core in range(cores):
                block = theirs if core == 0 else turn(theirs, "core", (core,), (cores,))
                at = ((side_at - a) % side * cores + (core_at - core) % cores) * count
                out = lax.dynamic_update_slice_in_dim(out, block.astype(f32), at, 0)
        return out

    grad_w_gate_up = assemble(gate_up_sums)
    grad_w_down = assemble(down_sums)

    grad_out = cotangent.astype(f32)
    grad_logits = (
        router * (grad_router - jnp.sum(router * grad_router, -1, keepdims=True))
    ).astype(bf16)
    grad_input_two = grad_slot_sum + dot(grad_logits, full_router, ((1,), (1,)))
    grad_w_router = dot(input_two, grad_logits, ((0,), (0,)))
    grad_ffn_gain = jnp.sum(grad_input_two * normed_two, 0)
    grad_residual = grad_out + norm_back(normed_two, inverse_two, grad_input_two * gain_ffn)
    grad_attn = grad_residual.astype(bf16)
    grad_w_out = dot(attended, grad_attn, ((0,), (0,)))
    grad_attended = rows_back(grad_attn, out_pieces, query_width).astype(bf16)
    grad_groups = jnp.transpose(
        grad_attended.reshape(length, KV_HEADS, groups, HEAD_DIM), (1, 0, 2, 3)
    )
    grad_query, grad_key, grad_value = lax.map(
        partial(attend_back, allowed=allowed, score_scale=score_scale),
        (query_groups, key_groups, value_groups, grad_groups, log_totals),
    )
    grad_query = jnp.transpose(grad_query, (1, 0, 2, 3)).reshape(length, HEADS, HEAD_DIM)
    grad_key = jnp.transpose(grad_key, (1, 0, 2)).reshape(2 * length, key_width)
    grad_value = jnp.transpose(grad_value, (1, 0, 2)).reshape(2 * length, key_width)
    grad_both = jnp.concatenate([grad_key, grad_value], 1)
    grad_both = grad_both[length:] + lax.ppermute(grad_both[:length].astype(bf16), "fsdp", before).astype(f32)
    grad_key = grad_both[:, :key_width].reshape(length, KV_HEADS, HEAD_DIM)
    grad_value = grad_both[:, key_width:]
    query_back = grad_query * cosine_table + rotate_back(grad_query * sine_table)
    key_back = grad_key * cosine_table + rotate_back(grad_key * sine_table)
    grad_qkv = jnp.concatenate(
        [query_back.reshape(length, query_width), key_back.reshape(length, key_width), grad_value],
        -1,
    ).astype(bf16)
    grad_w_qkv = dot(input_one, grad_qkv, ((0,), (0,)))
    grad_input_one = rows_back(grad_qkv, qkv_pieces, D)
    grad_attn_gain = jnp.sum(grad_input_one * normed_one, 0)
    grad_in = grad_residual + norm_back(normed_one, inverse_one, grad_input_one * gain_attn)
    pad = jnp.zeros((D, 128 - EXPERTS - 2), f32)
    rest = jnp.concatenate([grad_w_router, grad_attn_gain[:, None], grad_ffn_gain[:, None], pad], 1)
    out_sum = owned_sum(grad_w_out)
    qkv_sum = owned_sum(grad_w_qkv)
    rest_sum = owned_sum(rest)
    return (
        layer_out,
        grad_in,
        qkv_sum,
        out_sum,
        rest_sum[:, :EXPERTS],
        rest_sum[:, EXPERTS],
        rest_sum[:, EXPERTS + 1],
        grad_w_gate_up,
        grad_w_down,
    )


def solution(mesh):
    copies, shards = mesh.shape["rep"], mesh.shape["fsdp"]
    local = EXPERTS // shards
    cores = 2 if copies % 2 == 0 and local % 2 == 0 else 1
    side = 2 if cores == 2 and copies % 4 == 0 and local % 4 == 0 else 1
    names = ("line", "side", "core", "fsdp")
    parts = Mesh(mesh.devices.reshape(copies // (side * cores), side, cores, shards), names)
    rows, shard = P(names, None), P("fsdp", None)
    experts = P("fsdp", None, None)
    in_specs = (rows, rows, shard, shard, shard, P("fsdp"), P("fsdp"), experts, experts, rows)
    out_specs = (rows, rows, shard, shard, shard, P("fsdp"), P("fsdp"), experts, experts)
    return jax.shard_map(body, mesh=parts, in_specs=in_specs, out_specs=out_specs, check_vma=False)
```

time: 2000 us -> 930 us (0.47)
  waiting for transfers between devices: 1460 us -> 446 us
  local copies, waits for them, and re-layouts: 172 us -> 58.4 us
  starting transfers between devices: 7.93 us -> 75.1 us
  blocking collectives: 83.3 us -> 37.6 us
  other arithmetic: 81 us -> 105 us
    all_gather x4 -> x0, waiting for transfers between devices: 532 us -> none  [the longest x2 513 us: body(): pieces = lax.all_gather((w_gate_up, w_down), 'fsdp', axis=0, tiled=True)]
    reduce_scatter x4 -> x0, waiting for transfers between devices: 454 us -> none  [the longest x1 382 us: body(): lax.psum_scatter(jnp.concatenate([jnp.einsum(weight_forms[2], piece_rows,...]
    psum x1 -> x0, waiting for transfers between devices: 427 us -> none  [body(): lax.psum(grad_gu_own.astype(jnp.bfloat16), 'rep').astype(jnp.float32)]
    ppermute x4 -> x72, waiting for transfers between devices: 43 us -> 446 us  [the longest x49 183 us: turn(): return lax.ppermute(value, axes, pairs)]
    gather x10 -> x0, local copies, waits for them, and re-layouts: 78.8 us -> none  [the longest x5 17.2 us: body(): gate_vals = jnp.take_along_axis(router, routes, 1)]
    ppermute x4 -> x72, starting transfers between devices: 7.57 us -> 75.1 us  [the longest x49 35.8 us: turn(): return lax.ppermute(value, axes, pairs)]
    psum x1 -> x0, blocking collectives: 64.1 us -> none  [body(): lax.psum(owned_router.astype(jnp.bfloat16), 'rep').astype(jnp.float32)]
    dynamic_update_slice x0 -> x18, other arithmetic: none -> 35.6 us  [the longest x8 32.6 us: assemble(): out = lax.dynamic_update_slice_in_dim(out, block.astype(f32), at, 0)]
  transfers between devices with their start and end apart: 13 -> 72, of which waited for: 10 -> 26; matrix products, arithmetic and copies ran while one was open for 15% -> 31% of each run, Pallas kernels for 0% -> 0%
where the time goes in v1:
time: 930 us; the launch traced here: 920 us
  waiting for transfers between devices  446 us (48%)
  matrix products  194 us (21%)
  other arithmetic  105 us (11%)
  starting transfers between devices  75.1 us (8%)
  local copies, waits for them, and re-layouts  58.4 us (6%)
  blocking collectives  37.6 us (4%)
    ppermute x49, waiting for transfers between devices, turn(): return lax.ppermute(value, axes, pairs)  183 us
    ppermute x7, waiting for transfers between devices, line_sum(): lax.ppermute(total, axis, [(step, step + 1), (count - 1 - step, count - 2...  128 us
    ppermute x7, waiting for transfers between devices, line_sum(): lax.ppermute(total, axis, [(low + 1, low), (count - 2 - low, count - 1 -...  117 us
    dot_general x30, matrix products, dot(): lax.dot_general(left, right, (dims, ((), ())), preferred_element_type=f32)  108 us
    all_gather x1, blocking collectives, gathered(): return lax.all_gather(piece, 'fsdp', axis=0, tiled=True)  37.6 us
    ppermute x49, starting transfers between devices, turn(): return lax.ppermute(value, axes, pairs)  35.8 us
    dynamic_update_slice x8, other arithmetic, assemble(): out = lax.dynamic_update_slice_in_dim(out, block.astype(f32), at, 0)  32.6 us
  transfers between devices with their start and end apart: 72, of which 26 were waited for; matrix products, arithmetic and copies ran while one was open for 31% of the time, Pallas kernels for 0%

profile of v1, /device:TPU:0, one launch (start us, length us, event | category | flops | bytes accessed | tf_op | source)
XLA Modules:
  0.0 920.1 jit_solution(4672004367731621522)
XLA Ops:
  12.6 37.6 %all_gather.3 = bf16[1024,18]{0,1:T(8,128)(2,1)S(1)} all-gather(bf16[512,18]{0,1:T(8,128)(2,1)S(1)} %pad_maximum_fusion.21), channel_id=1, replica_groups=mesh['line'=4,'side'=2,'core'=2,'fsdp'=2] {'fsdp'}, dimensions={0}, use_global_device_ids=true | all-gather | bytes 55296 | tf_op jit(solution)/shard_map/all_gather | solution.py:213
  73.4 8.0 collective-permute-done.3
  113.7 31.4 %while.30 = (s32[]{:T(128)}, bf16[8,256,2,64]{1,3,2,0:T(8,128)(2,1)}, f32[8,2,256]{2,1,0:T(2,128)}, bf16[8,512,64]{1,2,0:T(8,128)(2,1)}, bf16[8,512,64]{1,2,0:T(...) while((s32[]{:T(128)}, ...), condition=%wide.region_4.5_spmd.clone.clone, body=%wide.region_1.4_spmd.clone.sunk.clone | while | flops 69336576 | bytes 3757153 | solution.py:279
  154.1 10.2 %collective-permute-done.9 = bf16[256,1024]{1,0:T(8,128)(2,1)S(1)} collective-permute-done((bf16[256,1024]{1,0:T(8,128)(2,1)S(1)}, bf16[256,1024]{1,0:T(8,128)(2,1)S(1)}, u32[]{:S(2)}, u32[]{:S(2)}) %collective-permute-start.9) | collective-permute-done | bytes 524320 | tf_op jit(solution)/shard_map/ppermute | solution.py:35
  167.4 9.4 %collective-permute-done.11 = bf16[256,1024]{1,0:T(8,128)(2,1)S(1)} collective-permute-done((bf16[256,1024]{1,0:T(8,128)(2,1)S(1)}, bf16[256,1024]{1,0:T(8,128)(2,1)S(1)}, u32[]{:S(2)}, u32[]{:S(2)}) %collective-permute-start.11) | collective-permute-done | bytes 524320 | tf_op jit(solution)/shard_map/ppermute | solution.py:35
  185.0 8.5 fusion.58
  200.8 8.4 fusion.55
  215.8 8.5 fusion.59
  240.2 9.9 %add_convert_fusion = bf16[2048,1024]{1,0:T(8,128)(2,1)S(1)} fusion(f32[2048,1024]{1,0:T(8,128)} %fusion.55, bf16[2048,512]{0,1:T(8,128)(2,1)} %copy-done.65, bf16[2048,512]{0,1:T(8,128)(2,1)} %copy-done.64, bf16[8,1024,1024]{2,1,0:T(8,128)(2,1)} %param.21, s32[]{:T(128)S(6)} %add.575), kind=kOutput, calls=%fused_computation.66 | convolution fusion | flops 4307550208 | bytes 18874372 | tf_op jit(solution)/shard_map/dot_general | solution.py:149
  288.0 101.0 %collective-permute-done.66 = bf16[1024,512]{1,0:T(8,128)(2,1)S(1)} collective-permute-done((bf16[1024,512]{1,0:T(8,128)(2,1)S(1)}, bf16[1024,512]{1,0:T(8,128)(2,1)S(1)}, u32[]{:S(2)}, u32[]{:S(2)}) %collective-permute-start.66) | collective-permute-done | bytes 1048608 | tf_op jit(solution)/shard_map/ppermute | solution.py:120
  395.7 19.3 %collective-permute-done.63 = bf16[1024,512]{1,0:T(8,128)(2,1)S(1)} collective-permute-done((bf16[1024,512]{1,0:T(8,128)(2,1)S(1)}, bf16[1024,512]{1,0:T(8,128)(2,1)S(1)}, u32[]{:S(2)}, u32[]{:S(2)}) %collective-permute-start.63) | collective-permute-done | bytes 1048608 | tf_op jit(solution)/shard_map/ppermute | solution.py:120
  447.0 70.3 %while.31 = (s32[]{:T(128)}, f32[8,256,2,64]{1,3,2,0:T(8,128)}, f32[8,512,64]{1,2,0:T(8,128)}, f32[8,512,64]{1,2,0:T(8,128)}, bf16[8,512,64]{1,2,0:T(8,128)(2,1)...) while((s32[]{:T(128)}, f32[8,256,2,64]{1,3,2,0:T(8,128)}, ...), condition=%wide.region_18.19_spmd.clone.clone, body=%wide.region_16.18_spmd.clone.sunk.clone | while | flops 170327552 | bytes 8996985 | solution.py:367
  522.7 11.3 %collective-permute-done.29 = bf16[256,1024]{0,1:T(8,128)(2,1)S(1)} collective-permute-done((bf16[256,1024]{0,1:T(8,128)(2,1)S(1)}, bf16[256,1024]{0,1:T(8,128)(2,1)S(1)}, u32[]{:S(2)}, u32[]{:S(2)}) %collective-permute-start.29) | collective-permute-done | bytes 524320 | tf_op jit(solution)/shard_map/ppermute | solution.py:375
  563.8 31.4 %collective-permute-done.59 = bf16[1024,1024]{1,0:T(8,128)(2,1)S(1)} collective-permute-done((bf16[1024,1024]{1,0:T(8,128)(2,1)S(1)}, bf16[1024,1024]{1,0:T(8,128)(2,1)S(1)}, u32[]{:S(2)}, u32[]{:S(2)}) %collective-permute-start.59) | collective-permute-done | bytes 2097184 | tf_op jit(solution)/shard_map/ppermute | solution.py:125
  595.5 44.7 %collective-permute-done.56 = bf16[1024,1024]{1,0:T(8,128)(2,1)S(1)} collective-permute-done((bf16[1024,1024]{1,0:T(8,128)(2,1)S(1)}, bf16[1024,1024]{1,0:T(8,128)(2,1)S(1)}, u32[]{:S(2)}, u32[]{:S(2)}) %collective-permute-start.56) | collective-permute-done | bytes 2097184 | tf_op jit(solution)/shard_map/ppermute | solution.py:125
  643.9 18.5 %collective-permute-done.65 = bf16[1024,512]{1,0:T(8,128)(2,1)S(1)} collective-permute-done((bf16[1024,512]{1,0:T(8,128)(2,1)S(1)}, bf16[1024,512]{1,0:T(8,128)(2,1)S(1)}, u32[]{:S(2)}, u32[]{:S(2)}) %collective-permute-start.65) | collective-permute-done | bytes 1048608 | tf_op jit(solution)/shard_map/ppermute | solution.py:125
  678.8 108.7 %collective-permute-done.40 = bf16[512,256]{1,0:T(8,128)(2,1)} collective-permute-done((bf16[512,256]{1,0:T(8,128)(2,1)S(1)}, bf16[512,256]{1,0:T(8,128)(2,1)}, u32[]{:S(2)}, u32[]{:S(2)}) %collective-permute-start.40) | collective-permute-done | bytes 262176 | tf_op jit(solution)/shard_map/ppermute | solution.py:35
  788.6 10.1 %collective-permute-done.15 = bf16[256,1024]{1,0:T(8,128)(2,1)} collective-permute-done((bf16[256,1024]{1,0:T(8,128)(2,1)}, bf16[256,1024]{1,0:T(8,128)(2,1)}, u32[]{:S(2)}, u32[]{:S(2)}) %collective-permute-start.15) | collective-permute-done | bytes 524320 | tf_op jit(solution)/shard_map/ppermute | solution.py:35
  798.7 9.8 %collective-permute-done.32 = bf16[512,512]{1,0:T(8,128)(2,1)} collective-permute-done((bf16[512,512]{1,0:T(8,128)(2,1)}, bf16[512,512]{1,0:T(8,128)(2,1)}, u32[]{:S(2)}, u32[]{:S(2)}) %collective-permute-start.32) | collective-permute-done | bytes 524320 | tf_op jit(solution)/shard_map/ppermute | solution.py:35
  836.8 10.1 %collective-permute-done.43 = bf16[512,256]{1,0:T(8,128)(2,1)S(1)} collective-permute-done((bf16[512,256]{1,0:T(8,128)(2,1)S(1)}, bf16[512,256]{1,0:T(8,128)(2,1)S(1)}, u32[]{:S(2)}, u32[]{:S(2)}) %collective-permute-start.43) | collective-permute-done | bytes 262176 | tf_op jit(solution)/shard_map/ppermute | solution.py:125
  856.5 9.0 collective-permute-done.35
  872.1 7.5 collective-permute-done.36
  880.9 11.6 %broadcast_in_dim.139 = f32[8,1024,1024]{2,1,0:T(8,128)} broadcast(f32[]{:T(128)} %constant.238.clone.1), dimensions={} | broadcast | bytes 33554436 | tf_op jit(solution)/shard_map/broadcast_in_dim | solution.py:341
  903.5 9.8 %convert_dynamic-update-slice_fusion.1 = f32[8,1024,1024]{2,1,0:T(8,128)} fusion(f32[8,1024,1024]{2,1,0:T(8,128)} %convert_dynamic-update-slice_fusion.2, s32[]{:T(128)S(6)} %select_n.364, bf16[2,1024,1024]{2,1,0:T(8,128)(2,1)} %collective-permute-done.61), kind=kLoop, calls=%fused_computation.63 | loop fusion | flops 2097152 | bytes 12582916 | tf_op jit(solution)/shard_map/dynamic_update_slice | solution.py:347
  (561 shorter events, 413.3 us)
Async XLA Ops:
  0.7 69.3 %collective-permute-start.17 = (bf16[256,1024]{1,0:T(8,128)(2,1)}, bf16[256,1024]{1,0:T(8,128)(2,1)}, u32[]{:S(2)}, u32[]{:S(2)}) collective-permute-start(bf16[256,1024]{1,0:T(8,128)(2,1)} %param.23), channel_id=1, source_target_pairs={{0,1},{1,0},{4,5},{5,4},{2,3},{3,2},{6,7},{7,6},{8,9},{9,8},{12,13... | collective-permute-start | bytes 1572872 | tf_op jit(solution)/shard_map/ppermute | solution.py:35
  70.0 107.2 %collective-permute-start.8 = (s32[4,256,8]{1,2,0:T(8,128)}, s32[4,256,8]{1,2,0:T(8,128)}, u32[]{:S(2)}, u32[]{:S(2)}) collective-permute-start(s32[4,256,8]{1,2,0:T(8,128)} %pad_add_fusion), channel_id=1, source_target_pairs={{0,2},{2,0},{1,3},{3,1},{4,6},{6,4},{5,7},{7,5},{8,10},{10,8},{9,1... | collective-permute-start | bytes 98312 | tf_op jit(solution)/shard_map/ppermute | solution.py:35
  72.9 108.4 %collective-permute-start.20 = (bf16[4,256,1024]{2,1,0:T(8,128)(2,1)}, bf16[4,256,1024]{2,1,0:T(8,128)(2,1)}, u32[]{:S(2)}, u32[]{:S(2)}) collective-permute-start(bf16[4,256,1024]{2,1,0:T(8,128)(2,1)} %pad_maximum_fusion.8), channel_id=1, source_target_pairs={{0,2},{2,0},{1,3},{3,1},{4,6},{6,4},{5,7},{7,5},{8,10},{10,8},{9,1... | collective-permute-start | bytes 6291464 | tf_op jit(solution)/shard_map/ppermute | solution.py:35
  81.5 66.6 %collective-permute-start.4 = (bf16[256,1024]{1,0:T(8,128)(2,1)}, bf16[256,1024]{1,0:T(8,128)(2,1)}, u32[]{:S(2)}, u32[]{:S(2)}) collective-permute-start(bf16[256,1024]{1,0:T(8,128)(2,1)} %collective-permute-done.3), channel_id=1, source_target_pairs={{0,2},{2,0},{1,3},{3,1},{4,6},{6,4},{5,7},{7,5},{8,10},{10,8},{9,1... | collective-permute-start | bytes 1572872 | tf_op jit(solution)/shard_map/ppermute | solution.py:35
  250.5 143.3 %collective-permute-start.21 = (bf16[4,256,1024]{2,1,0:T(8,128)(2,1)S(1)}, bf16[4,256,1024]{2,1,0:T(8,128)(2,1)S(1)}, u32[]{:S(2)}, u32[]{:S(2)}) collective-permute-start(bf16[4,256,1024]{2,1,0:T(8,128)(2,1)S(1)} %bitcast.376), channel_id=1, source_target_pairs={{0,2},{2,0},{1,3},{3,1},{4,6},{6,4},{5,7},{7,5},{8,10},{10,8},{9,1... | collective-permute-start | bytes 6291464 | tf_op jit(solution)/shard_map/ppermute | solution.py:35
  273.2 142.2 %collective-permute-start.57 = (bf16[1024,1024]{1,0:T(8,128)(2,1)S(1)}, bf16[1024,1024]{1,0:T(8,128)(2,1)S(1)}, u32[]{:S(2)}, u32[]{:S(2)}) collective-permute-start(bf16[1024,1024]{1,0:T(8,128)(2,1)S(1)} %fusion.57), channel_id=1, source_target_pairs={{0,8},{24,16},{1,9},{25,17},{2,10},{26,18},{3,11},{27,19},{4,12},{... | collective-permute-start | bytes 6291464 | tf_op jit(solution)/shard_map/ppermute | solution.py:120
  276.8 140.1 %collective-permute-start.54 = (bf16[1024,1024]{1,0:T(8,128)(2,1)S(1)}, bf16[1024,1024]{1,0:T(8,128)(2,1)S(1)}, u32[]{:S(2)}, u32[]{:S(2)}) collective-permute-start(bf16[1024,1024]{1,0:T(8,128)(2,1)S(1)} %fusion.56), channel_id=1, source_target_pairs={{0,8},{24,16},{1,9},{25,17},{2,10},{26,18},{3,11},{27,19},{4,12},{... | collective-permute-start | bytes 6291464 | tf_op jit(solution)/shard_map/ppermute | solution.py:120
  278.2 110.8 %collective-permute-start.66 = (bf16[1024,512]{1,0:T(8,128)(2,1)S(1)}, bf16[1024,512]{1,0:T(8,128)(2,1)S(1)}, u32[]{:S(2)}, u32[]{:S(2)}) collective-permute-start(bf16[1024,512]{1,0:T(8,128)(2,1)S(1)} %convolution_convert_fusion.2), channel_id=1, source_target_pairs={{0,8},{24,16},{1,9},{25,17},{2,10},{26,18},{3,11},{27,19},{4,12},{... | collective-permute-start | bytes 3145736 | tf_op jit(solution)/shard_map/ppermute | solution.py:120
  283.4 144.3 %collective-permute-start.13 = (bf16[4,256,1024]{2,1,0:T(8,128)(2,1)S(1)}, bf16[4,256,1024]{2,1,0:T(8,128)(2,1)S(1)}, u32[]{:S(2)}, u32[]{:S(2)}) collective-permute-start(bf16[4,256,1024]{2,1,0:T(8,128)(2,1)S(1)} %bitcast.377), channel_id=1, source_target_pairs={{0,2},{2,0},{1,3},{3,1},{4,6},{6,4},{5,7},{7,5},{8,10},{10,8},{9,1... | collective-permute-start | bytes 6291464 | tf_op jit(solution)/shard_map/ppermute | solution.py:35
  424.6 121.5 %collective-permute-start.64 = (bf16[1024,512]{1,0:T(8,128)(2,1)}, bf16[1024,512]{1,0:T(8,128)(2,1)}, u32[]{:S(2)}, u32[]{:S(2)}) collective-permute-start(bf16[1024,512]{1,0:T(8,128)(2,1)} %add.563), channel_id=1, source_target_pairs={{8,16},{16,8},{9,17},{17,9},{10,18},{18,10},{11,19},{19,11},{12,20... | collective-permute-start | bytes 3145736 | tf_op jit(solution)/shard_map/ppermute | solution.py:121
  427.6 114.0 %collective-permute-start.58 = (bf16[1024,1024]{1,0:T(8,128)(2,1)}, bf16[1024,1024]{1,0:T(8,128)(2,1)}, u32[]{:S(2)}, u32[]{:S(2)}) collective-permute-start(bf16[1024,1024]{1,0:T(8,128)(2,1)} %add.552), channel_id=1, source_target_pairs={{8,16},{16,8},{9,17},{17,9},{10,18},{18,10},{11,19},{19,11},{12,20... | collective-permute-start | bytes 6291464 | tf_op jit(solution)/shard_map/ppermute | solution.py:121
  431.9 114.8 %collective-permute-start.55 = (bf16[1024,1024]{1,0:T(8,128)(2,1)}, bf16[1024,1024]{1,0:T(8,128)(2,1)}, u32[]{:S(2)}, u32[]{:S(2)}) collective-permute-start(bf16[1024,1024]{1,0:T(8,128)(2,1)} %add.550), channel_id=1, source_target_pairs={{8,16},{16,8},{9,17},{17,9},{10,18},{18,10},{11,19},{19,11},{12,20... | collective-permute-start | bytes 6291464 | tf_op jit(solution)/shard_map/ppermute | solution.py:121
  438.1 116.6 %collective-permute-start.68 = (bf16[1024,512]{1,0:T(8,128)(2,1)}, bf16[1024,512]{1,0:T(8,128)(2,1)}, u32[]{:S(2)}, u32[]{:S(2)}) collective-permute-start(bf16[1024,512]{1,0:T(8,128)(2,1)} %add.566), channel_id=1, source_target_pairs={{8,0},{16,24},{9,1},{17,25},{10,2},{18,26},{11,3},{19,27},{12,4},{... | collective-permute-start | bytes 3145736 | tf_op jit(solution)/shard_map/ppermute | solution.py:125
  552.9 87.2 %collective-permute-start.56 = (bf16[1024,1024]{1,0:T(8,128)(2,1)S(1)}, bf16[1024,1024]{1,0:T(8,128)(2,1)S(1)}, u32[]{:S(2)}, u32[]{:S(2)}) collective-permute-start(bf16[1024,1024]{1,0:T(8,128)(2,1)S(1)} %add.551), channel_id=1, source_target_pairs={{8,0},{16,24},{9,1},{17,25},{10,2},{18,26},{11,3},{19,27},{12,4},{... | collective-permute-start | bytes 6291464 | tf_op jit(solution)/shard_map/ppermute | solution.py:125
  559.2 113.6 %collective-permute-start.16 = (bf16[256,1024]{1,0:T(8,128)(2,1)S(1)}, bf16[256,1024]{1,0:T(8,128)(2,1)S(1)}, u32[]{:S(2)}, u32[]{:S(2)}) collective-permute-start(bf16[256,1024]{1,0:T(8,128)(2,1)S(1)} %get-tuple-element.227), channel_id=1, source_target_pairs={{0,5},{1,4},{4,1},{5,0},{2,7},{3,6},{6,3},{7,2},{8,13},{9,12},{12,... | collective-permute-start | bytes 1572872 | tf_op jit(solution)/shard_map/ppermute | solution.py:35
  559.5 102.9 %collective-permute-start.65 = (bf16[1024,512]{1,0:T(8,128)(2,1)S(1)}, bf16[1024,512]{1,0:T(8,128)(2,1)S(1)}, u32[]{:S(2)}, u32[]{:S(2)}) collective-permute-start(bf16[1024,512]{1,0:T(8,128)(2,1)S(1)} %add.564), channel_id=1, source_target_pairs={{8,0},{16,24},{9,1},{17,25},{10,2},{18,26},{11,3},{19,27},{12,4},{... | collective-permute-start | bytes 3145736 | tf_op jit(solution)/shard_map/ppermute | solution.py:125
  561.3 82.5 %collective-permute-start.48 = (bf16[512,32]{0,1:T(8,128)(2,1)S(1)}, bf16[512,32]{0,1:T(8,128)(2,1)S(1)}, u32[]{:S(2)}, u32[]{:S(2)}) collective-permute-start(bf16[512,32]{0,1:T(8,128)(2,1)S(1)} %constant_dynamic-slice_fusion.1), channel_id=1, source_target_pairs={{0,4},{4,0},{1,5},{5,1},{2,6},{6,2},{3,7},{7,3},{8,12},{12,8},{9,1... | collective-permute-start | bytes 98312 | tf_op jit(solution)/shard_map/ppermute | solution.py:35
  595.2 72.9 %collective-permute-start.39 = (bf16[512,512]{1,0:T(8,128)(2,1)S(1)}, bf16[512,512]{1,0:T(8,128)(2,1)S(1)}, u32[]{:S(2)}, u32[]{:S(2)}) collective-permute-start(bf16[512,512]{1,0:T(8,128)(2,1)S(1)} %constant_dynamic-slice_fusion.5), channel_id=1, source_target_pairs={{0,1},{1,0},{2,3},{3,2},{4,5},{5,4},{6,7},{7,6},{8,9},{9,8},{10,11... | collective-permute-start | bytes 1572872 | tf_op jit(solution)/shard_map/ppermute | solution.py:35
  643.1 206.9 %collective-permute-start.61 = (bf16[2,1024,1024]{2,1,0:T(8,128)(2,1)}, bf16[2,1024,1024]{2,1,0:T(8,128)(2,1)}, u32[]{:S(2)}, u32[]{:S(2)}) collective-permute-start(bf16[2,1024,1024]{2,1,0:T(8,128)(2,1)} %pad_maximum_fusion.2), channel_id=1, source_target_pairs={{0,4},{4,0},{1,5},{5,1},{2,6},{6,2},{3,7},{7,3},{8,12},{12,8},{9,1... | collective-permute-start | bytes 12582920 | tf_op jit(solution)/shard_map/ppermute | solution.py:35
  667.6 166.0 %collective-permute-start.70 = (bf16[2,1024,512]{2,1,0:T(8,128)(2,1)}, bf16[2,1024,512]{2,1,0:T(8,128)(2,1)}, u32[]{:S(2)}, u32[]{:S(2)}) collective-permute-start(bf16[2,1024,512]{2,1,0:T(8,128)(2,1)} %pad_maximum_fusion.9), channel_id=1, source_target_pairs={{0,4},{4,0},{1,5},{5,1},{2,6},{6,2},{3,7},{7,3},{8,12},{12,8},{9,1... | collective-permute-start | bytes 6291464 | tf_op jit(solution)/shard_map/ppermute | solution.py:35
  669.7 117.8 %collective-permute-start.40 = (bf16[512,256]{1,0:T(8,128)(2,1)S(1)}, bf16[512,256]{1,0:T(8,128)(2,1)}, u32[]{:S(2)}, u32[]{:S(2)}) collective-permute-start(bf16[512,256]{1,0:T(8,128)(2,1)S(1)} %constant_dynamic-slice_fusion.4), channel_id=1, source_target_pairs={{0,4},{4,0},{1,5},{5,1},{2,6},{6,2},{3,7},{7,3},{8,12},{12,8},{9,1... | collective-permute-start | bytes 786440 | tf_op jit(solution)/shard_map/ppermute | solution.py:35
  673.6 125.1 %collective-permute-start.15 = (bf16[256,1024]{1,0:T(8,128)(2,1)}, bf16[256,1024]{1,0:T(8,128)(2,1)}, u32[]{:S(2)}, u32[]{:S(2)}) collective-permute-start(bf16[256,1024]{1,0:T(8,128)(2,1)} %get-tuple-element.228), channel_id=1, source_target_pairs={{0,4},{1,5},{4,0},{5,1},{2,6},{3,7},{6,2},{7,3},{8,12},{9,13},{12,... | collective-permute-start | bytes 1572872 | tf_op jit(solution)/shard_map/ppermute | solution.py:35
  677.3 131.3 %collective-permute-start.32 = (bf16[512,512]{1,0:T(8,128)(2,1)}, bf16[512,512]{1,0:T(8,128)(2,1)}, u32[]{:S(2)}, u32[]{:S(2)}) collective-permute-start(bf16[512,512]{1,0:T(8,128)(2,1)} %constant_dynamic-slice_fusion.7), channel_id=1, source_target_pairs={{0,4},{4,0},{1,5},{5,1},{2,6},{6,2},{3,7},{7,3},{8,12},{12,8},{9,1... | collective-permute-start | bytes 1572872 | tf_op jit(solution)/shard_map/ppermute | solution.py:35
  828.2 70.3 %collective-permute-start.60 = (bf16[2,1024,1024]{2,1,0:T(8,128)(2,1)}, bf16[2,1024,1024]{2,1,0:T(8,128)(2,1)S(1)}, u32[]{:S(2)}, u32[]{:S(2)}) collective-permute-start(bf16[2,1024,1024]{2,1,0:T(8,128)(2,1)} %pad_maximum_fusion.2), channel_id=1, source_target_pairs={{0,2},{2,0},{1,3},{3,1},{4,6},{6,4},{5,7},{7,5},{8,10},{10,8},{9,1... | collective-permute-start | bytes 12582920 | tf_op jit(solution)/shard_map/ppermute | solution.py:35
  (115 other events, 2099.3 us)

commit v2 on v1

v2 whole, which is shorter than its diff:
```python
import math
from functools import partial

import jax
import jax.numpy as jnp
from jax import lax
from jax.experimental import pallas as pl
from jax.experimental.pallas import tpu as pltpu
from jax.sharding import Mesh, PartitionSpec as P

D = 1024
HEADS = 16
KV_HEADS = 8
HEAD_DIM = 64
F = 512
TOP = 8
EXPERTS = 16
BLOCK = 256
QW = HEADS * HEAD_DIM
KVW = KV_HEADS * HEAD_DIM
EXTRA = 16
CHUNKS = 2
PAIR = 2 * HEAD_DIM

norm_eps = 1e-06
masked_score = -1e30
score_scale = HEAD_DIM ** (-0.5)
bf16, f32 = jnp.bfloat16, jnp.float32
VMEM = 56 * 1024 * 1024


def dot(left, right, dims=((1,), (0,))):
    return lax.dot_general(left, right, (dims, ((), ())), preferred_element_type=f32)


def turn(value, axes, steps, sizes):
    pairs = []
    for source in range(math.prod(sizes)):
        place, rest = [], source
        for size in reversed(sizes):
            place.append(rest % size)
            rest //= size
        place.reverse()
        target = 0
        for at, size, step in zip(place, sizes, steps):
            target = target * size + (at + step) % size
        pairs.append((source, target))
    return lax.ppermute(value, axes, pairs)


def own_part(value, axis, index, parts):
    size = value.shape[axis] // parts
    return lax.dynamic_slice_in_dim(value, index * size, size, axis)


def whole(shape):
    return pl.BlockSpec(shape, lambda *_: (0,) * len(shape))


SCALARS = pl.BlockSpec(memory_space=pltpu.SMEM)
STAY = pl.BlockSpec(memory_space=pl.ANY)


def call(kernel, out_shape, in_specs, operands, out_specs=None, scratch=(), grid=None, prefetch=0, aliases=None, flops=0):
    out_specs = [whole(s.shape) for s in out_shape] if out_specs is None else out_specs
    moved = sum(math.prod(s.shape) * s.dtype.itemsize for s in list(operands) + list(out_shape))
    spec = pltpu.PrefetchScalarGridSpec(
        num_scalar_prefetch=prefetch,
        grid=grid or (1,),
        in_specs=in_specs,
        out_specs=out_specs,
        scratch_shapes=list(scratch),
    )
    return pl.pallas_call(
        kernel,
        out_shape=list(out_shape),
        grid_spec=spec,
        input_output_aliases=aliases or {},
        compiler_params=pltpu.CompilerParams(vmem_limit_bytes=VMEM),
        cost_estimate=pl.CostEstimate(flops=flops, transcendentals=0, bytes_accessed=moved),
    )(*operands)


def array(shape, dtype):
    return jax.ShapeDtypeStruct(shape, dtype)


def normalize(rows):
    scale_inv = lax.rsqrt(jnp.mean(rows * rows, -1, keepdims=True) + norm_eps)
    return (rows * scale_inv, scale_inv)


def norm_back(normed, scale_inv, grad_normed):
    return scale_inv * (grad_normed - normed * jnp.mean(grad_normed * normed, -1, keepdims=True))


def lanes(shape):
    return lax.broadcasted_iota(jnp.int32, shape, len(shape) - 1)


def halves(values):
    low = lanes(values.shape) % HEAD_DIM < HEAD_DIM // 2
    half = HEAD_DIM // 2
    return jnp.where(low, pltpu.roll(values, PAIR - half, 1), pltpu.roll(values, half, 1))


def rotary_tables(places):
    at = jnp.arange(PAIR, dtype=jnp.int32) % HEAD_DIM
    middle = HEAD_DIM // 2
    frequency = 10000.0 ** (-(2.0 * (at % middle).astype(f32)) / HEAD_DIM)
    angles = places.astype(f32)[:, None] * frequency[None, :]
    sign = jnp.where(at < middle, -1.0, 1.0)[None, :]
    return (jnp.cos(angles), jnp.sin(angles) * sign)


def load_rows(pieces, offsets, target, sems):
    copies = []
    for i, piece in enumerate(pieces):
        copy = pltpu.make_async_copy(piece, target.at[pl.ds(pl.multiple_of(offsets[i], 16), piece.shape[0]), :], sems.at[i])
        copy.start()
        copies.append(copy)
    return copies


def project(hidden_prev, hidden_own, gain, cosines, sines, pieces, offsets):
    length, count = hidden_own.shape[0], len(pieces)

    def kernel(offsets_ref, prev_ref, own_ref, gain_ref, cos_ref, sin_ref, *rest):
        piece_refs, (q_ref, kv_ref, in_ref, weight, sems) = rest[:count], rest[count:]
        copies = load_rows(piece_refs, offsets_ref, weight, sems)
        for i, ref in enumerate((prev_ref, own_ref)):
            normed, _ = normalize(ref[...].astype(f32))
            in_ref[i * length : (i + 1) * length, :] = (normed * gain_ref[...]).astype(bf16)
        for copy in copies:
            copy.wait()
        values = dot(in_ref[length:, :], weight[:, :QW])
        cos_own, sin_own = cos_ref[length:, :], sin_ref[length:, :]
        for g in range(QW // PAIR):
            u = values[:, g * PAIR : (g + 1) * PAIR]
            q_ref[:, g * PAIR : (g + 1) * PAIR] = (u * cos_own + halves(u) * sin_own).astype(bf16)
        values = dot(in_ref[...], weight[:, QW:])
        for g in range(KVW // PAIR):
            u = values[:, g * PAIR : (g + 1) * PAIR]
            kv_ref[:, g * PAIR : (g + 1) * PAIR] = (u * cos_ref[...] + halves(u) * sin_ref[...]).astype(bf16)
        kv_ref[:, KVW:] = values[:, KVW:].astype(bf16)

    width = QW + 2 * KVW
    return call(
        kernel,
        [array((length, QW), bf16), array((2 * length, 2 * KVW), bf16), array((2 * length, D), bf16)],
        [SCALARS] + [whole(v.shape) for v in (hidden_prev, hidden_own, gain, cosines, sines)] + [STAY] * count,
        (offsets, hidden_prev, hidden_own, gain, cosines, sines, *pieces),
        scratch=[pltpu.VMEM((D, width), bf16), pltpu.SemaphoreType.DMA((count,))],
        flops=6 * length * D * D,
    )


def doubled(values, which):
    low = lanes(values.shape) < HEAD_DIM
    swapped = pltpu.roll(values, HEAD_DIM, 1)
    return jnp.where(low, values, swapped) if which == 0 else jnp.where(low, swapped, values)


def two_rows(pair):
    low = lanes(pair.shape) < HEAD_DIM
    zero = jnp.zeros_like(pair)
    return jnp.concatenate([jnp.where(low, pair, zero), jnp.where(low, zero, pair)], 0)


def named_experts(routes):
    shape = (routes.shape[0], 128)
    named = routes[:, 0:1] == lanes(shape)
    for k in range(1, TOP):
        named = named | (routes[:, k : k + 1] == lanes(shape))
    return named


def attend(query, kv, hidden_own, gain, router_w, routes, pieces, offsets, flag):
    length, count = query.shape[0], len(pieces)

    def kernel(offsets_ref, flag_ref, q_ref, kv_ref, own_ref, gain_ref, router_ref, routes_ref, *rest):
        piece_refs = rest[:count]
        att_ref, lse_ref, res_ref, gate_ref, pay_ref, weight, sems = rest[count:]
        copies = load_rows(piece_refs, offsets_ref, weight, sems)
        wide = (2 * length, 2 * length)
        bias = jnp.where((lanes((1, 2 * length)) >= length) | (flag_ref[0] > 0), 0.0, masked_score)
        lse_ref[...] = jnp.zeros(lse_ref.shape, f32)

        def pair_of_keys(jj, carry):
            at = pl.multiple_of(jj * PAIR, PAIR)
            keys = kv_ref[:, pl.ds(at, PAIR)].astype(f32)
            vals = kv_ref[:, pl.ds(KVW + at, PAIR)].astype(f32)
            for t in range(2):
                place = pl.multiple_of((2 * jj + t) * PAIR, PAIR)
                both = two_rows(q_ref[:, pl.ds(place, PAIR)].astype(f32)).astype(bf16)
                scores = dot(both, doubled(keys, t).astype(bf16), ((1,), (1,))) * score_scale + bias
                largest = jnp.max(scores, -1, keepdims=True)
                exponent = jnp.exp(scores - largest)
                totals = jnp.sum(exponent, -1, keepdims=True)
                probs = (exponent * (1.0 / totals)).astype(bf16)
                lse = largest + jnp.log(totals)
                lse_ref[...] = jnp.where(lanes(lse_ref.shape) == 2 * jj + t, lse, lse_ref[...])
                val = doubled(vals, t)
                low = lanes(val.shape) < HEAD_DIM
                zero = jnp.zeros_like(val)
                out = dot(probs[:length], jnp.where(low, val, zero).astype(bf16))
                out = out + dot(probs[length:], jnp.where(low, zero, val).astype(bf16))
                att_ref[:, pl.ds(place, PAIR)] = out.astype(bf16)
            return carry

        lax.fori_loop(0, KVW // PAIR, pair_of_keys, 0)
        for copy in copies:
            copy.wait()
        residual = own_ref[...].astype(f32) + dot(att_ref[...], weight[...])
        res_ref[...] = residual
        normed, _ = normalize(residual)
        rows = (normed * gain_ref[...]).astype(bf16)
        pay_ref[:length, :] = rows
        logits = dot(rows, router_ref[...], ((1,), (1,)))
        real = lanes(logits.shape) < EXPERTS
        logits = jnp.where(real, logits, masked_score)
        raised = jnp.where(real, jnp.exp(logits - jnp.max(logits, -1, keepdims=True)), 0.0)
        router = raised * (1.0 / jnp.sum(raised, -1, keepdims=True))
        gate_ref[...] = router
        gates = jnp.where(named_experts(routes_ref[...]), router, 0.0).T[:EXTRA]
        high = gates.astype(bf16)
        pay_ref[length:, :length] = high
        pay_ref[length:, length : 2 * length] = (gates - high.astype(f32)).astype(bf16)
        pay_ref[length:, 2 * length :] = jnp.zeros((EXTRA, D - 2 * length), bf16)

    return call(
        kernel,
        [
            array((length, QW), bf16),
            array((2 * length, 128), f32),
            array((length, D), f32),
            array((length, 128), f32),
            array((length + EXTRA, D), bf16),
        ],
        [SCALARS, SCALARS] + [whole(v.shape) for v in (query, kv, hidden_own, gain, router_w, routes)] + [STAY] * count,
        (offsets, flag, query, kv, hidden_own, gain, router_w, routes, *pieces),
        scratch=[pltpu.VMEM((QW, D), bf16), pltpu.SemaphoreType.DMA((count,))],
        flops=8 * length * D * D,
    )


def expert(rows, grads, w_gate_up, w_down, index, chunk, chunks):
    sources, tall = len(rows), rows[0].shape[1]
    blocks = sources * rows[0].shape[0]
    length = tall - EXTRA
    step = 2
    part = F // chunks
    turns = rows[0].shape[0] // step

    def kernel(index_ref, *refs):
        row_refs, grad_refs = refs[:sources], refs[sources : 2 * sources]
        gate_ref, up_ref, down_ref, dgu_ref, hid_ref, sum_ref, out_ref, acc, both_ref, grad_ref, table_ref = refs[2 * sources :]
        i = pl.program_id(0)
        for source, (row_ref, source_ref) in enumerate(zip(row_refs, grad_refs)):

            @pl.when((i >= source * turns) & (i < (source + 1) * turns))
            def _():
                for b in range(step):
                    both_ref[b * length : (b + 1) * length, :] = row_ref[b, :length, :]
                    grad_ref[b * length : (b + 1) * length, :] = source_ref[b]
                    high, low = row_ref[b, length:, :length], row_ref[b, length:, length : 2 * length]
                    table_ref[b] = high.astype(f32) + low.astype(f32)

        both, grad = both_ref[...], grad_ref[...]
        columns = []
        for b in range(step):
            table = table_ref[b]
            mine = lax.broadcasted_iota(jnp.int32, table.shape, 0) == index_ref[1]
            row = jnp.sum(jnp.where(mine, table, 0.0), 0, keepdims=True)
            columns.append(jnp.broadcast_to(row, (128, length)).T[:, :1])
        gate = jnp.concatenate(columns, 0)
        gate_part, up_part = dot(both, gate_ref[0]), dot(both, up_ref[0])
        sigmoid_g = jax.nn.sigmoid(gate_part)
        silu_g = gate_part * sigmoid_g
        hidden = silu_g * up_part
        raw = dot(grad, down_ref[0])
        sums = jnp.sum(raw * hidden, 1, keepdims=True)
        gated = (gate * hidden).astype(bf16)
        grad_hidden = gate * raw
        grad_gate = (grad_hidden * up_part * sigmoid_g * (1.0 + gate_part * (1.0 - sigmoid_g))).astype(bf16)
        grad_up = (grad_hidden * silu_g).astype(bf16)
        for b in range(step):
            at = slice(b * length, (b + 1) * length)
            dgu_ref[b, :, :part] = grad_gate[at]
            dgu_ref[b, :, part:] = grad_up[at]
            hid_ref[b] = gated[at]
            sum_ref[b] = jnp.broadcast_to(sums[at], (length, 128)).T[:8]
        terms = (
            dot(both, grad_gate, ((0,), (0,))),
            dot(both, grad_up, ((0,), (0,))),
            dot(grad, gated, ((0,), (0,))),
        )
        for p, term in enumerate(terms):
            at = slice(p * part, (p + 1) * part)

            @pl.when(i == 0)
            def _():
                acc[:, at] = term

            @pl.when((i > 0) & (i < blocks // step - 1))
            def _():
                acc[:, at] += term

            @pl.when(i == blocks // step - 1)
            def _():
                out_ref[:, at] = (acc[:, at] + term).astype(bf16)

    def block(*shape):
        return pl.BlockSpec((step,) + shape, lambda i, index: (i,) + (0,) * len(shape))

    def source_block(source, *shape):
        def at(i, index):
            return (jnp.clip(i - source * turns, 0, turns - 1),) + (0,) * len(shape)

        return pl.BlockSpec((step,) + shape, at)

    def columns_of(at):
        return pl.BlockSpec((1, D, part), lambda i, index: (index[0], 0, at))

    return call(
        kernel,
        [
            array((blocks, length, 2 * part), bf16),
            array((blocks, length, part), bf16),
            array((blocks, 8, length), f32),
            array((D, 3 * part), bf16),
        ],
        [source_block(s, tall, D) for s in range(sources)]
        + [source_block(s, length, D) for s in range(sources)]
        + [columns_of(chunk), columns_of(chunks + chunk), columns_of(chunk)],
        (index, *rows, *grads, w_gate_up, w_gate_up, w_down),
        out_specs=[
            block(length, 2 * part),
            block(length, part),
            block(8, length),
            pl.BlockSpec((D, 3 * part), lambda i, index: (0, 0)),
        ],
        scratch=[
            pltpu.VMEM((D, 3 * part), f32),
            pltpu.VMEM((step * length, D), bf16),
            pltpu.VMEM((step * length, D), bf16),
            pltpu.VMEM((step, EXTRA, length), f32),
        ],
        grid=(blocks // step,),
        prefetch=1,
        flops=blocks * length * D * part * 12,
    )


def row_grads(parts, sums, weights, indices, chunks):
    blocks, length = parts[0].shape[0], parts[0].shape[1]
    count, experts = len(parts), len(parts) // chunks
    wide = parts[0].shape[2] * chunks // F
    part = F // chunks
    tall = length + (EXTRA if sums else 0)
    step = 2

    def kernel(indices_ref, *refs):
        part_refs, weight_refs = refs[:count], refs[count : count + experts]
        sum_refs, out_ref = refs[count + experts : -1], refs[-1]
        total = None
        for e in range(experts):
            for c in range(chunks):
                ref = part_refs[e * chunks + c]
                both = jnp.concatenate([ref[b] for b in range(step)], 0)
                for w in range(wide):
                    at = w * F + c * part
                    term = dot(both[:, w * part : (w + 1) * part], weight_refs[e][0, :, at : at + part], ((1,), (1,)))
                    total = term if total is None else total + term
        for b in range(step):
            out_ref[b, :length, :] = total[b * length : (b + 1) * length].astype(bf16)
            if sums:
                table = jnp.zeros((EXTRA, length), f32)
                at = lax.broadcasted_iota(jnp.int32, table.shape, 0)
                for e in range(experts):
                    grads = sum_refs[e * chunks][b, :1, :]
                    for c in range(1, chunks):
                        grads = grads + sum_refs[e * chunks + c][b, :1, :]
                    table = jnp.where(at == indices_ref[2 * e + 1], grads, table)
                high = table.astype(bf16)
                out_ref[b, length:, :length] = high
                out_ref[b, length:, length : 2 * length] = (table - high.astype(f32)).astype(bf16)
                out_ref[b, length:, 2 * length :] = jnp.zeros((EXTRA, D - 2 * length), bf16)

    def block(*shape):
        return pl.BlockSpec((step,) + shape, lambda i, index: (i,) + (0,) * len(shape))

    def weight(e):
        return pl.BlockSpec((1,) + weights.shape[1:], lambda i, index: (index[2 * e], 0, 0))

    return call(
        kernel,
        [array((blocks, tall, D), bf16)],
        [block(*v.shape[1:]) for v in parts] + [weight(e) for e in range(experts)] + [block(8, length)] * len(sums),
        (indices, *parts, *[weights] * experts, *sums),
        out_specs=[block(tall, D)],
        grid=(blocks // step,),
        prefetch=1,
        flops=blocks * length * D * part * wide * 2 * count,
    )[0]


def middle_back(returned, residual, router, routes, cotangent, gain, router_w, pieces, offsets):
    length, count, terms = residual.shape[0], len(pieces), len(returned)

    def kernel(offsets_ref, *rest):
        term_refs, rest = rest[:terms], rest[terms:]
        res_ref, gate_ref, routes_ref, cot_ref, gain_ref, router_ref = rest[:6]
        piece_refs = rest[6 : 6 + count]
        gres_ref, gatt_ref, small_ref, weight, sems = rest[6 + count :]
        copies = load_rows(piece_refs, offsets_ref, weight, sems)
        total = term_refs[0][...].astype(f32)
        for ref in term_refs[1:]:
            total = total + ref[...].astype(f32)
        table = total[length:, :length] + total[length:, length : 2 * length]
        gate_grads = jnp.concatenate([table, jnp.zeros((128 - EXTRA, length), f32)], 0).T
        grad_router = jnp.where(named_experts(routes_ref[...]), gate_grads, 0.0)
        router = gate_ref[...]
        grad_logits = (router * (grad_router - jnp.sum(router * grad_router, -1, keepdims=True))).astype(bf16)
        grad_input = total[:length] + dot(grad_logits, router_ref[...])
        normed, inverse = normalize(res_ref[...])
        gain_row = gain_ref[...]
        rows = (normed * gain_row).astype(bf16)
        small_ref[...] = dot(rows, grad_logits, ((0,), (0,)))
        gain_grad = jnp.sum(grad_input * normed, 0, keepdims=True)
        column = jnp.broadcast_to(gain_grad, (128, D)).T
        small_ref[...] = jnp.where(lanes((D, 128)) == EXPERTS, column, small_ref[...])
        grad_residual = cot_ref[...].astype(f32) + norm_back(normed, inverse, grad_input * gain_row)
        gres_ref[...] = grad_residual
        grad_attn = grad_residual.astype(bf16)
        for copy in copies:
            copy.wait()
        gatt_ref[...] = dot(grad_attn, weight[...], ((1,), (1,))).astype(bf16)

    operands = (*returned, residual, router, routes, cotangent, gain, router_w)
    return call(
        kernel,
        [array((length, D), f32), array((length, QW), bf16), array((D, 128), f32)],
        [SCALARS] + [whole(v.shape) for v in operands] + [STAY] * count,
        (offsets, *operands, *pieces),
        scratch=[pltpu.VMEM((QW, D), bf16), pltpu.SemaphoreType.DMA((count,))],
        flops=5 * length * D * D,
    )


def attend_back(query, kv, grad, lse, cosines, sines, flag):
    length = query.shape[0]

    def kernel(flag_ref, q_ref, kv_ref, grad_ref, lse_ref, cos_ref, sin_ref, dq_ref, dkv_ref):
        bias = jnp.where((lanes((1, 2 * length)) >= length) | (flag_ref[0] > 0), 0.0, masked_score)
        cos_own, sin_own = cos_ref[length:, :], sin_ref[length:, :]

        def back(values, cos, sin):
            return (values * cos - halves(values) * sin).astype(bf16)

        def pair_of_keys(jj, carry):
            at = pl.multiple_of(jj * PAIR, PAIR)
            keys = kv_ref[:, pl.ds(at, PAIR)].astype(f32)
            vals = kv_ref[:, pl.ds(KVW + at, PAIR)].astype(f32)
            key_grads, val_grads = [], []
            for t in range(2):
                place = pl.multiple_of((2 * jj + t) * PAIR, PAIR)
                both = two_rows(q_ref[:, pl.ds(place, PAIR)].astype(f32)).astype(bf16)
                outs = two_rows(grad_ref[:, pl.ds(place, PAIR)].astype(f32)).astype(bf16)
                key = doubled(keys, t).astype(bf16)
                val = doubled(vals, t).astype(bf16)
                own = lanes(lse_ref.shape) == 2 * jj + t
                total = jnp.sum(jnp.where(own, lse_ref[...], 0.0), -1, keepdims=True)
                scores = dot(both, key, ((1,), (1,))) * score_scale + bias
                probs = jnp.exp(scores - total)
                grad_probs = dot(outs, val, ((1,), (1,)))
                inner = jnp.sum(probs * grad_probs, -1, keepdims=True)
                grad_scores = (probs * (grad_probs - inner)).astype(bf16)
                grad_query = dot(grad_scores, key) * score_scale
                low = lanes((length, PAIR)) < HEAD_DIM
                grad_query = jnp.where(low, grad_query[:length], grad_query[length:])
                dq_ref[:, pl.ds(place, PAIR)] = back(grad_query, cos_own, sin_own)
                key_grad = dot(grad_scores, both, ((0,), (0,))) * score_scale
                val_grad = dot(probs.astype(bf16), outs, ((0,), (0,)))
                key_grads.append(key_grad + pltpu.roll(key_grad, HEAD_DIM, 1))
                val_grads.append(val_grad + pltpu.roll(val_grad, HEAD_DIM, 1))
            low = lanes((2 * length, PAIR)) < HEAD_DIM
            dkv_ref[:, pl.ds(at, PAIR)] = back(jnp.where(low, *key_grads), cos_ref[...], sin_ref[...])
            dkv_ref[:, pl.ds(KVW + at, PAIR)] = jnp.where(low, *val_grads).astype(bf16)
            return carry

        lax.fori_loop(0, KVW // PAIR, pair_of_keys, 0)

    operands = (query, kv, grad, lse, cosines, sines)
    return call(
        kernel,
        [array((length, QW), bf16), array((2 * length, 2 * KVW), bf16)],
        [SCALARS] + [whole(v.shape) for v in operands],
        (flag, *operands),
        flops=20 * length * D * D,
    )


def project_back(inputs, grad_query, grad_kv, hidden_prev, hidden_own, attended, grad_residual, small, pieces, offsets, parts):
    length, count = grad_query.shape[0], len(pieces)
    width = QW + 2 * KVW

    def kernel(offsets_ref, in_ref, dq_ref, dkv_ref, prev_ref, own_ref, att_ref, res_ref, small_ref, *rest):
        piece_refs, (grad_ref, gown_ref, gprev_ref, weight, sems) = rest[:count], rest[count:]
        copies = load_rows(piece_refs, offsets_ref, weight, sems)
        rows = D // parts

        def write(at, values):
            for p in range(parts):
                grad_ref[p, :, at : at + values.shape[1]] = values[p * rows : (p + 1) * rows].astype(bf16)

        write(0, dot(in_ref[length:, :], dq_ref[...], ((0,), (0,))))
        write(QW, dot(in_ref[...], dkv_ref[...], ((0,), (0,))))
        write(width, dot(att_ref[...], res_ref[...].astype(bf16), ((0,), (0,))))
        for copy in copies:
            copy.wait()
        from_kv = dot(dkv_ref[...], weight[:, QW:], ((1,), (1,)))
        own = from_kv[length:] + dot(dq_ref[...], weight[:, :QW], ((1,), (1,)))
        gown_ref[...] = own
        gprev_ref[...] = from_kv[:length].astype(bf16)
        normed_own, _ = normalize(own_ref[...].astype(f32))
        normed_prev, _ = normalize(prev_ref[...].astype(f32))
        gain_grad = jnp.sum(own * normed_own + from_kv[:length] * normed_prev, 0, keepdims=True)
        column = jnp.broadcast_to(gain_grad, (128, D)).T
        write(width + D, jnp.where(lanes((D, 128)) == EXPERTS + 1, column, small_ref[...]))

    operands = (inputs, grad_query, grad_kv, hidden_prev, hidden_own, attended, grad_residual, small)
    return call(
        kernel,
        [array((parts, D // parts, width + D + 128), bf16), array((length, D), f32), array((length, D), bf16)],
        [SCALARS] + [whole(v.shape) for v in operands] + [STAY] * count,
        (offsets, *operands, *pieces),
        scratch=[pltpu.VMEM((D, width), bf16), pltpu.SemaphoreType.DMA((count,))],
        flops=10 * length * D * D,
    )


def first_back(grad_own, grad_later, grad_residual, hidden_own, gain):
    def kernel(own_ref, later_ref, res_ref, hid_ref, gain_ref, out_ref):
        normed, inverse = normalize(hid_ref[...].astype(f32))
        grad = (own_ref[...] + later_ref[...].astype(f32)) * gain_ref[...]
        out_ref[...] = res_ref[...] + norm_back(normed, inverse, grad)

    operands = (grad_own, grad_later, grad_residual, hidden_own, gain)
    return call(kernel, [array(grad_own.shape, f32)], [whole(v.shape) for v in operands], operands)[0]


def place(sources, experts, outs, shapes, chunk, chunks):
    part = F // chunks
    count = sum(source.shape[0] for source in sources)

    def kernel(experts_ref, *refs):
        source_refs = refs[: len(sources)]
        gate_up_ref, down_ref, wide, sems = refs[len(sources) + len(outs) :]
        copies = []
        values = [ref.at[i] for ref in source_refs for i in range(ref.shape[0])]
        for i, source in enumerate(values):
            wide[i] = source[...].astype(f32)
            for p, target in enumerate(
                (
                    gate_up_ref.at[experts_ref[i], :, chunk * part : (chunk + 1) * part],
                    gate_up_ref.at[experts_ref[i], :, F + chunk * part : F + (chunk + 1) * part],
                    down_ref.at[experts_ref[i], :, chunk * part : (chunk + 1) * part],
                )
            ):
                copy = pltpu.make_async_copy(wide.at[i, :, p * part : (p + 1) * part], target, sems.at[i, p])
                copy.start()
                copies.append(copy)
        for copy in copies:
            copy.wait()

    return call(
        kernel,
        shapes,
        [SCALARS] + [whole(v.shape) for v in sources] + [STAY] * len(outs),
        (experts, *sources, *outs),
        out_specs=[STAY, STAY],
        scratch=[pltpu.VMEM((count, D, 3 * part), f32), pltpu.SemaphoreType.DMA((count, 3))],
        aliases={1 + len(sources) + i: i for i in range(len(outs))},
    )


def unpack(sources, offsets, rows):
    count = sum(source.shape[0] for source in sources)
    deep, wide = sources[0].shape[1:]
    widths = (QW + 2 * KVW, D, wide - QW - 2 * KVW - D)

    def kernel(offsets_ref, *refs):
        source_refs, out_refs, (values_ref, sems) = refs[: len(sources)], refs[len(sources) : -2], refs[-2:]
        copies = []
        for i, source in enumerate([ref.at[i] for ref in source_refs for i in range(ref.shape[0])]):
            values_ref[i] = source[...].astype(f32)
            start = 0
            for p, (out_ref, width) in enumerate(zip(out_refs, widths)):
                target = out_ref.at[pl.ds(pl.multiple_of(offsets_ref[i], 8), deep), :]
                copy = pltpu.make_async_copy(values_ref.at[i, :, start : start + width], target, sems.at[i, p])
                copy.start()
                copies.append(copy)
                start += width
        for copy in copies:
            copy.wait()

    return call(
        kernel,
        [array((rows, width), f32) for width in widths],
        [SCALARS] + [whole(v.shape) for v in sources],
        (offsets, *sources),
        out_specs=[STAY] * 3,
        scratch=[pltpu.VMEM((count, deep, wide), f32), pltpu.SemaphoreType.DMA((count, 3))],
    )


def tie(values, after):
    return lax.optimization_barrier((values, after))[0]


def doubling_sum(value, axis):
    count, step = lax.axis_size(axis), 1
    if count & (count - 1):
        return lax.psum(value, axis)
    while step < count:
        value = value + lax.ppermute(value, axis, [(i, i ^ step) for i in range(count)])
        step *= 2
    return value


def body(
    hidden_in, routes, w_qkv, w_out, w_router, attn_gain, ffn_gain, w_gate_up, w_down, cotangent
):
    length = hidden_in.shape[0]
    line, shards = lax.axis_size("line"), lax.axis_size("fsdp")
    side, cores = lax.axis_size("side"), lax.axis_size("core")
    shard, side_at, core_at = lax.axis_index("fsdp"), lax.axis_index("side"), lax.axis_index("core")
    near = [(a, s) for s in range(shards) for a in range(side)]
    local_experts = w_gate_up.shape[0]
    count = local_experts // (side * cores)
    barrier = lax.optimization_barrier

    def other_core(value, core=1):
        return turn(value, "core", (core,), (cores,))

    def other_side(value, step=1):
        return turn(value, "side", (step,), (side,))

    def fetch(piece, after=()):
        rows = piece.shape[0]
        out, offsets = [piece], [shard * rows]
        part = own_part(piece, 0, core_at * side + side_at, cores * side)
        if after:
            part = tie(part, after)
        small_rows = part.shape[0]
        for step in range(1, shards):
            base = (shard - step) % shards * rows
            first = turn(part, "fsdp", (step,), (shards,))
            for a in range(side):
                theirs = other_side(first, a) if a else first
                for core in range(cores):
                    out.append(other_core(theirs, core) if core else theirs)
                    at = (core_at - core) % cores * side + (side_at - a) % side
                    offsets.append(base + at * small_rows)
        return out, jnp.stack(offsets).astype(jnp.int32)

    def over_cores(first):
        return [other_core(first, core) if core else first for core in range(cores)]

    def core_sums(blocks):
        total = blocks[: len(near)]
        for core in range(1, cores):
            total = total + other_core(blocks[core * len(near) : (core + 1) * len(near)], -core % cores)
        return total

    def shard_sums(total, step_of=None):
        total = total.reshape((shards, side) + total.shape[1:])
        out = total[0].astype(f32)
        for s in range(1, shards):
            out = out + turn(total[s], "fsdp", (-s % shards,), (shards,)).astype(f32)
        return out.astype(bf16)

    def send_back(total):
        out = [total[0]]
        for i, (a, s) in enumerate(near):
            if (a, s) != (0, 0):
                out.append(turn(total[i], ("side", "fsdp"), (-a % side, -s % shards), (side, shards)))
        return out

    parity = shard % 2
    flag = parity.astype(jnp.int32)[None]
    later = [(i, i + 1) for i in range(0, shards, 2)]
    before = [(i + 1, i) for i in range(0, shards, 2)]
    small_rows = w_router.shape[0]
    small = jnp.concatenate([w_router.T, attn_gain[None], ffn_gain[None]], 0)
    qkv_pieces, qkv_offsets = fetch(w_qkv)
    hidden_prev = lax.ppermute(hidden_in, "fsdp", later)
    full_small = jnp.zeros((EXPERTS + 2, D), bf16)
    for step in range(shards):
        theirs = turn(small, "fsdp", (step,), (shards,)) if step else small
        full_small = lax.dynamic_update_slice_in_dim(full_small, theirs, (shard - step) % shards * small_rows, 1)
    gain_attn = full_small[EXPERTS : EXPERTS + 1].astype(f32)
    gain_ffn = full_small[EXPERTS + 1 :].astype(f32)
    router_w = jnp.pad(full_small[:EXPERTS], ((0, 128 - EXPERTS), (0, 0)))
    sideways = jnp.stack([other_side(cotangent, a) if a else cotangent for a in range(side)])
    out_pieces, out_offsets = fetch(w_out, (hidden_prev, qkv_pieces[1:]))
    sideways = tie(sideways, out_pieces[1:2])
    grads_near = [turn(sideways, "fsdp", (s,), (shards,)) if s else sideways for s in range(shards)]
    grads_near = over_cores(jnp.concatenate(grads_near, 0))
    rows_at = jnp.arange(length, dtype=jnp.int32)
    cosines, sines = rotary_tables(jnp.concatenate([rows_at, parity * length + rows_at]))

    queries, kv, inputs = project(hidden_prev, hidden_in, gain_attn, cosines, sines, qkv_pieces, qkv_offsets)
    attended, lse, residual, router, payload = attend(
        queries, kv, hidden_in, gain_ffn, router_w, routes, out_pieces, out_offsets, flag
    )
    rows_near = [turn(payload, ("side", "fsdp"), (a, s), (side, shards)) if (a, s) != (0, 0) else payload for a, s in near]
    rows_near = over_cores(jnp.stack(rows_near))

    mine_at = (side_at * cores + core_at) * count
    indices = [jnp.stack([mine_at + e, shard * local_experts + mine_at + e]).astype(jnp.int32) for e in range(count)]
    minis = [(e, c) for e in range(count) for c in range(CHUNKS)]
    number = len(minis)
    order = jnp.stack([((side_at - a) % side * cores + (core_at - core) % cores) for core in range(cores) for a in range(side)])
    order = order.astype(jnp.int32)
    shapes = [array((local_experts, D, 2 * F), f32), array((local_experts, D, F), f32)]

    now = {"indices": indices, "offsets": (out_offsets, qkv_offsets), "order": order, "chunks": {}, "outs": ()}
    now.update(half={}, total={}, full={}, pair={}, grads_gu=[], hiddens=[], sums=[])
    flying = {}

    def mini():
        i = len(now["sums"])
        e, c = minis[i]
        found = expert(rows_near, grads_near, w_gate_up, w_down, now["indices"][e], c, CHUNKS)
        now["grads_gu"].append(found[0])
        now["hiddens"].append(found[1])
        now["sums"].append(found[2])
        now["chunks"][i] = found[3]

    def returns():
        grads = row_grads(now["grads_gu"], now["sums"], w_gate_up, jnp.concatenate(now["indices"]), CHUNKS)
        flying["returned"] = send_back(core_sums(grads))
        now["indices"] = tie(now["indices"], grads)
        now["mixed"] = row_grads(now["hiddens"], (), w_down, jnp.concatenate(now["indices"]), CHUNKS)
        for name in ("grads_gu", "hiddens", "sums"):
            del now[name]

    def middle():
        now["grad_residual"], grad_attended, now["small"] = middle_back(
            flying.pop("returned"), residual, router, routes, cotangent, gain_ffn, router_w, out_pieces, now["offsets"][0]
        )
        now["grad_query"], now["grad_kv"] = attend_back(queries, kv, grad_attended, lse, cosines, sines, flag)

    def ending():
        weights, now["grad_own"], grad_prev = project_back(
            inputs, now.pop("grad_query"), now.pop("grad_kv"), hidden_prev, hidden_in, attended,
            now["grad_residual"], now.pop("small"), qkv_pieces, now["offsets"][1], shards * cores * side,
        )
        weights = weights.reshape((shards, cores, side) + weights.shape[1:])
        total = own_part(weights, 1, core_at, cores)
        for core in range(1, cores):
            total = total + other_core(own_part(weights, 1, (core_at + core) % cores, cores), core)
        flying["owned"] = own_part(total, 0, shard, shards)
        for step in range(1, shards):
            theirs = turn(own_part(total, 0, (shard + step) % shards, shards), "fsdp", (step,), (shards,))
            flying["owned"] = flying["owned"] + theirs
        flying["grad_later"] = lax.ppermute(tie(grad_prev, total), "fsdp", before)

    def sideways_sum():
        value = flying.pop("owned")
        total = own_part(value, 2, side_at, side)
        for a in range(1, side):
            total = total + other_side(own_part(value, 2, (side_at + a) % side, side), a)
        flying["chunk"] = total[0, 0, 0]

    def first():
        now["grad_in"] = first_back(now["grad_own"], flying.pop("grad_later"), now["grad_residual"], hidden_in, gain_attn)

    def mixture_one():
        flying["mixed"] = shard_sums(core_sums(now.pop("mixed")))

    def mixture_two():
        mixed = flying.pop("mixed")
        total = residual + mixed[0].astype(f32)
        for a in range(1, side):
            total = total + other_side(mixed[a], -a % side).astype(f32)
        now["layer_out"] = total.astype(bf16)

    def last_chunk():
        now["chunks"][number] = flying.pop("chunk")

    def put(i, sources):
        if i < number:
            e, c = minis[i]
            now["outs"] = place(sources, now["order"] * count + e, now["outs"], shapes, c, CHUNKS)
        else:
            rows = sources[0].shape[1]
            at = jnp.stack([(core_at - core) % cores * side + (side_at - a) % side for core in range(cores) for a in range(side)])
            now["owned"] = unpack(sources, at.astype(jnp.int32) * rows, rows * cores * side)

    jobs = {
        0: [mini, mini],
        1: [mini] * (number - 3) + [returns],
        2: [middle],
        3: [ending],
        4: [sideways_sum, mixture_one, last_chunk],
        5: [first, mixture_two],
    }
    if number < 4:
        jobs.update({0: [mini] * (number - 1), 1: [returns]})
    mini()
    place_at = lax.axis_index("line")
    end = (place_at == 0) | (place_at == line - 1)
    entry = {i: i for i in range(number)}
    entry[number] = max(number, 5)
    for r in range(entry[number] + 5):
        got = {}
        enters = [i for i in entry if entry[i] == r]
        at = {s: [i for i in entry if entry[i] + s == r] for s in range(5)}
        if line == 4:
            raw = now["chunks"].get(enters[0]) if enters else None
            leaves = at[2]
            done = now["total"].get(leaves[0]) if leaves else None
            if raw is not None and done is not None and raw.shape == done.shape:
                got["pair"] = lax.ppermute(jnp.where(end, raw, done), "line", [(0, 1), (1, 0), (2, 3), (3, 2)])
            else:
                if raw is not None:
                    got["in"] = lax.ppermute(raw, "line", [(0, 1), (3, 2)])
                if done is not None:
                    got["out"] = lax.ppermute(done, "line", [(1, 0), (2, 3)])
            for i in at[1]:
                got["middle"] = lax.ppermute(now["half"][i], "line", [(1, 2), (2, 1)])
        else:
            for i in at[2]:
                now["full"][i] = doubling_sum(now["chunks"][i], "line")
        for i in at[3]:
            got["side"] = [other_side(now["full"][i], a) for a in range(1, side)]
        for i in at[4]:
            got["core"] = [other_core(now["pair"][i], core) for core in range(1, cores)]
        for job in jobs.get(r, ()):
            job()
        now, got = barrier((now, got))
        for i in at[4]:
            put(i, [now["pair"].pop(i)] + got["core"])
        for i in at[3]:
            now["pair"][i] = jnp.stack([now["full"].pop(i)] + got["side"])
        if line == 4:
            for i in at[2]:
                now["full"][i] = jnp.where(end, got["pair"] if "pair" in got else got["out"], now["total"].pop(i))
            for i in at[1]:
                now["total"][i] = now["half"].pop(i) + got["middle"]
            for i in enters:
                now["half"][i] = now["chunks"].pop(i) + (got["pair"] if "pair" in got else got["in"])

    qkv_sum, out_sum, rest = now["owned"]
    return (
        now["layer_out"],
        now["grad_in"],
        qkv_sum,
        out_sum,
        rest[:, :EXPERTS],
        rest[:, EXPERTS + 1],
        rest[:, EXPERTS],
        now["outs"][0],
        now["outs"][1],
    )


def solution(mesh):
    copies, shards = mesh.shape["rep"], mesh.shape["fsdp"]
    local = EXPERTS // shards
    cores = 2 if copies % 2 == 0 and local % 2 == 0 else 1
    side = 2 if cores == 2 and copies % 4 == 0 and local % 4 == 0 else 1
    names = ("line", "side", "core", "fsdp")
    parts = Mesh(mesh.devices.reshape(copies // (side * cores), side, cores, shards), names)
    rows, shard = P(names, None), P("fsdp", None)
    experts = P("fsdp", None, None)
    in_specs = (rows, rows, shard, shard, shard, P("fsdp"), P("fsdp"), experts, experts, rows)
    out_specs = (rows, rows, shard, shard, shard, P("fsdp"), P("fsdp"), experts, experts)
    return jax.shard_map(body, mesh=parts, in_specs=in_specs, out_specs=out_specs, check_vma=False)
```

time: 930 us -> 619 us (0.67)
  matrix products: 194 us -> 0 us
  Pallas kernels: 0 us -> 189 us
  waiting for transfers between devices: 446 us -> 271 us
  other arithmetic: 105 us -> 56.6 us
  blocking collectives: 37.6 us -> 0 us
  local copies, waits for them, and re-layouts: 58.4 us -> 26.8 us
  starting transfers between devices: 75.1 us -> 64.6 us
    dot_general x86 -> x0, matrix products: 194 us -> none  [the longest x30 108 us: dot(): lax.dot_general(left, right, (dims, ((), ())), preferred_element_type=f32)]
    pallas_call x0 -> x17, Pallas kernels: none -> 189 us  [call(): pl.pallas_call(kernel, out_shape=list(out_shape), grid_spec=spec, input_o...]
    ppermute x23 -> x15, waiting for transfers between devices: 263 us -> 94.3 us  [the longest x3 39.2 us: body(): got['out'] = lax.ppermute(done, 'line', [(1, 0), (2, 3)])]
    dynamic_update_slice x26 -> x0, other arithmetic: 40.4 us -> none  [the longest x8 32.6 us: assemble(): out = lax.dynamic_update_slice_in_dim(out, block.astype(f32), at, 0)]
    all_gather x1 -> x0, blocking collectives: 37.6 us -> none  [gathered(): return lax.all_gather(piece, 'fsdp', axis=0, tiled=True)]
    broadcast_in_dim x14 -> x3, local copies, waits for them, and re-layouts: 17.4 us -> 1.37 us  [the longest x2 1.36 us: body(): small = jnp.concatenate([w_router.T, attn_gain[None], ffn_gain[None]], 0)]
    select_n x3 -> x6, other arithmetic: 0.05 us -> 11 us  [the longest x2 6.68 us: body(): jnp.where(end, raw, done)]
    ppermute x49 -> x36, starting transfers between devices: 35.8 us -> 26.4 us  [turn(): return lax.ppermute(value, axes, pairs)]
  transfers between devices with their start and end apart: 72 -> 51, of which waited for: 26 -> 23; matrix products, arithmetic and copies ran while one was open for 31% -> 11% of each run, Pallas kernels for 0% -> 19%
where the time goes in v2:
time: 619 us; the launch traced here: 610 us
  waiting for transfers between devices  271 us (44%)
  Pallas kernels  189 us (31%)
  starting transfers between devices  64.6 us (10%)
  other arithmetic  56.6 us (9%)
  local copies, waits for them, and re-layouts  26.8 us (4%)
    pallas_call x17, Pallas kernels, call(): pl.pallas_call(kernel, out_shape=list(out_shape), grid_spec=spec, input_o...  189 us
    ppermute x36, waiting for transfers between devices, turn(): return lax.ppermute(value, axes, pairs)  177 us
    ppermute x3, waiting for transfers between devices, body(): got['out'] = lax.ppermute(done, 'line', [(1, 0), (2, 3)])  39.2 us
    ppermute x2, waiting for transfers between devices, body(): lax.ppermute(jnp.where(end, raw, done), 'line', [(0, 1), (1, 0), (2, 3),...  30.5 us
    ppermute x36, starting transfers between devices, turn(): return lax.ppermute(value, axes, pairs)  26.4 us
    ppermute x3, waiting for transfers between devices, body(): got['in'] = lax.ppermute(raw, 'line', [(0, 1), (3, 2)])  20.9 us
    ppermute x3, starting transfers between devices, body(): got['in'] = lax.ppermute(raw, 'line', [(0, 1), (3, 2)])  12.8 us
  transfers between devices with their start and end apart: 51, of which 23 were waited for; matrix products, arithmetic and copies ran while one was open for 11% of the time, Pallas kernels for 19%

profile of v2, /device:TPU:0, one launch (start us, length us, event | category | flops | bytes accessed | tf_op | source)
XLA Modules:
  0.0 609.9 jit_solution(17557768339030052471)
XLA Ops:
  4.8 11.9 %collective-permute-done.2.rest_1_ = bf16[128,2048]{1,0:T(8,128)(2,1)S(1)} collective-permute-done((bf16[128,2048]{1,0:T(8,128)(2,1)S(1)}, bf16[128,2048]{1,0:T(8,128)(2,1)S(1)}, u32[]{:S(2)}, u32[]{:S(2)}) %collective-permute-start.2) | collective-permute-done | bytes 524320 | tf_op jit(solution)/shard_map/ppermute | solution.py:48
  22.0 7.9 %collective-permute-done.4.rest_3_ = bf16[128,2048]{1,0:T(8,128)(2,1)S(1)} collective-permute-done((bf16[128,2048]{1,0:T(8,128)(2,1)S(1)}, bf16[128,2048]{1,0:T(8,128)(2,1)S(1)}, u32[]{:S(2)}, u32[]{:S(2)}) %collective-permute-start.4) | collective-permute-done | bytes 524320 | tf_op jit(solution)/shard_map/ppermute | solution.py:48
  62.8 10.2 %shard_map.170 = (bf16[256,1024]{1,0:T(8,128)(2,1)}, f32[512,128]{1,0:T(8,128)}, f32[256,1024]{1,0:T(8,128)}, f32[256,128]{1,0:T(8,128)}, bf16[272,1024]{1,0:T(8,128)(2,1)}) custom-call(s32[5]{0:T(128)} %stack.149.offsets_ref, s32[1]{0:T(128)} %bitcast.7.flag_ref, bf16[256,1024]{1,0:T(8,128)(2,1)} %get-tuple-element.166.q_ref, ...), custom_call_target="tpu_custom_call" | custom-call | flops 2147483648 | bytes 6991896 | tf_op jit(solution)/shard_map/pallas_call | solution.py:74
  77.6 12.1 %collective-permute-done.12 = bf16[272,1024]{1,0:T(8,128)(2,1)S(1)} collective-permute-done((bf16[272,1024]{1,0:T(8,128)(2,1)}, bf16[272,1024]{1,0:T(8,128)(2,1)S(1)}, u32[]{:S(2)}, u32[]{:S(2)}) %collective-permute-start.12) | collective-permute-done | bytes 557088 | tf_op jit(solution)/shard_map/ppermute | solution.py:48
  89.7 14.3 %collective-permute-done.11 = bf16[272,1024]{1,0:T(8,128)(2,1)S(1)} collective-permute-done((bf16[272,1024]{1,0:T(8,128)(2,1)}, bf16[272,1024]{1,0:T(8,128)(2,1)S(1)}, u32[]{:S(2)}, u32[]{:S(2)}) %collective-permute-start.11) | collective-permute-done | bytes 557088 | tf_op jit(solution)/shard_map/ppermute | solution.py:48
  112.1 17.0 %shard_map.171 = (bf16[8,256,512]{2,1,0:T(8,128)(2,1)}, bf16[8,256,256]{2,1,0:T(8,128)(2,1)}, f32[8,8,256]{2,1,0:T(8,128)}, bf16[1024,768]{1,0:T(8,128)(2,1)}) custom-call(s32[2]{0:T(128)} %pad_add_fusion.index_ref, bf16[4,272,1024]{2,1,0:T(8,128)(2,1)} %copy-done, bf16[4,272,1024]{2,1,0:T(8,128)(2,1)} %collective-permute-done.13.refs_1_, ...), custom_call_target="tpu_custom_call" | custom-call | flops 6442450944 | bytes 55377928 | tf_op jit(solution)/shard_map/pallas_call | solution.py:74
  133.6 17.0 %shard_map.172 = (bf16[8,256,512]{2,1,0:T(8,128)(2,1)}, bf16[8,256,256]{2,1,0:T(8,128)(2,1)}, f32[8,8,256]{2,1,0:T(8,128)}, bf16[1024,768]{1,0:T(8,128)(2,1)}) custom-call(s32[2]{0:T(128)} %pad_add_fusion.index_ref, bf16[4,272,1024]{2,1,0:T(8,128)(2,1)} %copy-done, bf16[4,272,1024]{2,1,0:T(8,128)(2,1)} %collective-permute-done.13.refs_1_, ...), custom_call_target="tpu_custom_call" | custom-call | flops 6442450944 | bytes 55377928 | tf_op jit(solution)/shard_map/pallas_call | solution.py:74
  150.7 17.0 %shard_map.173 = (bf16[8,256,512]{2,1,0:T(8,128)(2,1)}, bf16[8,256,256]{2,1,0:T(8,128)(2,1)}, f32[8,8,256]{2,1,0:T(8,128)}, bf16[1024,768]{1,0:T(8,128)(2,1)}) custom-call(s32[2]{0:T(128)} %pad_add_fusion.1.index_ref, bf16[4,272,1024]{2,1,0:T(8,128)(2,1)} %copy-done, bf16[4,272,1024]{2,1,0:T(8,128)(2,1)} %collective-permute-done.13.refs_1_, ...), custom_call_target="tpu_custom_call" | custom-call | flops 6442450944 | bytes 55377928 | tf_op jit(solution)/shard_map/pallas_call | solution.py:74
  168.4 17.1 %shard_map.174 = (bf16[8,256,512]{2,1,0:T(8,128)(2,1)}, bf16[8,256,256]{2,1,0:T(8,128)(2,1)}, f32[8,8,256]{2,1,0:T(8,128)}, bf16[1024,768]{1,0:T(8,128)(2,1)}) custom-call(s32[2]{0:T(128)} %pad_add_fusion.1.index_ref, bf16[4,272,1024]{2,1,0:T(8,128)(2,1)} %copy-done, bf16[4,272,1024]{2,1,0:T(8,128)(2,1)} %collective-permute-done.13.refs_1_, ...), custom_call_target="tpu_custom_call" | custom-call | flops 6442450944 | bytes 55377928 | tf_op jit(solution)/shard_map/pallas_call | solution.py:74
  185.5 26.3 %shard_map.175 = bf16[8,272,1024]{2,1,0:T(8,128)(2,1)} custom-call(s32[4]{0:T(128)} %pad_add_fusion.3.indices_ref, bf16[8,256,512]{2,1,0:T(8,128)(2,1)} %get-tuple-element.190.refs_0_, bf16[8,256,512]{2,1,0:T(8,128)(2,1)} %get-tuple-element.191.refs_1_, bf16[8,256,512]{2,1,0:T(8,128)(2,1)} %get-tuple-element.192.refs_2_, ...), custom_call_target="tpu_custom_call" | custom-call | flops 8589934592 | bytes 46661648 | tf_op jit(solution)/shard_map/pallas_call | solution.py:74
  222.6 9.4 %shard_map.176 = bf16[8,256,1024]{2,1,0:T(8,128)(2,1)} custom-call(s32[4]{0:T(128)} %pad_add_fusion.4.indices_ref, bf16[8,256,256]{2,1,0:T(8,128)(2,1)} %get-tuple-element.200.refs_0_, bf16[8,256,256]{2,1,0:T(8,128)(2,1)} %get-tuple-element.201.refs_1_, bf16[8,256,256]{2,1,0:T(8,128)(2,1)} %get-tuple-element.202.refs_2_, ...), custom_call_target="tpu_custom_call" | custom-call | flops 4294967296 | bytes 25165840 | tf_op jit(solution)/shard_map/pallas_call | solution.py:74
  232.0 20.9 %collective-permute-done.18 = bf16[1024,768]{1,0:T(8,128)(2,1)} collective-permute-done((bf16[1024,768]{1,0:T(8,128)(2,1)S(1)}, bf16[1024,768]{1,0:T(8,128)(2,1)}, u32[]{:S(2)}, u32[]{:S(2)}) %collective-permute-start.18) | collective-permute-done | bytes 1572896 | tf_op jit(solution)/shard_map/ppermute | solution.py:830
  272.9 12.4 %collective-permute-done.21.rest_1_ = bf16[272,1024]{1,0:T(8,128)(2,1)} collective-permute-done((bf16[272,1024]{1,0:T(8,128)(2,1)}, bf16[272,1024]{1,0:T(8,128)(2,1)}, u32[]{:S(2)}, u32[]{:S(2)}) %collective-permute-start.21) | collective-permute-done | bytes 557088 | tf_op jit(solution)/shard_map/ppermute | solution.py:48
  285.3 11.3 %collective-permute-done.22.rest_2_ = bf16[272,1024]{1,0:T(8,128)(2,1)} collective-permute-done((bf16[272,1024]{1,0:T(8,128)(2,1)}, bf16[272,1024]{1,0:T(8,128)(2,1)}, u32[]{:S(2)}, u32[]{:S(2)}) %collective-permute-start.22) | collective-permute-done | bytes 557088 | tf_op jit(solution)/shard_map/ppermute | solution.py:48
  302.3 12.9 %shard_map.178 = (bf16[256,1024]{1,0:T(8,128)(2,1)}, bf16[512,1024]{1,0:T(8,128)(2,1)}) custom-call(s32[1]{0:T(128)} %bitcast.7.flag_ref, bf16[256,1024]{1,0:T(8,128)(2,1)} %get-tuple-element.166.q_ref, bf16[512,1024]{1,0:T(8,128)(2,1)} %get-tuple-element.167.kv_ref, bf16[256,1024]{1,0:T(8,128)(2,1)} %get-tuple-element.212.grad_ref, ...), custom_call_target="tpu_custom_call" | custom-call | flops 5368709120 | bytes 4456452 | tf_op jit(solution)/shard_map/pallas_call | solution.py:74
  315.2 10.9 %shard_map.179 = (bf16[8,128,3200]{2,1,0:T(8,128)(2,1)}, f32[256,1024]{1,0:T(8,128)}, bf16[256,1024]{1,0:T(8,128)(2,1)}) custom-call(s32[5]{0:T(128)} %stack.149.offsets_ref, bf16[512,1024]{1,0:T(8,128)(2,1)} %get-tuple-element.226.in_ref, bf16[256,1024]{1,0:T(8,128)(2,1)} %get-tuple-element.227.dq_ref, bf16[512,1024]{1,0:T(8,128)(2,1)} %get-tuple-element.228.dkv_ref, ...), custom_call_target="tpu_custom_call" | custom-call | flops 2684354560 | bytes 18087956 | tf_op jit(solution)/shard_map/pallas_call | solution.py:74
  345.5 30.5 %collective-permute-done.30 = bf16[1024,768]{1,0:T(8,128)(2,1)} collective-permute-done((bf16[1024,768]{1,0:T(8,128)(2,1)}, bf16[1024,768]{1,0:T(8,128)(2,1)}, u32[]{:S(2)}, u32[]{:S(2)}) %collective-permute-start.30) | collective-permute-done | bytes 1572896 | tf_op jit(solution)/shard_map/ppermute | solution.py:827
  406.3 26.8 %collective-permute-done.34 = bf16[1024,768]{1,0:T(8,128)(2,1)} collective-permute-done((bf16[1024,768]{1,0:T(8,128)(2,1)S(1)}, bf16[1024,768]{1,0:T(8,128)(2,1)}, u32[]{:S(2)}, u32[]{:S(2)}) %collective-permute-start.34) | collective-permute-done | bytes 1572896 | tf_op jit(solution)/shard_map/ppermute | solution.py:832
  450.2 17.6 %collective-permute-done.38 = bf16[2,256,1024]{2,1,0:T(8,128)(2,1)S(1)} collective-permute-done((bf16[2,256,1024]{2,1,0:T(8,128)(2,1)S(1)}, bf16[2,256,1024]{2,1,0:T(8,128)(2,1)S(1)}, u32[]{:S(2)}, u32[]{:S(2)}) %collective-permute-start.38) | collective-permute-done | bytes 1048608 | tf_op jit(solution)/shard_map/ppermute | solution.py:48
  473.5 22.4 %collective-permute-done.39 = bf16[256,1024]{1,0:T(8,128)(2,1)S(1)} collective-permute-done((bf16[256,1024]{1,0:T(8,128)(2,1)S(1)}, bf16[256,1024]{1,0:T(8,128)(2,1)S(1)}, u32[]{:S(2)}, u32[]{:S(2)}) %collective-permute-start.39) | collective-permute-done | bytes 524320 | tf_op jit(solution)/shard_map/ppermute | solution.py:48
  529.1 23.3 %collective-permute-done.46 = bf16[1024,768]{1,0:T(8,128)(2,1)S(1)} collective-permute-done((bf16[1024,768]{1,0:T(8,128)(2,1)S(1)}, bf16[1024,768]{1,0:T(8,128)(2,1)S(1)}, u32[]{:S(2)}, u32[]{:S(2)}) %collective-permute-start.46) | collective-permute-done | bytes 1572896 | tf_op jit(solution)/shard_map/ppermute | solution.py:48
  564.4 12.4 %collective-permute-done.48 = bf16[128,3200]{1,0:T(8,128)(2,1)S(1)} collective-permute-done((bf16[128,3200]{1,0:T(8,128)(2,1)S(1)}, bf16[128,3200]{1,0:T(8,128)(2,1)S(1)}, u32[]{:S(2)}, u32[]{:S(2)}) %collective-permute-start.48) | collective-permute-done | bytes 819232 | tf_op jit(solution)/shard_map/ppermute | solution.py:832
  578.4 7.7 %shard_map.184 = (f32[8,1024,1024]{2,1,0:T(8,128)}, f32[8,1024,512]{2,1,0:T(8,128)}) custom-call(s32[4]{0:T(128)} %multiply_add_fusion.experts_ref, bf16[2,1024,768]{2,1,0:T(8,128)(2,1)} %copy-done.5, bf16[2,1024,768]{2,1,0:T(8,128)(2,1)} %copy-done.15, f32[8,1024,1024]{2,1,0:T(8,128)} %get-tuple-element.304.refs_2_, ...), custom_call_target="tpu_custom_call", output_to_operand_aliasing={{0}: (3, {}), {1}: (4, {})} | custom-call | bytes 106954768 | tf_op jit(solution)/shard_map/pallas_call | solution.py:74
  586.1 9.9 %collective-permute-done.49 = bf16[128,3200]{1,0:T(8,128)(2,1)S(1)} collective-permute-done((bf16[128,3200]{1,0:T(8,128)(2,1)S(1)}, bf16[128,3200]{1,0:T(8,128)(2,1)S(1)}, u32[]{:S(2)}, u32[]{:S(2)}) %collective-permute-start.49) | collective-permute-done | bytes 819232 | tf_op jit(solution)/shard_map/ppermute | solution.py:48
  (247 shorter events, 228.8 us)
Async XLA Ops:
  54.6 49.8 %collective-permute-start.15 = (bf16[2,256,1024]{2,1,0:T(8,128)(2,1)S(1)}, bf16[2,256,1024]{2,1,0:T(8,128)(2,1)S(1)}, u32[]{:S(2)}, u32[]{:S(2)}) collective-permute-start(bf16[2,256,1024]{2,1,0:T(8,128)(2,1)S(1)} %pad_maximum_fusion.6), channel_id=1, source_target_pairs={{0,1},{1,0},{2,3},{3,2},{4,5},{5,4},{6,7},{7,6},{8,9},{9,8},{10,11... | collective-permute-start | bytes 3145736 | tf_op jit(solution)/shard_map/ppermute | solution.py:48
  75.5 28.6 %collective-permute-start.11 = (bf16[272,1024]{1,0:T(8,128)(2,1)}, bf16[272,1024]{1,0:T(8,128)(2,1)S(1)}, u32[]{:S(2)}, u32[]{:S(2)}) collective-permute-start(bf16[272,1024]{1,0:T(8,128)(2,1)} %get-tuple-element.169), channel_id=1, source_target_pairs={{0,1},{1,0},{4,5},{5,4},{2,3},{3,2},{6,7},{7,6},{8,9},{9,8},{12,13... | collective-permute-start | bytes 1671176 | tf_op jit(solution)/shard_map/ppermute | solution.py:48
  76.0 28.1 %collective-permute-start.10 = (bf16[272,1024]{1,0:T(8,128)(2,1)}, bf16[272,1024]{1,0:T(8,128)(2,1)S(1)}, u32[]{:S(2)}, u32[]{:S(2)}) collective-permute-start(bf16[272,1024]{1,0:T(8,128)(2,1)} %get-tuple-element.169), channel_id=1, source_target_pairs={{0,4},{1,5},{4,0},{5,1},{2,6},{3,7},{6,2},{7,3},{8,12},{9,13},{12,... | collective-permute-start | bytes 1671176 | tf_op jit(solution)/shard_map/ppermute | solution.py:48
  129.1 38.6 %collective-permute-start.17 = (bf16[1024,768]{1,0:T(8,128)(2,1)}, bf16[1024,768]{1,0:T(8,128)(2,1)S(1)}, u32[]{:S(2)}, u32[]{:S(2)}) collective-permute-start(bf16[1024,768]{1,0:T(8,128)(2,1)} %get-tuple-element.187), channel_id=1, source_target_pairs={{0,8},{24,16},{1,9},{25,17},{2,10},{26,18},{3,11},{27,19},{4,12},{... | collective-permute-start | bytes 4718600 | tf_op jit(solution)/shard_map/ppermute | solution.py:830
  215.2 51.0 %collective-permute-start.20 = (bf16[4,272,1024]{2,1,0:T(8,128)(2,1)}, bf16[4,272,1024]{2,1,0:T(8,128)(2,1)}, u32[]{:S(2)}, u32[]{:S(2)}) collective-permute-start(bf16[4,272,1024]{2,1,0:T(8,128)(2,1)} %slice.78), channel_id=1, source_target_pairs={{0,2},{2,0},{1,3},{3,1},{4,6},{6,4},{5,7},{7,5},{8,10},{10,8},{9,1... | collective-permute-start | bytes 6684680 | tf_op jit(solution)/shard_map/ppermute | solution.py:48
  215.2 37.7 %collective-permute-start.18 = (bf16[1024,768]{1,0:T(8,128)(2,1)S(1)}, bf16[1024,768]{1,0:T(8,128)(2,1)}, u32[]{:S(2)}, u32[]{:S(2)}) collective-permute-start(bf16[1024,768]{1,0:T(8,128)(2,1)S(1)} %copy-done.18), channel_id=1, source_target_pairs={{0,8},{24,16},{1,9},{25,17},{2,10},{26,18},{3,11},{27,19},{4,12},{... | collective-permute-start | bytes 4718600 | tf_op jit(solution)/shard_map/ppermute | solution.py:830
  220.2 32.7 %collective-permute-start.19 = (bf16[1024,768]{1,0:T(8,128)(2,1)S(1)}, bf16[1024,768]{1,0:T(8,128)(2,1)}, u32[]{:S(2)}, u32[]{:S(2)}) collective-permute-start(bf16[1024,768]{1,0:T(8,128)(2,1)S(1)} %add.287), channel_id=1, source_target_pairs={{8,16},{16,8},{9,17},{17,9},{10,18},{18,10},{11,19},{19,11},{12,20... | collective-permute-start | bytes 4718600 | tf_op jit(solution)/shard_map/ppermute | solution.py:834
  254.8 60.3 %collective-permute-start.24 = (bf16[1024,768]{1,0:T(8,128)(2,1)S(1)}, bf16[1024,768]{1,0:T(8,128)(2,1)}, u32[]{:S(2)}, u32[]{:S(2)}) collective-permute-start(bf16[1024,768]{1,0:T(8,128)(2,1)S(1)} %add.289), channel_id=1, source_target_pairs={{8,16},{16,8},{9,17},{17,9},{10,18},{18,10},{11,19},{19,11},{12,20... | collective-permute-start | bytes 4718600 | tf_op jit(solution)/shard_map/ppermute | solution.py:834
  260.2 55.0 %collective-permute-start.25 = (bf16[1024,768]{1,0:T(8,128)(2,1)}, bf16[1024,768]{1,0:T(8,128)(2,1)S(1)}, u32[]{:S(2)}, u32[]{:S(2)}) collective-permute-start(bf16[1024,768]{1,0:T(8,128)(2,1)} %get-tuple-element.345), channel_id=1, source_target_pairs={{0,8},{8,0},{16,24},{24,16},{1,9},{9,1},{17,25},{25,17},{2,10},{10... | collective-permute-start | bytes 4718600 | tf_op jit(solution)/shard_map/ppermute | solution.py:827
  270.9 25.7 %collective-permute-start.22 = (bf16[272,1024]{1,0:T(8,128)(2,1)}, bf16[272,1024]{1,0:T(8,128)(2,1)}, u32[]{:S(2)}, u32[]{:S(2)}) collective-permute-start(bf16[272,1024]{1,0:T(8,128)(2,1)} %get-tuple-element.348), channel_id=1, source_target_pairs={{0,1},{1,0},{4,5},{5,4},{2,3},{3,2},{6,7},{7,6},{8,9},{9,8},{12,13... | collective-permute-start | bytes 1671176 | tf_op jit(solution)/shard_map/ppermute | solution.py:48
  338.8 37.1 %collective-permute-start.30 = (bf16[1024,768]{1,0:T(8,128)(2,1)}, bf16[1024,768]{1,0:T(8,128)(2,1)}, u32[]{:S(2)}, u32[]{:S(2)}) collective-permute-start(bf16[1024,768]{1,0:T(8,128)(2,1)} %get-tuple-element.343), channel_id=1, source_target_pairs={{0,8},{8,0},{16,24},{24,16},{1,9},{9,1},{17,25},{25,17},{2,10},{10... | collective-permute-start | bytes 4718600 | tf_op jit(solution)/shard_map/ppermute | solution.py:827
  340.2 36.5 %collective-permute-start.31 = (bf16[1024,768]{1,0:T(8,128)(2,1)}, bf16[1024,768]{1,0:T(8,128)(2,1)}, u32[]{:S(2)}, u32[]{:S(2)}) collective-permute-start(bf16[1024,768]{1,0:T(8,128)(2,1)} %get-tuple-element.248), channel_id=1, source_target_pairs={{0,4},{4,0},{1,5},{5,1},{2,6},{6,2},{3,7},{7,3},{8,12},{12,8},{9,1... | collective-permute-start | bytes 4718600 | tf_op jit(solution)/shard_map/ppermute | solution.py:48
  344.3 37.7 %collective-permute-start.27 = (bf16[1,1,2,128,3200]{4,3,2,1,0:T(8,128)(2,1)}, bf16[1,1,2,128,3200]{4,3,2,1,0:T(8,128)(2,1)}, u32[]{:S(2)}, u32[]{:S(2)}) collective-permute-start(bf16[1,1,2,128,3200]{4,3,2,1,0:T(8,128)(2,1)} %constant_dynamic-slice_fusion.1), channel_id=1, source_target_pairs={{0,1},{1,0},{2,3},{3,2},{4,5},{5,4},{6,7},{7,6},{8,9},{9,8},{10,11... | collective-permute-start | bytes 4915208 | tf_op jit(solution)/shard_map/ppermute | solution.py:48
  380.5 57.3 %collective-permute-start.32 = (bf16[2,1024,768]{2,1,0:T(8,128)(2,1)}, bf16[2,1024,768]{2,1,0:T(8,128)(2,1)}, u32[]{:S(2)}, u32[]{:S(2)}) collective-permute-start(bf16[2,1024,768]{2,1,0:T(8,128)(2,1)} %pad_maximum_fusion.refs_0_), channel_id=1, source_target_pairs={{0,2},{2,0},{1,3},{3,1},{4,6},{6,4},{5,7},{7,5},{8,10},{10,8},{9,1... | collective-permute-start | bytes 9437192 | tf_op jit(solution)/shard_map/ppermute | solution.py:48
  386.7 53.5 %collective-permute-start.37 = (bf16[4,256,1024]{2,1,0:T(8,128)(2,1)}, bf16[4,256,1024]{2,1,0:T(8,128)(2,1)}, u32[]{:S(2)}, u32[]{:S(2)}) collective-permute-start(bf16[4,256,1024]{2,1,0:T(8,128)(2,1)} %slice.66), channel_id=1, source_target_pairs={{0,2},{2,0},{1,3},{3,1},{4,6},{6,4},{5,7},{7,5},{8,10},{10,8},{9,1... | collective-permute-start | bytes 6291464 | tf_op jit(solution)/shard_map/ppermute | solution.py:48
  394.4 38.8 %collective-permute-start.34 = (bf16[1024,768]{1,0:T(8,128)(2,1)S(1)}, bf16[1024,768]{1,0:T(8,128)(2,1)}, u32[]{:S(2)}, u32[]{:S(2)}) collective-permute-start(bf16[1024,768]{1,0:T(8,128)(2,1)S(1)} %add.309), channel_id=1, source_target_pairs={{8,0},{16,24},{9,1},{17,25},{10,2},{18,26},{11,3},{19,27},{12,4},{... | collective-permute-start | bytes 4718600 | tf_op jit(solution)/shard_map/ppermute | solution.py:832
  403.1 34.8 %collective-permute-start.35 = (bf16[1024,768]{1,0:T(8,128)(2,1)}, bf16[1024,768]{1,0:T(8,128)(2,1)}, u32[]{:S(2)}, u32[]{:S(2)}) collective-permute-start(bf16[1024,768]{1,0:T(8,128)(2,1)} %get-tuple-element.265), channel_id=1, source_target_pairs={{0,4},{4,0},{1,5},{5,1},{2,6},{6,2},{3,7},{7,3},{8,12},{12,8},{9,1... | collective-permute-start | bytes 4718600 | tf_op jit(solution)/shard_map/ppermute | solution.py:48
  440.2 73.4 %collective-permute-start.40 = (bf16[2,1024,768]{2,1,0:T(8,128)(2,1)S(1)}, bf16[2,1024,768]{2,1,0:T(8,128)(2,1)}, u32[]{:S(2)}, u32[]{:S(2)}) collective-permute-start(bf16[2,1024,768]{2,1,0:T(8,128)(2,1)S(1)} %pad_maximum_fusion.1.refs_0_), channel_id=1, source_target_pairs={{0,2},{2,0},{1,3},{3,1},{4,6},{6,4},{5,7},{7,5},{8,10},{10,8},{9,1... | collective-permute-start | bytes 9437192 | tf_op jit(solution)/shard_map/ppermute | solution.py:48
  446.0 67.6 %collective-permute-start.42 = (bf16[1024,768]{1,0:T(8,128)(2,1)S(1)}, bf16[1024,768]{1,0:T(8,128)(2,1)}, u32[]{:S(2)}, u32[]{:S(2)}) collective-permute-start(bf16[1024,768]{1,0:T(8,128)(2,1)S(1)} %add.314), channel_id=1, source_target_pairs={{8,0},{16,24},{9,1},{17,25},{10,2},{18,26},{11,3},{19,27},{12,4},{... | collective-permute-start | bytes 4718600 | tf_op jit(solution)/shard_map/ppermute | solution.py:832
  449.1 64.5 %collective-permute-start.43 = (bf16[1024,768]{1,0:T(8,128)(2,1)S(1)}, bf16[1024,768]{1,0:T(8,128)(2,1)S(1)}, u32[]{:S(2)}, u32[]{:S(2)}) collective-permute-start(bf16[1024,768]{1,0:T(8,128)(2,1)S(1)} %broadcast_select_fusion.1), channel_id=1, source_target_pairs={{0,4},{4,0},{1,5},{5,1},{2,6},{6,2},{3,7},{7,3},{8,12},{12,8},{9,1... | collective-permute-start | bytes 4718600 | tf_op jit(solution)/shard_map/ppermute | solution.py:48
  468.3 27.7 %collective-permute-start.39 = (bf16[256,1024]{1,0:T(8,128)(2,1)S(1)}, bf16[256,1024]{1,0:T(8,128)(2,1)S(1)}, u32[]{:S(2)}, u32[]{:S(2)}) collective-permute-start(bf16[256,1024]{1,0:T(8,128)(2,1)S(1)} %slice_bitcast_fusion.4), channel_id=1, source_target_pairs={{0,4},{4,0},{1,5},{5,1},{2,6},{6,2},{3,7},{7,3},{8,12},{12,8},{9,1... | collective-permute-start | bytes 1572872 | tf_op jit(solution)/shard_map/ppermute | solution.py:48
  469.1 44.5 %collective-permute-start.41 = (bf16[128,3200]{1,0:T(8,128)(2,1)}, bf16[128,3200]{1,0:T(8,128)(2,1)}, u32[]{:S(2)}, u32[]{:S(2)}) collective-permute-start(bf16[128,3200]{1,0:T(8,128)(2,1)} %add_bitcast_fusion), channel_id=1, source_target_pairs={{0,8},{24,16},{1,9},{25,17},{2,10},{26,18},{3,11},{27,19},{4,12},{... | collective-permute-start | bytes 2457608 | tf_op jit(solution)/shard_map/ppermute | solution.py:830
  513.9 38.5 %collective-permute-start.44 = (bf16[2,1024,768]{2,1,0:T(8,128)(2,1)S(1)}, bf16[2,1024,768]{2,1,0:T(8,128)(2,1)}, u32[]{:S(2)}, u32[]{:S(2)}) collective-permute-start(bf16[2,1024,768]{2,1,0:T(8,128)(2,1)S(1)} %pad_maximum_fusion.2.refs_0_), channel_id=1, source_target_pairs={{0,2},{2,0},{1,3},{3,1},{4,6},{6,4},{5,7},{7,5},{8,10},{10,8},{9,1... | collective-permute-start | bytes 9437192 | tf_op jit(solution)/shard_map/ppermute | solution.py:48
  516.7 35.8 %collective-permute-start.46 = (bf16[1024,768]{1,0:T(8,128)(2,1)S(1)}, bf16[1024,768]{1,0:T(8,128)(2,1)S(1)}, u32[]{:S(2)}, u32[]{:S(2)}) collective-permute-start(bf16[1024,768]{1,0:T(8,128)(2,1)S(1)} %broadcast_select_fusion), channel_id=1, source_target_pairs={{0,4},{4,0},{1,5},{5,1},{2,6},{6,2},{3,7},{7,3},{8,12},{12,8},{9,1... | collective-permute-start | bytes 4718600 | tf_op jit(solution)/shard_map/ppermute | solution.py:48
  (69 other events, 1000.6 us)

commit v3 on v2

v3 whole, which is shorter than its diff:
```python
import math
from functools import partial

import jax
import jax.numpy as jnp
from jax import lax
from jax.experimental import pallas as pl
from jax.experimental.pallas import tpu as pltpu
from jax.sharding import Mesh, PartitionSpec as P

D = 1024
HEADS = 16
KV_HEADS = 8
HEAD_DIM = 64
F = 512
TOP = 8
EXPERTS = 16
BLOCK = 256
QW = HEADS * HEAD_DIM
KVW = KV_HEADS * HEAD_DIM
EXTRA = 16
CHUNKS = 2
PAIR = 2 * HEAD_DIM

norm_eps = 1e-06
masked_score = -1e30
score_scale = HEAD_DIM ** (-0.5)
bf16, f32 = jnp.bfloat16, jnp.float32
VMEM = 56 * 1024 * 1024


def dot(left, right, dims=((1,), (0,))):
    return lax.dot_general(left, right, (dims, ((), ())), preferred_element_type=f32)


def turn(value, axes, steps, sizes):
    pairs = []
    for source in range(math.prod(sizes)):
        place, rest = [], source
        for size in reversed(sizes):
            place.append(rest % size)
            rest //= size
        place.reverse()
        target = 0
        for at, size, step in zip(place, sizes, steps):
            target = target * size + (at + step) % size
        pairs.append((source, target))
    return lax.ppermute(value, axes, pairs)


def own_part(value, axis, index, parts):
    size = value.shape[axis] // parts
    return lax.dynamic_slice_in_dim(value, index * size, size, axis)


def whole(shape):
    return pl.BlockSpec(shape, lambda *_: (0,) * len(shape))


SCALARS = pl.BlockSpec(memory_space=pltpu.SMEM)
STAY = pl.BlockSpec(memory_space=pl.ANY)


def call(kernel, out_shape, in_specs, operands, out_specs=None, scratch=(), grid=None, prefetch=0, aliases=None):
    out_specs = [whole(s.shape) for s in out_shape] if out_specs is None else out_specs
    spec = pltpu.PrefetchScalarGridSpec(
        num_scalar_prefetch=prefetch,
        grid=grid or (1,),
        in_specs=in_specs,
        out_specs=out_specs,
        scratch_shapes=list(scratch),
    )
    return pl.pallas_call(
        kernel,
        out_shape=list(out_shape),
        grid_spec=spec,
        input_output_aliases=aliases or {},
        compiler_params=pltpu.CompilerParams(vmem_limit_bytes=VMEM),
        cost_estimate=pl.CostEstimate(flops=0, transcendentals=0, bytes_accessed=0),
    )(*operands)


def array(shape, dtype):
    return jax.ShapeDtypeStruct(shape, dtype)


def normalize(rows):
    scale_inv = lax.rsqrt(jnp.mean(rows * rows, -1, keepdims=True) + norm_eps)
    return (rows * scale_inv, scale_inv)


def norm_back(normed, scale_inv, grad_normed):
    return scale_inv * (grad_normed - normed * jnp.mean(grad_normed * normed, -1, keepdims=True))


def lanes(shape):
    return lax.broadcasted_iota(jnp.int32, shape, len(shape) - 1)


def halves(values):
    low = lanes(values.shape) % HEAD_DIM < HEAD_DIM // 2
    half = HEAD_DIM // 2
    return jnp.where(low, pltpu.roll(values, PAIR - half, 1), pltpu.roll(values, half, 1))


def rotary_tables(places):
    at = jnp.arange(PAIR, dtype=jnp.int32) % HEAD_DIM
    middle = HEAD_DIM // 2
    frequency = 10000.0 ** (-(2.0 * (at % middle).astype(f32)) / HEAD_DIM)
    angles = places.astype(f32)[:, None] * frequency[None, :]
    sign = jnp.where(at < middle, -1.0, 1.0)[None, :]
    return (jnp.cos(angles), jnp.sin(angles) * sign)


def load_rows(pieces, offsets, target, sems):
    copies = []
    for i, piece in enumerate(pieces):
        copy = pltpu.make_async_copy(piece, target.at[pl.ds(pl.multiple_of(offsets[i], 16), piece.shape[0]), :], sems.at[i])
        copy.start()
        copies.append(copy)
    return copies


def project(hidden_prev, hidden_own, gain, cosines, sines, pieces, offsets):
    length, count = hidden_own.shape[0], len(pieces)

    def kernel(offsets_ref, prev_ref, own_ref, gain_ref, cos_ref, sin_ref, *rest):
        piece_refs, (q_ref, kv_ref, in_ref, weight, sems) = rest[:count], rest[count:]
        copies = load_rows(piece_refs, offsets_ref, weight, sems)
        for i, ref in enumerate((prev_ref, own_ref)):
            normed, _ = normalize(ref[...].astype(f32))
            in_ref[i * length : (i + 1) * length, :] = (normed * gain_ref[...]).astype(bf16)
        for copy in copies:
            copy.wait()
        values = dot(in_ref[length:, :], weight[:, :QW])
        cos_own, sin_own = cos_ref[length:, :], sin_ref[length:, :]
        for g in range(QW // PAIR):
            u = values[:, g * PAIR : (g + 1) * PAIR]
            q_ref[:, g * PAIR : (g + 1) * PAIR] = (u * cos_own + halves(u) * sin_own).astype(bf16)
        values = dot(in_ref[...], weight[:, QW:])
        for g in range(KVW // PAIR):
            u = values[:, g * PAIR : (g + 1) * PAIR]
            kv_ref[:, g * PAIR : (g + 1) * PAIR] = (u * cos_ref[...] + halves(u) * sin_ref[...]).astype(bf16)
        kv_ref[:, KVW:] = values[:, KVW:].astype(bf16)

    width = QW + 2 * KVW
    return call(
        kernel,
        [array((length, QW), bf16), array((2 * length, 2 * KVW), bf16), array((2 * length, D), bf16)],
        [SCALARS] + [whole(v.shape) for v in (hidden_prev, hidden_own, gain, cosines, sines)] + [STAY] * count,
        (offsets, hidden_prev, hidden_own, gain, cosines, sines, *pieces),
        scratch=[pltpu.VMEM((D, width), bf16), pltpu.SemaphoreType.DMA((count,))],
    )


def doubled(values, which):
    low = lanes(values.shape) < HEAD_DIM
    swapped = pltpu.roll(values, HEAD_DIM, 1)
    return jnp.where(low, values, swapped) if which == 0 else jnp.where(low, swapped, values)


def two_rows(pair):
    low = lanes(pair.shape) < HEAD_DIM
    zero = jnp.zeros_like(pair)
    return jnp.concatenate([jnp.where(low, pair, zero), jnp.where(low, zero, pair)], 0)


def named_experts(routes):
    shape = (routes.shape[0], 128)
    named = routes[:, 0:1] == lanes(shape)
    for k in range(1, TOP):
        named = named | (routes[:, k : k + 1] == lanes(shape))
    return named


def attend(query, kv, flag):
    length = query.shape[0]

    def kernel(flag_ref, q_ref, kv_ref, att_ref, lse_ref):
        bias = jnp.where((lanes((1, 2 * length)) >= length) | (flag_ref[0] > 0), 0.0, masked_score)
        lse_ref[...] = jnp.zeros(lse_ref.shape, f32)

        def pair_of_keys(jj, carry):
            at = pl.multiple_of(jj * PAIR, PAIR)
            keys = kv_ref[:, pl.ds(at, PAIR)].astype(f32)
            vals = kv_ref[:, pl.ds(KVW + at, PAIR)].astype(f32)
            for t in range(2):
                place = pl.multiple_of((2 * jj + t) * PAIR, PAIR)
                both = two_rows(q_ref[:, pl.ds(place, PAIR)].astype(f32)).astype(bf16)
                scores = dot(both, doubled(keys, t).astype(bf16), ((1,), (1,))) * score_scale + bias
                largest = jnp.max(scores, -1, keepdims=True)
                exponent = jnp.exp(scores - largest)
                totals = jnp.sum(exponent, -1, keepdims=True)
                probs = (exponent * (1.0 / totals)).astype(bf16)
                lse = largest + jnp.log(totals)
                lse_ref[...] = jnp.where(lanes(lse_ref.shape) == 2 * jj + t, lse, lse_ref[...])
                val = doubled(vals, t)
                low = lanes(val.shape) < HEAD_DIM
                zero = jnp.zeros_like(val)
                out = dot(probs[:length], jnp.where(low, val, zero).astype(bf16))
                out = out + dot(probs[length:], jnp.where(low, zero, val).astype(bf16))
                att_ref[:, pl.ds(place, PAIR)] = out.astype(bf16)
            return carry

        lax.fori_loop(0, KVW // PAIR, pair_of_keys, 0)

    return call(
        kernel,
        [array((length, QW), bf16), array((2 * length, 128), f32)],
        [SCALARS, whole(query.shape), whole(kv.shape)],
        (flag, query, kv),
    )


def enter_experts(attended, hidden_own, gain, router_w, routes, pieces, offsets):
    length, count = attended.shape[0], len(pieces)

    def kernel(offsets_ref, att_ref, own_ref, gain_ref, router_ref, routes_ref, *rest):
        piece_refs, (res_ref, gate_ref, pay_ref, weight, sems) = rest[:count], rest[count:]
        copies = load_rows(piece_refs, offsets_ref, weight, sems)
        for copy in copies:
            copy.wait()
        residual = own_ref[...].astype(f32) + dot(att_ref[...], weight[...])
        res_ref[...] = residual
        normed, _ = normalize(residual)
        rows = (normed * gain_ref[...]).astype(bf16)
        pay_ref[:length, :] = rows
        logits = dot(rows, router_ref[...], ((1,), (1,)))
        real = lanes(logits.shape) < EXPERTS
        logits = jnp.where(real, logits, masked_score)
        raised = jnp.where(real, jnp.exp(logits - jnp.max(logits, -1, keepdims=True)), 0.0)
        router = raised * (1.0 / jnp.sum(raised, -1, keepdims=True))
        gate_ref[...] = router
        gates = jnp.where(named_experts(routes_ref[...]), router, 0.0).T[:EXTRA]
        high = gates.astype(bf16)
        pay_ref[length:, :length] = high
        pay_ref[length:, length : 2 * length] = (gates - high.astype(f32)).astype(bf16)
        pay_ref[length:, 2 * length :] = jnp.zeros((EXTRA, D - 2 * length), bf16)

    operands = (attended, hidden_own, gain, router_w, routes)
    return call(
        kernel,
        [array((length, D), f32), array((length, 128), f32), array((length + EXTRA, D), bf16)],
        [SCALARS] + [whole(v.shape) for v in operands] + [STAY] * count,
        (offsets, *operands, *pieces),
        scratch=[pltpu.VMEM((QW, D), bf16), pltpu.SemaphoreType.DMA((count,))],
    )


def write_chunks(out_refs, at, values):
    part = F // len(out_refs)
    for c, out_ref in enumerate(out_refs):
        out_ref[:, at * part : (at + 1) * part] = values[:, c * part : (c + 1) * part].astype(bf16)


def expert(rows, grads, w_gate_up, w_down, index, chunks):
    sources, blocks, tall = len(grads), len(rows), rows[0].shape[0]
    length = tall - EXTRA
    step = 2
    turns = grads[0].shape[0] // step
    steps = blocks // step

    def kernel(index_ref, *refs):
        row_refs, grad_refs, refs = refs[:blocks], refs[blocks : blocks + sources], refs[blocks + sources :]
        gate_up_ref, down_ref, dgu_ref, hid_ref, sum_ref = refs[:5]
        out_refs, (both_ref, grad_ref, table_ref, *accs) = refs[5 : 5 + chunks], refs[5 + chunks :]
        i = pl.program_id(0)
        for source, source_ref in enumerate(grad_refs):

            @pl.when((i >= source * turns) & (i < (source + 1) * turns))
            def _():
                for b in range(step):
                    grad_ref[b * length : (b + 1) * length, :] = source_ref[b]

        for j, row_ref in enumerate(row_refs):
            b = j % step

            @pl.when(i == j // step)
            def _():
                both_ref[b * length : (b + 1) * length, :] = row_ref[:length, :]
                high, low = row_ref[length:, :length], row_ref[length:, length : 2 * length]
                table_ref[b] = high.astype(f32) + low.astype(f32)

        both, grad = both_ref[...], grad_ref[...]
        columns = []
        for b in range(step):
            table = table_ref[b]
            mine = lax.broadcasted_iota(jnp.int32, table.shape, 0) == index_ref[1]
            row = jnp.sum(jnp.where(mine, table, 0.0), 0, keepdims=True)
            columns.append(jnp.broadcast_to(row, (128, length)).T[:, :1])
        gate = jnp.concatenate(columns, 0)
        gate_up = dot(both, gate_up_ref[0])
        gate_part, up_part = gate_up[:, :F], gate_up[:, F:]
        sigmoid_g = jax.nn.sigmoid(gate_part)
        silu_g = gate_part * sigmoid_g
        hidden = silu_g * up_part
        raw = dot(grad, down_ref[0])
        sums = jnp.sum(raw * hidden, 1, keepdims=True)
        gated = (gate * hidden).astype(bf16)
        grad_hidden = gate * raw
        grad_gate = (grad_hidden * up_part * sigmoid_g * (1.0 + gate_part * (1.0 - sigmoid_g))).astype(bf16)
        grad_up = (grad_hidden * silu_g).astype(bf16)
        for b in range(step):
            at = slice(b * length, (b + 1) * length)
            dgu_ref[b, :, :F] = grad_gate[at]
            dgu_ref[b, :, F:] = grad_up[at]
            hid_ref[b] = gated[at]
            sum_ref[b] = jnp.broadcast_to(sums[at], (length, 128)).T[:8]
        if not chunks:
            return
        for p, (left, right) in enumerate(((both, grad_gate), (both, grad_up), (grad, gated))):
            term, acc = dot(left, right, ((0,), (0,))), accs[p]

            @pl.when(i == 0)
            def _():
                acc[...] = term

            @pl.when((i > 0) & (i < steps - 1))
            def _():
                acc[...] += term

            @pl.when(i == steps - 1)
            def _():
                write_chunks(out_refs, p, acc[...] + term)

    def block(*shape):
        return pl.BlockSpec((step,) + shape, lambda i, index: (i,) + (0,) * len(shape))

    def source_block(source, *shape):
        def at(i, index):
            return (jnp.clip(i - source * turns, 0, turns - 1),) + (0,) * len(shape)

        return pl.BlockSpec((step,) + shape, at)

    def weight(*shape):
        return pl.BlockSpec((1,) + shape, lambda i, index: (index[0], 0, 0))

    shapes = [array((blocks, length, 2 * F), bf16), array((blocks, length, F), bf16), array((blocks, 8, length), f32)]
    scratch = [
        pltpu.VMEM((step * length, D), bf16),
        pltpu.VMEM((step * length, D), bf16),
        pltpu.VMEM((step, EXTRA, length), f32),
    ]
    return call(
        kernel,
        shapes + [array((D, 3 * F // chunks), bf16)] * chunks if chunks else shapes,
        [whole((tall, D))] * blocks
        + [source_block(s, length, D) for s in range(sources)]
        + [weight(D, 2 * F), weight(D, F)],
        (index, *rows, *grads, w_gate_up, w_down),
        out_specs=[block(length, 2 * F), block(length, F), block(8, length)]
        + [pl.BlockSpec((D, 3 * F // chunks), lambda i, index: (0, 0)) for _ in range(chunks)],
        scratch=scratch + ([pltpu.VMEM((D, F), f32)] * 3 if chunks else []),
        grid=(steps,),
        prefetch=1,
    )


def gate_column(table, expert):
    mine = lax.broadcasted_iota(jnp.int32, table.shape, 0) == expert
    row = jnp.sum(jnp.where(mine, table, 0.0), 0, keepdims=True)
    return jnp.broadcast_to(row, (128, table.shape[1])).T[:, :1]


def last_expert(rows, grads, w_gate_up, w_down, indices, earlier, sums):
    sources, blocks, tall = len(grads), len(rows), rows[0].shape[0]
    length = tall - EXTRA
    step = 2
    turns = grads[0].shape[0] // step
    steps = blocks // step
    others = len(earlier)

    def kernel(indices_ref, *refs):
        row_refs, grad_refs, refs = refs[:blocks], refs[blocks : blocks + sources], refs[blocks + sources :]
        gate_up_ref, down_ref, refs = refs[0], refs[1], refs[2:]
        earlier_refs, weight_refs, sum_refs, refs = refs[:others], refs[others : 2 * others], refs[2 * others : 3 * others], refs[3 * others :]
        dgu_ref, hid_ref, out_refs, (both_ref, grad_ref, table_ref) = refs[0], refs[1], refs[2 : 2 + sources], refs[2 + sources :]
        i = pl.program_id(0)
        for source, source_ref in enumerate(grad_refs):

            @pl.when((i >= source * turns) & (i < (source + 1) * turns))
            def _():
                for b in range(step):
                    grad_ref[b * length : (b + 1) * length, :] = source_ref[b]

        for j, row_ref in enumerate(row_refs):
            b = j % step

            @pl.when(i == j // step)
            def _():
                both_ref[b * length : (b + 1) * length, :] = row_ref[:length, :]
                high, low = row_ref[length:, :length], row_ref[length:, length : 2 * length]
                table_ref[b] = high.astype(f32) + low.astype(f32)

        both, grad = both_ref[...], grad_ref[...]
        gate = jnp.concatenate([gate_column(table_ref[b], indices_ref[2 * others + 1]) for b in range(step)], 0)
        gate_up = dot(both, gate_up_ref[0])
        gate_part, up_part = gate_up[:, :F], gate_up[:, F:]
        sigmoid_g = jax.nn.sigmoid(gate_part)
        silu_g = gate_part * sigmoid_g
        hidden = silu_g * up_part
        raw = dot(grad, down_ref[0])
        own = jnp.sum(raw * hidden, 1, keepdims=True)
        gated = (gate * hidden).astype(bf16)
        grad_hidden = gate * raw
        grad_gate = (grad_hidden * up_part * sigmoid_g * (1.0 + gate_part * (1.0 - sigmoid_g))).astype(bf16)
        grad_up = (grad_hidden * silu_g).astype(bf16)
        total = dot(jnp.concatenate([grad_gate, grad_up], 1), gate_up_ref[0], ((1,), (1,)))
        for part_ref, weight_ref in zip(earlier_refs, weight_refs):
            part = jnp.concatenate([part_ref[b] for b in range(step)], 0)
            total = total + dot(part, weight_ref[0], ((1,), (1,)))
        for b in range(step):
            at = slice(b * length, (b + 1) * length)
            dgu_ref[b, :, :F] = grad_gate[at]
            dgu_ref[b, :, F:] = grad_up[at]
            hid_ref[b] = gated[at]
            table = jnp.zeros((EXTRA, length), f32)
            place = lax.broadcasted_iota(jnp.int32, table.shape, 0)
            for e in range(others):
                table = jnp.where(place == indices_ref[2 * e + 1], sum_refs[e][b, :1, :], table)
            row = jnp.broadcast_to(own[at], (length, 128)).T[:1]
            table = jnp.where(place == indices_ref[2 * others + 1], row, table)
            high = table.astype(bf16)
            for source, out_ref in enumerate(out_refs):

                @pl.when((i >= source * turns) & (i < (source + 1) * turns))
                def _():
                    out_ref[b, :length, :] = total[at].astype(bf16)
                    out_ref[b, length:, :length] = high
                    out_ref[b, length:, length : 2 * length] = (table - high.astype(f32)).astype(bf16)
                    out_ref[b, length:, 2 * length :] = jnp.zeros((EXTRA, D - 2 * length), bf16)

    def block(*shape):
        return pl.BlockSpec((step,) + shape, lambda i, index: (i,) + (0,) * len(shape))

    def source_block(source, *shape):
        def at(i, index):
            return (jnp.clip(i - source * turns, 0, turns - 1),) + (0,) * len(shape)

        return pl.BlockSpec((step,) + shape, at)

    def weight(e, *shape):
        return pl.BlockSpec((1,) + shape, lambda i, index: (index[2 * e], 0, 0))

    return call(
        kernel,
        [array((blocks, length, 2 * F), bf16), array((blocks, length, F), bf16)]
        + [array((blocks // sources, tall, D), bf16)] * sources,
        [whole((tall, D))] * blocks
        + [source_block(s, length, D) for s in range(sources)]
        + [weight(others, D, 2 * F), weight(others, D, F)]
        + [block(length, 2 * F)] * others
        + [weight(e, D, 2 * F) for e in range(others)]
        + [block(8, length)] * others,
        (indices, *rows, *grads, w_gate_up, w_down, *earlier, *[w_gate_up] * others, *sums),
        out_specs=[block(length, 2 * F), block(length, F)] + [source_block(s, tall, D) for s in range(sources)],
        scratch=[
            pltpu.VMEM((step * length, D), bf16),
            pltpu.VMEM((step * length, D), bf16),
            pltpu.VMEM((step, EXTRA, length), f32),
        ],
        grid=(steps,),
        prefetch=1,
    )


def weight_grads(rows, grads, grad_gate_up, hidden, chunks, after):
    sources, blocks, tall = len(grads), len(rows), rows[0].shape[0]
    length = tall - EXTRA
    step = 2
    turns = grads[0].shape[0] // step
    steps = blocks // step

    def kernel(after_ref, *refs):
        row_refs, grad_refs, refs = refs[:blocks], refs[blocks : blocks + sources], refs[blocks + sources :]
        dgu_ref, hid_ref, out_refs = refs[0], refs[1], refs[2 : 2 + chunks]
        both_ref, grad_ref, *accs = refs[2 + chunks :]
        i = pl.program_id(0)
        for source, source_ref in enumerate(grad_refs):

            @pl.when((i >= source * turns) & (i < (source + 1) * turns))
            def _():
                for b in range(step):
                    grad_ref[b * length : (b + 1) * length, :] = source_ref[b]

        for j, row_ref in enumerate(row_refs):
            b = j % step

            @pl.when(i == j // step)
            def _():
                both_ref[b * length : (b + 1) * length, :] = row_ref[:length, :]

        both, grad = both_ref[...], grad_ref[...]
        grad_gate = jnp.concatenate([dgu_ref[b, :, :F] for b in range(step)], 0)
        grad_up = jnp.concatenate([dgu_ref[b, :, F:] for b in range(step)], 0)
        gated = jnp.concatenate([hid_ref[b] for b in range(step)], 0)
        for p, (left, right) in enumerate(((both, grad_gate), (both, grad_up), (grad, gated))):
            term, acc = dot(left, right, ((0,), (0,))), accs[p]

            @pl.when(i == 0)
            def _():
                acc[...] = term

            @pl.when((i > 0) & (i < steps - 1))
            def _():
                acc[...] += term

            @pl.when(i == steps - 1)
            def _():
                write_chunks(out_refs, p, acc[...] + term)

    def block(*shape):
        return pl.BlockSpec((step,) + shape, lambda i, after: (i,) + (0,) * len(shape))

    def source_block(source, *shape):
        def at(i, after):
            return (jnp.clip(i - source * turns, 0, turns - 1),) + (0,) * len(shape)

        return pl.BlockSpec((step,) + shape, at)

    return call(
        kernel,
        [array((D, 3 * F // chunks), bf16)] * chunks,
        [whole((tall, D))] * blocks
        + [source_block(s, length, D) for s in range(sources)]
        + [block(length, 2 * F), block(length, F)],
        (after, *rows, *grads, grad_gate_up, hidden),
        out_specs=[pl.BlockSpec((D, 3 * F // chunks), lambda i, after: (0, 0)) for _ in range(chunks)],
        scratch=[pltpu.VMEM((step * length, D), bf16)] * 2 + [pltpu.VMEM((D, F), f32)] * 3,
        grid=(steps,),
        prefetch=1,
    )


def row_terms(parts, weights, indices, sources):
    blocks, length, width = parts[0].shape
    count = len(parts)
    step = 2
    turns = blocks // step // sources

    def kernel(indices_ref, *refs):
        part_refs, weight_refs, out_refs = refs[:count], refs[count : 2 * count], refs[2 * count :]
        i = pl.program_id(0)
        total = None
        for part_ref, weight_ref in zip(part_refs, weight_refs):
            term = dot(jnp.concatenate([part_ref[b] for b in range(step)], 0), weight_ref[0], ((1,), (1,)))
            total = term if total is None else total + term
        for source, out_ref in enumerate(out_refs):

            @pl.when((i >= source * turns) & (i < (source + 1) * turns))
            def _():
                for b in range(step):
                    out_ref[b] = total[b * length : (b + 1) * length].astype(bf16)

    def weight(e):
        return pl.BlockSpec((1,) + weights.shape[1:], lambda i, index: (index[2 * e], 0, 0))

    def source_block(source):
        return pl.BlockSpec((step, length, D), lambda i, index: (jnp.clip(i - source * turns, 0, turns - 1), 0, 0))

    return call(
        kernel,
        [array((blocks // sources, length, D), bf16)] * sources,
        [pl.BlockSpec((step, length, width), lambda i, index: (i, 0, 0))] * count + [weight(e) for e in range(count)],
        (indices, *parts, *[weights] * count),
        out_specs=[source_block(s) for s in range(sources)],
        grid=(blocks // step,),
        prefetch=1,
    )


def backward(
    returned, residual, router, routes, cotangent, gain, router_w, query, kv, lse, cosines, sines, inputs,
    hidden_prev, hidden_own, attended, out_pieces, out_offsets, qkv_pieces, qkv_offsets, flag, core, shards, cores,
):
    length, terms = residual.shape[0], len(returned)
    width = QW + 2 * KVW
    out_count, qkv_count = len(out_pieces), len(qkv_pieces)

    deep = D // (shards * cores)

    def kernel(out_offsets_ref, qkv_offsets_ref, flag_ref, core_ref, *rest):
        term_refs, rest = rest[:terms], rest[terms:]
        res_ref, gate_ref, routes_ref, cot_ref, gain_ref, router_ref, q_ref, kv_ref, lse_ref, cos_ref, sin_ref = rest[:11]
        in_ref, prev_ref, own_ref, att_ref, rest = *rest[11:15], rest[15:]
        out_refs, qkv_refs, rest = rest[:out_count], rest[out_count : out_count + qkv_count], rest[out_count + qkv_count :]
        gres_ref, gown_ref, gprev_ref, own_grad_ref = rest[:4]
        far_refs, rest = rest[4 : 4 + 3 * (cores - 1)], rest[4 + 3 * (cores - 1) :]
        w_out, w_qkv, gatt_ref, dq_ref, dkv_ref, small_ref, out_sems, qkv_sems = rest
        out_copies = load_rows(out_refs, out_offsets_ref, w_out, out_sems)
        qkv_copies = load_rows(qkv_refs, qkv_offsets_ref, w_qkv, qkv_sems)
        total = term_refs[0][...].astype(f32)
        for ref in term_refs[1:]:
            total = total + ref[...].astype(f32)
        table = total[length:, :length] + total[length:, length : 2 * length]
        gate_grads = jnp.concatenate([table, jnp.zeros((128 - EXTRA, length), f32)], 0).T
        grad_router = jnp.where(named_experts(routes_ref[...]), gate_grads, 0.0)
        router = gate_ref[...]
        grad_logits = (router * (grad_router - jnp.sum(router * grad_router, -1, keepdims=True))).astype(bf16)
        grad_input = total[:length] + dot(grad_logits, router_ref[...])
        normed, inverse = normalize(res_ref[...])
        gain_row = gain_ref[...]
        rows = (normed * gain_row).astype(bf16)
        small = dot(rows, grad_logits, ((0,), (0,)))
        gain_grad = jnp.sum(grad_input * normed, 0, keepdims=True)
        small_ref[...] = jnp.where(lanes((D, 128)) == EXPERTS, jnp.broadcast_to(gain_grad, (128, D)).T, small)
        grad_residual = cot_ref[...].astype(f32) + norm_back(normed, inverse, grad_input * gain_row)
        gres_ref[...] = grad_residual
        grad_attn = grad_residual.astype(bf16)
        for copy in out_copies:
            copy.wait()
        gatt_ref[...] = dot(grad_attn, w_out[...], ((1,), (1,))).astype(bf16)

        def write(at, values):
            group = min(at // D, 2)
            start = at - group * D
            for p in range(shards * cores):
                rows_of = values[p * deep : (p + 1) * deep]
                for j in range(cores):

                    @pl.when((core_ref[0] + j) % cores == p % cores)
                    def _():
                        if j == 0:
                            own_grad_ref[p // cores, :, at : at + values.shape[1]] = rows_of.astype(bf16)
                        else:
                            ref = far_refs[3 * (j - 1) + group]
                            ref[p // cores, :, start : start + values.shape[1]] = rows_of.astype(bf16)

        write(width, dot(att_ref[...], grad_attn, ((0,), (0,))))

        bias = jnp.where((lanes((1, 2 * length)) >= length) | (flag_ref[0] > 0), 0.0, masked_score)
        cos_own, sin_own = cos_ref[length:, :], sin_ref[length:, :]

        def back(values, cos, sin):
            return (values * cos - halves(values) * sin).astype(bf16)

        def pair_of_keys(jj, carry):
            at = pl.multiple_of(jj * PAIR, PAIR)
            keys = kv_ref[:, pl.ds(at, PAIR)].astype(f32)
            vals = kv_ref[:, pl.ds(KVW + at, PAIR)].astype(f32)
            key_grads, val_grads = [], []
            for t in range(2):
                place = pl.multiple_of((2 * jj + t) * PAIR, PAIR)
                both = two_rows(q_ref[:, pl.ds(place, PAIR)].astype(f32)).astype(bf16)
                outs = two_rows(gatt_ref[:, pl.ds(place, PAIR)].astype(f32)).astype(bf16)
                key = doubled(keys, t).astype(bf16)
                val = doubled(vals, t).astype(bf16)
                own = lanes(lse_ref.shape) == 2 * jj + t
                log_total = jnp.sum(jnp.where(own, lse_ref[...], 0.0), -1, keepdims=True)
                scores = dot(both, key, ((1,), (1,))) * score_scale + bias
                probs = jnp.exp(scores - log_total)
                grad_probs = dot(outs, val, ((1,), (1,)))
                inner = jnp.sum(probs * grad_probs, -1, keepdims=True)
                grad_scores = (probs * (grad_probs - inner)).astype(bf16)
                grad_query = dot(grad_scores, key) * score_scale
                low = lanes((length, PAIR)) < HEAD_DIM
                grad_query = jnp.where(low, grad_query[:length], grad_query[length:])
                dq_ref[:, pl.ds(place, PAIR)] = back(grad_query, cos_own, sin_own)
                key_grad = dot(grad_scores, both, ((0,), (0,))) * score_scale
                val_grad = dot(probs.astype(bf16), outs, ((0,), (0,)))
                key_grads.append(key_grad + pltpu.roll(key_grad, HEAD_DIM, 1))
                val_grads.append(val_grad + pltpu.roll(val_grad, HEAD_DIM, 1))
            low = lanes((2 * length, PAIR)) < HEAD_DIM
            dkv_ref[:, pl.ds(at, PAIR)] = back(jnp.where(low, *key_grads), cos_ref[...], sin_ref[...])
            dkv_ref[:, pl.ds(KVW + at, PAIR)] = jnp.where(low, *val_grads).astype(bf16)
            return carry

        lax.fori_loop(0, KVW // PAIR, pair_of_keys, 0)
        write(0, dot(in_ref[length:, :], dq_ref[...], ((0,), (0,))))
        write(QW, dot(in_ref[...], dkv_ref[...], ((0,), (0,))))
        for copy in qkv_copies:
            copy.wait()
        from_kv = dot(dkv_ref[...], w_qkv[:, QW:], ((1,), (1,)))
        own = from_kv[length:] + dot(dq_ref[...], w_qkv[:, :QW], ((1,), (1,)))
        gown_ref[...] = own
        gprev_ref[...] = from_kv[:length].astype(bf16)
        normed_own, _ = normalize(own_ref[...].astype(f32))
        normed_prev, _ = normalize(prev_ref[...].astype(f32))
        gain_grad = jnp.sum(own * normed_own + from_kv[:length] * normed_prev, 0, keepdims=True)
        column = jnp.broadcast_to(gain_grad, (128, D)).T
        write(width + D, jnp.where(lanes((D, 128)) == EXPERTS + 1, column, small_ref[...]))

    operands = (
        *returned, residual, router, routes, cotangent, gain, router_w, query, kv, lse, cosines, sines, inputs,
        hidden_prev, hidden_own, attended,
    )
    return call(
        kernel,
        [
            array((length, D), f32),
            array((length, D), f32),
            array((length, D), bf16),
        ]
        + [array((shards, deep, width + D + 128), bf16)]
        + [array((shards, deep, w), bf16) for w in (D, D, D + 128)] * (cores - 1),
        [SCALARS] * 4 + [whole(v.shape) for v in operands] + [STAY] * (out_count + qkv_count),
        (out_offsets, qkv_offsets, flag, core, *operands, *out_pieces, *qkv_pieces),
        scratch=[
            pltpu.VMEM((QW, D), bf16),
            pltpu.VMEM((D, width), bf16),
            pltpu.VMEM((length, QW), bf16),
            pltpu.VMEM((length, QW), bf16),
            pltpu.VMEM((2 * length, 2 * KVW), bf16),
            pltpu.VMEM((D, 128), f32),
            pltpu.SemaphoreType.DMA((out_count,)),
            pltpu.SemaphoreType.DMA((qkv_count,)),
        ],
    )


def first_back(grad_sum, grad_residual, hidden_own, gain):
    def kernel(sum_ref, res_ref, hid_ref, gain_ref, out_ref):
        normed, inverse = normalize(hid_ref[...].astype(f32))
        grad = sum_ref[...] * gain_ref[...]
        out_ref[...] = res_ref[...] + norm_back(normed, inverse, grad)

    operands = (grad_sum, grad_residual, hidden_own, gain)
    return call(kernel, [array(grad_sum.shape, f32)], [whole(v.shape) for v in operands], operands)[0]


def place(sources, experts, outs, shapes, chunk, chunks):
    part = F // chunks
    count = sum(source.shape[0] for source in sources)

    def kernel(experts_ref, *refs):
        source_refs = refs[: len(sources)]
        gate_up_ref, down_ref, wide, sems = refs[len(sources) + len(outs) :]
        copies = []
        values = [ref.at[i] for ref in source_refs for i in range(ref.shape[0])]
        for i, source in enumerate(values):
            wide[i] = source[...].astype(f32)
            for p, target in enumerate(
                (
                    gate_up_ref.at[experts_ref[i], :, chunk * part : (chunk + 1) * part],
                    gate_up_ref.at[experts_ref[i], :, F + chunk * part : F + (chunk + 1) * part],
                    down_ref.at[experts_ref[i], :, chunk * part : (chunk + 1) * part],
                )
            ):
                copy = pltpu.make_async_copy(wide.at[i, :, p * part : (p + 1) * part], target, sems.at[i, p])
                copy.start()
                copies.append(copy)
        for copy in copies:
            copy.wait()

    return call(
        kernel,
        shapes,
        [SCALARS] + [whole(v.shape) for v in sources] + [STAY] * len(outs),
        (experts, *sources, *outs),
        out_specs=[STAY, STAY],
        scratch=[pltpu.VMEM((count, D, 3 * part), f32), pltpu.SemaphoreType.DMA((count, 3))],
        aliases={1 + len(sources) + i: i for i in range(len(outs))},
    )


def unpack(sources, offsets, rows):
    count = sum(source.shape[0] for source in sources)
    deep, wide = sources[0].shape[1:]
    widths = (QW + 2 * KVW, D)

    def kernel(offsets_ref, *refs):
        source_refs, refs = refs[: len(sources)], refs[len(sources) :]
        out_refs, router_ref, ffn_ref, attn_ref, values_ref, rest_ref, sems = refs[:2], *refs[2:]
        copies = []
        for i, source in enumerate([ref.at[i] for ref in source_refs for i in range(ref.shape[0])]):
            values_ref[i] = source[...].astype(f32)
            at = pl.multiple_of(offsets_ref[i], 8)
            start = 0
            for p, (out_ref, width) in enumerate(zip(out_refs, widths)):
                copy = pltpu.make_async_copy(values_ref.at[i, :, start : start + width], out_ref.at[pl.ds(at, deep), :], sems.at[i, p])
                copy.start()
                copies.append(copy)
                start += width
            rest_ref[pl.ds(at, deep), :] = values_ref[i, :, start:]
        router_ref[...] = rest_ref[:, :EXPERTS]
        turned = rest_ref[...].T
        ffn_ref[...] = turned[EXPERTS : EXPERTS + 1]
        attn_ref[...] = turned[EXPERTS + 1 : EXPERTS + 2]
        for copy in copies:
            copy.wait()

    return call(
        kernel,
        [array((rows, width), f32) for width in widths] + [array((rows, EXPERTS), f32)] + [array((1, rows), f32)] * 2,
        [SCALARS] + [whole(v.shape) for v in sources],
        (offsets, *sources),
        out_specs=[STAY] * 2 + [whole((rows, EXPERTS))] + [whole((1, rows))] * 2,
        scratch=[
            pltpu.VMEM((count, deep, wide), f32),
            pltpu.VMEM((rows, wide - sum(widths)), f32),
            pltpu.SemaphoreType.DMA((count, 2)),
        ],
    )


def post(function, flags, arrays, outs):
    parts = 4

    def cut(shape):
        return shape[:-2] + (shape[-2] // parts, shape[-1])

    def kernel(flags_ref, *refs):
        values = function([flags_ref[i] for i in range(flags.shape[0])], *[ref[...] for ref in refs[: len(arrays)]])
        for ref, value in zip(refs[len(arrays) :], values):
            if isinstance(value, tuple):
                for i, v in enumerate(value):
                    ref[i] = v.astype(ref.dtype)
            else:
                ref[...] = value.astype(ref.dtype)

    def spec(shape):
        return pl.BlockSpec(cut(shape), lambda i: (0,) * (len(shape) - 2) + (i, 0))

    return call(
        kernel,
        outs,
        [SCALARS] + [spec(v.shape) for v in arrays],
        (flags, *arrays),
        out_specs=[spec(v.shape) for v in outs],
        grid=(parts,),
    )


def tie(values, after):
    return lax.optimization_barrier((values, after))[0]


def doubling_sum(value, axis):
    count, step = lax.axis_size(axis), 1
    if count & (count - 1):
        return lax.psum(value, axis)
    while step < count:
        value = value + lax.ppermute(value, axis, [(i, i ^ step) for i in range(count)])
        step *= 2
    return value


def body(
    hidden_in, routes, w_qkv, w_out, w_router, attn_gain, ffn_gain, w_gate_up, w_down, cotangent
):
    line, shards = lax.axis_size("line"), lax.axis_size("fsdp")
    side, cores = lax.axis_size("side"), lax.axis_size("core")
    shard, side_at, core_at = lax.axis_index("fsdp"), lax.axis_index("side"), lax.axis_index("core")
    length = hidden_in.shape[0]
    near = [(a, s) for s in range(shards) for a in range(side)]
    local_experts = w_gate_up.shape[0]
    count = local_experts // (side * cores)
    barrier = lax.optimization_barrier

    def other_core(value, core=1):
        return turn(value, "core", (core,), (cores,))

    def other_side(value, step=1):
        return turn(value, "side", (step,), (side,))

    def from_shard(part, step):
        return turn(part, "fsdp", (step,), (shards,))

    def fetch_start(piece, sides):
        part = own_part(piece, 0, core_at * sides + side_at % sides, cores * sides)
        return [from_shard(part, step) for step in range(1, shards)]

    def fetch_end(piece, first, sides):
        rows = piece.shape[0]
        out, offsets = [piece], [shard * rows]
        for step, part in enumerate(first, 1):
            base = (shard - step) % shards * rows
            for a in range(sides):
                theirs = other_side(part, a) if a else part
                for core in range(cores):
                    out.append(other_core(theirs, core) if core else theirs)
                    at = (core_at - core) % cores * sides + (side_at - a) % sides
                    offsets.append(base + at * part.shape[0])
        return out, jnp.stack(offsets).astype(jnp.int32)

    def over_cores(first):
        return [other_core(first, core) if core else first for core in range(cores)]

    def far_blocks(blocks):
        return [other_core(blocks[core * len(near) : (core + 1) * len(near)], -core % cores) for core in range(1, cores)]

    def add_up(first, others):
        for other in others:
            first = first + other
        return first

    def send_back(total):
        out = [total[0]]
        for i, (a, s) in enumerate(near):
            if (a, s) != (0, 0):
                out.append(turn(total[i], ("side", "fsdp"), (-a % side, -s % shards), (side, shards)))
        return out

    parity = shard % 2
    flag = parity.astype(jnp.int32)[None]
    later = [(i, i + 1) for i in range(0, shards, 2)]
    before = [(i + 1, i) for i in range(0, shards, 2)]

    small_rows = w_router.shape[0]
    small = jnp.concatenate([w_router.T, attn_gain[None], ffn_gain[None]], 0)
    qkv_first = fetch_start(w_qkv, side)
    hidden_prev = lax.ppermute(hidden_in, "fsdp", later)
    full_small = jnp.zeros((EXPERTS + 2, D), bf16)
    for step in range(shards):
        theirs = from_shard(small, step) if step else small
        full_small = lax.dynamic_update_slice_in_dim(full_small, theirs, (shard - step) % shards * small_rows, 1)
    gain_attn = full_small[EXPERTS : EXPERTS + 1].astype(f32)
    gain_ffn = full_small[EXPERTS + 1 :].astype(f32)
    router_w = jnp.pad(full_small[:EXPERTS], ((0, 128 - EXPERTS), (0, 0)))
    sideways = [other_side(cotangent, a) for a in range(1, side)]
    across = [from_shard(cotangent, s) for s in range(1, shards)]
    rows_at = jnp.arange(length, dtype=jnp.int32)
    cosines, sines = rotary_tables(jnp.concatenate([rows_at, parity * length + rows_at]))
    qkv_pieces, qkv_offsets = fetch_end(w_qkv, qkv_first, side)
    out_first = fetch_start(tie(w_out, (hidden_prev, qkv_first)), 1)

    across, hidden_prev = barrier((across, hidden_prev))
    corners = [[other_side(v, a) for a in range(1, side)] for v in across]
    queries, kv, inputs = project(hidden_prev, hidden_in, gain_attn, cosines, sines, qkv_pieces, qkv_offsets)
    out_first, queries, kv = barrier((out_first, queries, kv))
    out_pieces, out_offsets = fetch_end(w_out, out_first, 1)
    attended, lse = attend(queries, kv, flag)
    grads_near = [cotangent] + sideways + [v for first, rest in zip(across, corners) for v in [first] + rest]
    grads_near = jnp.stack(tie(grads_near, attended))
    out_pieces, attended, grads_near = barrier((out_pieces, attended, grads_near))
    grads_near = over_cores(grads_near)
    residual, router, payload = enter_experts(attended, hidden_in, gain_ffn, router_w, routes, out_pieces, out_offsets)
    rows_near = [turn(payload, ("side", "fsdp"), (a, s), (side, shards)) if (a, s) != (0, 0) else payload for a, s in near]
    rows_near = rows_near + [other_core(v, core) for core in range(1, cores) for v in rows_near]

    clock = []

    def run(function, *inputs):
        if clock:
            inputs = barrier((inputs, tuple(clock)))[0]
        out = function(*inputs)
        clock[:] = jax.tree.leaves(out)
        return out

    mine_at = (side_at * cores + core_at) * count
    indices = [jnp.stack([mine_at + e, shard * local_experts + mine_at + e]).astype(jnp.int32) for e in range(count)]
    both = jnp.concatenate(indices)
    order = jnp.stack([((side_at - a) % side * cores + (core_at - core) % cores) for core in range(cores) for a in range(side)])
    order = order.astype(jnp.int32) * count
    shapes = [array((local_experts, D, 2 * F), f32), array((local_experts, D, F), f32)]
    place_at = lax.axis_index("line")
    end = (place_at == 0) | (place_at == line - 1)

    def go_in(raw):
        return lax.ppermute(raw, "line", [(0, 1), (3, 2)])

    def cross(half):
        return lax.ppermute(half, "line", [(1, 2), (2, 1)])

    def in_and_out(sent):
        return lax.ppermute(sent, "line", [(0, 1), (1, 0), (2, 3), (3, 2)])

    def go_out(total):
        return lax.ppermute(total, "line", [(1, 0), (2, 3)])

    def chosen(got, kept):
        return jnp.where(end, got, kept)

    def sides(full):
        return [other_side(full, a) for a in range(1, side)]

    def core_swaps(pair):
        return [other_core(pair, core) for core in range(1, cores)]

    def stacked(full, others):
        return jnp.stack([full] + others)

    def plus(first, second):
        return first + second

    def split(blocks):
        return [blocks[core * len(near) : (core + 1) * len(near)] for core in range(cores)]

    def near_sums(first, others):
        total = add_up(first, others)
        return [total[i] for i in range(len(near))]

    def placed(pair, swaps, outs, e, c):
        return place([pair] + swaps, order + e, outs, shapes, c, CHUNKS)

    def back(terms):
        return backward(
            terms, residual, router, routes, cotangent, gain_ffn, router_w, queries, kv, lse, cosines, sines, inputs, hidden_prev,
            hidden_in, attended, out_pieces, out_offsets, qkv_pieces, qkv_offsets, flag, core_at.astype(jnp.int32)[None], shards, cores,
        )

    def by_shard(total):
        return total[0] if shards == 1 else own_part(total, 0, shard, shards)[0], [
            own_part(total, 0, (shard + step) % shards, shards)[0] for step in range(1, shards)
        ]

    def by_side(total):
        return own_part(total, 0, side_at, side), [own_part(total, 0, (side_at + a) % side, side) for a in range(1, side)]

    def by_step(total):
        return [total[s * side : (s + 1) * side] for s in range(shards)]

    def by_near(total):
        return total[0], [total[a] for a in range(1, side)]

    def swap_lines(value, step):
        return lax.ppermute(value, "line", [(i, i ^ step) for i in range(line)])

    flags = jnp.stack([end, shard > 0, side_at > 0]).astype(jnp.int32)

    def f(value):
        return value.astype(f32)

    def pick(flag, got, kept):
        return jnp.where(flag > 0, f(got), f(kept))

    def steps(function, outs, *arrays):
        outs = [v if isinstance(v, jax.ShapeDtypeStruct) else array(v, bf16) for v in outs]
        return run(lambda *v: tuple(post(function, flags, v, outs)), *arrays)

    if (line, side, cores, shards, count) != (4, 2, 2, 2, 2):
        grads_gu, hiddens, sums, chunks = [], [], [], []
        for e in range(count - 1):
            grad_gu, hidden, total, *parts = expert(rows_near, grads_near, w_gate_up, w_down, indices[e], CHUNKS)
            grads_gu.append(grad_gu)
            hiddens.append(hidden)
            sums.append(total)
            chunks.append(parts)
        grad_gu, hidden, *blocks = last_expert(rows_near, grads_near, w_gate_up, w_down, both, grads_gu, sums)
        hiddens.append(hidden)
        chunks.append(weight_grads(rows_near, grads_near, grad_gu, hidden, CHUNKS, both))
        terms = row_terms(hiddens, w_down, both, cores)
        returned = send_back([v for v in add_up(blocks[0], [other_core(g, -c % cores) for c, g in enumerate(blocks[1:], 1)])])
        mixed = send_back([v for v in add_up(terms[0], [other_core(g, -c % cores) for c, g in enumerate(terms[1:], 1)])])
        grad_residual, grad_own, grad_prev, own_w, *other_w = back(returned)
        joined = [jnp.concatenate(other_w[i : i + 3], -1) for i in range(0, len(other_w), 3)]
        own_w = add_up(own_w, [other_core(w, core) for core, w in enumerate(joined, 1)])
        own_w, other_w = by_shard(own_w)
        own_w = add_up(own_w, [from_shard(w, step) for step, w in enumerate(other_w, 1)])
        own_w = add_up(own_w, [other_side(own_w, a) for a in range(1, side)])

        def line_sum(value):
            if line & (line - 1):
                return lax.psum(value, "line")
            for bit in range(line.bit_length() - 1):
                value = value + swap_lines(value, 1 << bit)
            return value

        sum_w, outs = line_sum(own_w), ()
        for e, parts in enumerate(chunks):
            for c, part in enumerate(parts):
                full = line_sum(part)
                pair = jnp.stack([full] + sides(full))
                outs = placed(pair, core_swaps(pair), outs, e, c)
        at_w = jnp.stack([(core_at - core) % cores for core in range(cores)]).astype(jnp.int32) * sum_w.shape[0]
        qkv_sum, out_sum, router_sum, ffn_sum, attn_sum = unpack(
            [w[None] for w in [sum_w] + core_swaps(sum_w)], at_w, sum_w.shape[0] * cores
        )
        grad_sum = grad_own + lax.ppermute(grad_prev, "fsdp", before).astype(f32)
        grad_in = first_back(grad_sum, grad_residual, hidden_in, gain_attn)
        layer_out = add_up(residual, [m.astype(f32) for m in mixed]).astype(bf16)
        return (
            layer_out, grad_in, qkv_sum, out_sum, router_sum, attn_sum[0], ffn_sum[0], outs[0], outs[1],
        )

    gu_0, hid_0, sum_0, *parts_0 = run(lambda i: expert(rows_near, grads_near, w_gate_up, w_down, i, CHUNKS), indices[0])
    chunk = parts_0[0].shape
    two = (2,) + chunk
    in_0 = go_in(parts_0[0])
    gu_1, hid_1, first_half, other_half = run(
        lambda i: last_expert(rows_near, grads_near, w_gate_up, w_down, i, [gu_0], [sum_0]), both
    )
    far = [other_core(other_half)]
    (half_0,) = steps(lambda flag, raw, got: (f(raw) + f(got),), [chunk], parts_0[0], in_0)
    middle_0, in_1 = cross(half_0), go_in(parts_0[1])
    mixed, mixed_other = run(lambda i: row_terms([hid_0, hid_1], w_down, i, cores), both)
    blocks = run(near_sums, first_half, far)
    returned = send_back(blocks)
    parts_1 = run(lambda i: weight_grads(rows_near, grads_near, gu_1, hid_1, CHUNKS, i), both)

    def step_1(flag, half, middle, own, got, raw):
        total = f(half) + f(middle)
        return total, f(own) + f(got), pick(flag[0], raw, total)

    total_0, half_1, sent_2 = steps(step_1, [chunk] * 3, half_0, middle_0, parts_0[1], in_1, parts_1[0])
    both_2, middle_1 = in_and_out(sent_2), cross(half_1)
    grad_residual, grad_own, grad_prev, own_w, *other_w = run(back, returned)
    far_w = [other_core(w) for w in other_w]
    deep, wide = own_w.shape[1:]

    def step_2(flag, own, got, total, half, middle, raw, w, *far):
        summed = f(half) + f(middle)
        joined = f(w) + jnp.concatenate([f(v) for v in far], -1)
        mine, theirs = pick(flag[1], joined[1], joined[0]), pick(flag[1], joined[0], joined[1])
        return f(own) + f(got), pick(flag[0], got, total), summed, pick(flag[0], raw, summed), mine, theirs

    half_2, full_0, total_1, sent_3, own_w, other_w = steps(
        step_2, [chunk] * 4 + [(deep, wide)] * 2,
        parts_1[0], both_2, total_0, half_1, middle_1, parts_1[1], own_w, *far_w,
    )
    side_0, middle_2, both_3 = other_side(full_0), cross(half_2), in_and_out(sent_3)
    far_w, far_m = from_shard(other_w, 1), other_core(mixed_other)

    def step_3(flag, own, got, total, half, middle, first, other, w, far, m, m_far):
        terms = f(m) + f(m_far)
        return (
            f(own) + f(got), pick(flag[0], got, total), f(half) + f(middle), (first, other), f(w) + f(far), terms[:2], terms[2:],
        )

    rows_of = mixed.shape[1]
    half_3, full_1, total_2, pair_0, own_w, own_m, other_m = steps(
        step_3, [chunk] * 3 + [two, (deep, wide)] + [(2, rows_of, D)] * 2,
        parts_1[1], both_3, total_1, half_2, middle_2, full_0, side_0, own_w, far_w, mixed, far_m,
    )
    side_1, middle_3, out_2, core_0 = other_side(full_1), cross(half_3), go_out(total_2), other_core(pair_0)
    in_w = go_in(own_w)

    def step_4(flag, got, total, half, middle, first, other, w, far):
        return pick(flag[0], got, total), f(half) + f(middle), (first, other), f(w) + f(far)

    full_2, total_3, pair_1, half_w = steps(
        step_4, [chunk] * 2 + [two, (deep, wide)], out_2, total_2, half_3, middle_3, full_1, side_1, own_w, in_w
    )
    side_2, out_3, middle_w, core_1 = other_side(full_2), go_out(total_3), cross(half_w), other_core(pair_1)
    far_m = from_shard(other_m, 1)
    outs = run(lambda pair, swap: placed(pair, [swap], (), 0, 0), pair_0, core_0)

    def step_5(flag, got, total, first, other, w, far, m, m_far):
        terms = f(m) + f(m_far)
        return pick(flag[0], got, total), (first, other), f(w) + f(far), terms[0], terms[1]

    full_3, pair_2, total_w, own_m, other_m = steps(
        step_5, [chunk, two, (deep, wide)] + [(rows_of, D)] * 2, out_3, total_3, full_2, side_2, half_w, middle_w, own_m, far_m
    )
    side_3, out_w, core_2 = other_side(full_3), go_out(total_w), other_core(pair_2)
    far_m = other_side(other_m)
    grad_later = lax.ppermute(grad_prev, "fsdp", before)
    outs = run(lambda pair, swap, outs: placed(pair, [swap], outs, 0, 1), pair_1, core_1, outs)

    def step_6(flag, first, other, got, w, rest, m, m_far, own, back):
        return (first, other), pick(flag[0], got, w), rest + f(m) + f(m_far), own + f(back)

    pair_3, full_w, layer_out, grad_sum = steps(
        step_6, [two, (deep, wide), (rows_of, D), array((rows_of, D), f32)],
        full_3, side_3, out_w, total_w, residual, own_m, far_m, grad_own, grad_later,
    )
    core_3, side_w = other_core(pair_3), other_side(full_w)
    grad_in = run(lambda grad: first_back(grad, grad_residual, hidden_in, gain_attn), grad_sum)
    outs = run(lambda pair, swap, outs: placed(pair, [swap], outs, 1, 0), pair_2, core_2, outs)
    outs = run(lambda pair, swap, outs: placed(pair, [swap], outs, 1, 1), pair_3, core_3, outs)
    (sum_w,) = steps(lambda flag, w, far: (f(w) + f(far),), [(deep, wide)], full_w, side_w)
    core_w = other_core(sum_w)
    at_w = jnp.stack([(core_at - core) % cores for core in range(cores)]).astype(jnp.int32) * deep
    qkv_sum, out_sum, router_sum, ffn_sum, attn_sum = run(lambda *v: unpack([w[None] for w in v], at_w, deep * cores), sum_w, core_w)
    return (
        layer_out,
        grad_in,
        qkv_sum,
        out_sum,
        router_sum,
        attn_sum[0],
        ffn_sum[0],
        outs[0],
        outs[1],
    )


def solution(mesh):
    copies, shards = mesh.shape["rep"], mesh.shape["fsdp"]
    local = EXPERTS // shards
    cores = 2 if copies % 2 == 0 and local % 2 == 0 else 1
    side = 2 if cores == 2 and copies % 4 == 0 and local % 4 == 0 else 1
    names = ("line", "side", "core", "fsdp")
    parts = Mesh(mesh.devices.reshape(copies // (side * cores), side, cores, shards), names)
    rows, shard = P(names, None), P("fsdp", None)
    experts = P("fsdp", None, None)
    in_specs = (rows, rows, shard, shard, shard, P("fsdp"), P("fsdp"), experts, experts, rows)
    out_specs = (rows, rows, shard, shard, shard, P("fsdp"), P("fsdp"), experts, experts)
    return jax.shard_map(body, mesh=parts, in_specs=in_specs, out_specs=out_specs, check_vma=False)
```

time: 619 us -> 541 us (0.87)
  the two profiles are of different devices: /device:TPU:0 before, /device:TPU:9 now
where the time goes in v3:
time: 541 us; the launch traced here: 531 us
  Pallas kernels  223 us (41%)
  waiting for transfers between devices  195 us (36%)
  starting transfers between devices  77 us (14%)
  local copies, waits for them, and re-layouts  24.7 us (5%)
  other arithmetic  9.33 us (2%)
    pallas_call x22, Pallas kernels, call(): pl.pallas_call(kernel, out_shape=list(out_shape), grid_spec=spec, input_o...  223 us
    ppermute x39, waiting for transfers between devices, turn(): return lax.ppermute(value, axes, pairs)  109 us
    ppermute x39, starting transfers between devices, turn(): return lax.ppermute(value, axes, pairs)  46.7 us
    ppermute x3, waiting for transfers between devices, go_out(): return lax.ppermute(total, 'line', [(1, 0), (2, 3)])  34.4 us
    ppermute x2, waiting for transfers between devices, in_and_out(): return lax.ppermute(sent, 'line', [(0, 1), (1, 0), (2, 3), (3, 2)])  32.3 us
    unnamed x78, local copies, waits for them, and re-layouts  18.8 us
    ppermute x5, starting transfers between devices, cross(): return lax.ppermute(half, 'line', [(1, 2), (2, 1)])  13.9 us
  transfers between devices with their start and end apart: 54, of which 24 were waited for; matrix products, arithmetic and copies ran while one was open for 3% of the time, Pallas kernels for 33%

profile of v3, /device:TPU:9, one launch (start us, length us, event | category | flops | bytes accessed | tf_op | source)
XLA Modules:
  0.0 530.8 jit_solution(17839818884194639336)
XLA Ops:
  6.7 8.0 %collective-permute-done.1.rest_1_.rest_23_ = bf16[128,2048]{1,0:T(8,128)(2,1)S(1)} collective-permute-done((bf16[128,2048]{1,0:T(8,128)(2,1)S(1)}, bf16[128,2048]{1,0:T(8,128)(2,1)S(1)}, u32[]{:S(2)}, u32[]{:S(2)}) %collective-permute-start.1) | collective-permute-done | bytes 524320 | tf_op jit(solution)/shard_map/ppermute | solution.py:48
  18.3 6.9 %collective-permute-done.prev_ref.rest_16_ = bf16[256,1024]{1,0:T(8,128)(2,1)S(1)} collective-permute-done((bf16[256,1024]{1,0:T(8,128)(2,1)}, bf16[256,1024]{1,0:T(8,128)(2,1)S(1)}, u32[]{:S(2)}, u32[]{:S(2)}) %collective-permute-start) | collective-permute-done | bytes 524320 | tf_op jit(solution)/shard_map/ppermute | solution.py:902
  49.7 8.4 %shard_map.170 = (bf16[256,1024]{1,0:T(8,128)(2,1)}, f32[512,128]{1,0:T(8,128)}) custom-call(s32[1]{0:T(128)} %bitcast.15.flag_ref, bf16[256,1024]{1,0:T(8,128)(2,1)} %get-tuple-element.180.q_ref.rest_10_, bf16[512,1024]{1,0:T(8,128)(2,1)} %get-tuple-element.181.kv_ref.rest_11_), custom_call_target="tpu_custom_call" | custom-call | tf_op jit(solution)/shard_map/pallas_call | solution.py:73
  71.8 10.5 %collective-permute-done.11.refs_1_ = bf16[272,1024]{1,0:T(8,128)(2,1)S(1)} collective-permute-done((bf16[272,1024]{1,0:T(8,128)(2,1)}, bf16[272,1024]{1,0:T(8,128)(2,1)S(1)}, u32[]{:S(2)}, u32[]{:S(2)}) %collective-permute-start.11) | collective-permute-done | bytes 557088 | tf_op jit(solution)/shard_map/ppermute | solution.py:48
  84.0 10.3 %collective-permute-done.12.refs_2_ = bf16[272,1024]{1,0:T(8,128)(2,1)S(1)} collective-permute-done((bf16[272,1024]{1,0:T(8,128)(2,1)}, bf16[272,1024]{1,0:T(8,128)(2,1)S(1)}, u32[]{:S(2)}, u32[]{:S(2)}) %collective-permute-start.12) | collective-permute-done | bytes 557088 | tf_op jit(solution)/shard_map/ppermute | solution.py:48
  98.7 27.2 %shard_map.172 = (bf16[8,256,1024]{2,1,0:T(8,128)(2,1)}, bf16[8,256,512]{2,1,0:T(8,128)(2,1)}, f32[8,8,256]{2,1,0:T(8,128)}, bf16[1024,768]{1,0:T(8,128)(2,1)}, bf16[1024,768]{1,0:T(8,128)(2,1)}) custom-call(s32[2]{0:T(128)} %pad_add_fusion.1.index_ref, bf16[272,1024]{1,0:T(8,128)(2,1)} %get-tuple-element.192.refs_0_, bf16[272,1024]{1,0:T(8,128)(2,1)} %copy-done.2, ...), custom_call_target="tpu_custom_call" | custom-call | tf_op jit(solution)/shard_map/pallas_call | solution.py:73
  127.8 26.8 %shard_map.173 = (bf16[8,256,1024]{2,1,0:T(8,128)(2,1)}, bf16[8,256,512]{2,1,0:T(8,128)(2,1)}, bf16[4,272,1024]{2,1,0:T(8,128)(2,1)}, bf16[4,272,1024]{2,1,0:T(8,128)(2,1)}) custom-call(s32[4]{0:T(128)} %pad_add_fusion.indices_ref.after_ref, bf16[272,1024]{1,0:T(8,128)(2,1)} %get-tuple-element.192.refs_0_, bf16[272,1024]{1,0:T(8,128)(2,1)} %copy-done.2, ...), custom_call_target="tpu_custom_call" | custom-call | tf_op jit(solution)/shard_map/pallas_call | solution.py:73
  156.8 7.0 %collective-permute-done.20.refs_1_ = bf16[1024,768]{1,0:T(8,128)(2,1)} collective-permute-done((bf16[1024,768]{1,0:T(8,128)(2,1)}, bf16[1024,768]{1,0:T(8,128)(2,1)}, u32[]{:S(2)}, u32[]{:S(2)}) %collective-permute-start.20) | collective-permute-done | bytes 1572896 | tf_op jit(solution)/shard_map/ppermute | solution.py:950
  171.0 9.8 %shard_map.175 = (bf16[4,256,1024]{2,1,0:T(8,128)(2,1)}, bf16[4,256,1024]{2,1,0:T(8,128)(2,1)}) custom-call(s32[4]{0:T(128)} %pad_add_fusion.indices_ref.after_ref, bf16[8,256,512]{2,1,0:T(8,128)(2,1)} %get-tuple-element.195.refs_0_, bf16[8,256,512]{2,1,0:T(8,128)(2,1)} %get-tuple-element.203.refs_1_.refs_11_, bf16[8,1024,512]{2,1,0:T(8,128)(2,1)} %refs_3_.1, ...), custom_call_target="tpu_custom_call" | custom-call | tf_op jit(solution)/shard_map/pallas_call | solution.py:73
  186.1 17.8 %shard_map.176 = (bf16[1024,768]{1,0:T(8,128)(2,1)}, bf16[1024,768]{1,0:T(8,128)(2,1)}) custom-call(s32[4]{0:T(128)} %pad_add_fusion.indices_ref.after_ref, bf16[272,1024]{1,0:T(8,128)(2,1)} %get-tuple-element.192.refs_0_, bf16[272,1024]{1,0:T(8,128)(2,1)} %copy-done.2, bf16[272,1024]{1,0:T(8,128)(2,1)} %copy-done.3, ...), custom_call_target="tpu_custom_call" | custom-call | tf_op jit(solution)/shard_map/pallas_call | solution.py:73
  214.5 26.3 %shard_map.178 = (f32[256,1024]{1,0:T(8,128)}, f32[256,1024]{1,0:T(8,128)}, bf16[256,1024]{1,0:T(8,128)(2,1)}, bf16[2,256,3200]{2,1,0:T(8,128)(2,1)}, bf16[2,256...) custom-call(s32[3]{0:T(128)} %pad_add_fusion.2.offsets_ref.out_offsets_ref, ...), custom_call_target="tpu_custom_call" | custom-call | tf_op jit(solution)/shard_map/pallas_call | solution.py:73
  252.0 9.1 %shard_map.179 = (bf16[1024,768]{1,0:T(8,128)(2,1)}, bf16[1024,768]{1,0:T(8,128)(2,1)}, bf16[1024,768]{1,0:T(8,128)(2,1)}, bf16[1024,768]{1,0:T(8,128)(2,1)}, bf...) custom-call(s32[3]{0:T(128)} %add_convert_fusion.1.flags_ref, bf16[1024,768]{1,0:T(8,128)(2,1)} %get-tuple-element.237.refs_4_.refs_0_, ...), custom_call_target="tpu_custom_call" | custom-call | tf_op jit(solution)/shard_map/pallas_call | solution.py:73
  266.4 32.3 %collective-permute-done.31.refs_1_ = bf16[1024,768]{1,0:T(8,128)(2,1)S(1)} collective-permute-done((bf16[1024,768]{1,0:T(8,128)(2,1)}, bf16[1024,768]{1,0:T(8,128)(2,1)S(1)}, u32[]{:S(2)}, u32[]{:S(2)}) %collective-permute-start.31) | collective-permute-done | bytes 1572896 | tf_op jit(solution)/shard_map/ppermute | solution.py:956
  303.6 10.6 %shard_map.180 = (bf16[1024,768]{1,0:T(8,128)(2,1)}, bf16[1024,768]{1,0:T(8,128)(2,1)}, bf16[1024,768]{1,0:T(8,128)(2,1)}, bf16[2,1024,768]{2,1,0:T(8,128)(2,1)}...) custom-call(s32[3]{0:T(128)} %add_convert_fusion.1.flags_ref, ...), custom_call_target="tpu_custom_call" | custom-call | tf_op jit(solution)/shard_map/pallas_call | solution.py:73
  324.4 30.8 %collective-permute-done.36.refs_0_ = bf16[1024,768]{1,0:T(8,128)(2,1)S(1)} collective-permute-done((bf16[1024,768]{1,0:T(8,128)(2,1)}, bf16[1024,768]{1,0:T(8,128)(2,1)S(1)}, u32[]{:S(2)}, u32[]{:S(2)}) %collective-permute-start.36) | collective-permute-done | bytes 1572896 | tf_op jit(solution)/shard_map/ppermute | solution.py:959
  361.3 7.9 %shard_map.181 = (bf16[1024,768]{1,0:T(8,128)(2,1)}, bf16[1024,768]{1,0:T(8,128)(2,1)}, bf16[2,1024,768]{2,1,0:T(8,128)(2,1)}, bf16[256,3200]{1,0:T(8,128)(2,1)}) custom-call(s32[3]{0:T(128)} %add_convert_fusion.1.flags_ref, bf16[1024,768]{1,0:T(8,128)(2,1)} %copy-done.24, bf16[1024,768]{1,0:T(8,128)(2,1)} %get-tuple-element.272.refs_1_, ...), custom_call_target="tpu_custom_call" | custom-call | tf_op jit(solution)/shard_map/pallas_call | solution.py:73
  377.7 7.7 %shard_map.182 = (f32[8,1024,1024]{2,1,0:T(8,128)}, f32[8,1024,512]{2,1,0:T(8,128)}) custom-call(s32[4]{0:T(128)} %get-tuple-element.351.experts_ref, bf16[2,1024,768]{2,1,0:T(8,128)(2,1)} %get-tuple-element.283.refs_0_, bf16[2,1024,768]{2,1,0:T(8,128)(2,1)} %collective-permute-done.44.refs_1_), custom_call_target="tpu_custom_call" | custom-call | tf_op jit(solution)/shard_map/pallas_call | solution.py:73
  385.5 16.5 %collective-permute-done.43.refs_7_ = bf16[2,256,1024]{2,1,0:T(8,128)(2,1)} collective-permute-done((bf16[2,256,1024]{2,1,0:T(8,128)(2,1)}, bf16[2,256,1024]{2,1,0:T(8,128)(2,1)}, u32[]{:S(2)}, u32[]{:S(2)}) %collective-permute-start.43) | collective-permute-done | bytes 1048608 | tf_op jit(solution)/shard_map/ppermute | solution.py:48
  408.6 7.4 %shard_map.183 = (bf16[1024,768]{1,0:T(8,128)(2,1)}, bf16[2,1024,768]{2,1,0:T(8,128)(2,1)}, bf16[256,3200]{1,0:T(8,128)(2,1)}, bf16[256,1024]{1,0:T(8,128)(2,1)}, bf16[256,1024]{1,0:T(8,128)(2,1)}) custom-call(s32[3]{0:T(128)} %add_convert_fusion.1.flags_ref, bf16[1024,768]{1,0:T(8,128)(2,1)} %collective-permute-done.40.refs_0_, ...), custom_call_target="tpu_custom_call" | custom-call | tf_op jit(solution)/shard_map/pallas_call | solution.py:73
  424.7 7.7 %shard_map.184 = (f32[8,1024,1024]{2,1,0:T(8,128)}, f32[8,1024,512]{2,1,0:T(8,128)}) custom-call(s32[4]{0:T(128)} %get-tuple-element.351.experts_ref, bf16[2,1024,768]{2,1,0:T(8,128)(2,1)} %get-tuple-element.300.refs_0_, bf16[2,1024,768]{2,1,0:T(8,128)(2,1)} %copy-done.4, ...), custom_call_target="tpu_custom_call", output_to_operand_aliasing={{0}: (3, {}), {1}: (4, {})} | custom-call | tf_op jit(solution)/shard_map/pallas_call | solution.py:73
  432.5 30.6 %collective-permute-done.47.refs_6_ = bf16[256,1024]{1,0:T(8,128)(2,1)} collective-permute-done((bf16[256,1024]{1,0:T(8,128)(2,1)}, bf16[256,1024]{1,0:T(8,128)(2,1)}, u32[]{:S(2)}, u32[]{:S(2)}) %collective-permute-start.47) | collective-permute-done | bytes 524320 | tf_op jit(solution)/shard_map/ppermute | solution.py:48
  479.8 7.7 %shard_map.187 = (f32[8,1024,1024]{2,1,0:T(8,128)}, f32[8,1024,512]{2,1,0:T(8,128)}) custom-call(s32[4]{0:T(128)} %get-tuple-element.350.experts_ref, bf16[2,1024,768]{2,1,0:T(8,128)(2,1)} %get-tuple-element.320.refs_0_, bf16[2,1024,768]{2,1,0:T(8,128)(2,1)} %copy-done.5, ...), custom_call_target="tpu_custom_call", output_to_operand_aliasing={{0}: (3, {}), {1}: (4, {})} | custom-call | tf_op jit(solution)/shard_map/pallas_call | solution.py:73
  489.2 7.7 %shard_map.188 = (f32[8,1024,1024]{2,1,0:T(8,128)}, f32[8,1024,512]{2,1,0:T(8,128)}) custom-call(s32[4]{0:T(128)} %get-tuple-element.350.experts_ref, bf16[2,1024,768]{2,1,0:T(8,128)(2,1)} %get-tuple-element.326.refs_0_, bf16[2,1024,768]{2,1,0:T(8,128)(2,1)} %copy-done.6, ...), custom_call_target="tpu_custom_call", output_to_operand_aliasing={{0}: (3, {}), {1}: (4, {})} | custom-call | tf_op jit(solution)/shard_map/pallas_call | solution.py:73
  497.0 15.5 %collective-permute-done.50.refs_1_ = bf16[256,3200]{1,0:T(8,128)(2,1)S(1)} collective-permute-done((bf16[256,3200]{1,0:T(8,128)(2,1)}, bf16[256,3200]{1,0:T(8,128)(2,1)S(1)}, u32[]{:S(2)}, u32[]{:S(2)}) %collective-permute-start.50) | collective-permute-done | bytes 1638432 | tf_op jit(solution)/shard_map/ppermute | solution.py:48
  (209 shorter events, 178.6 us)
Async XLA Ops:
  59.4 39.2 %collective-permute-start.18 = (bf16[4,256,1024]{2,1,0:T(8,128)(2,1)S(1)}, bf16[4,256,1024]{2,1,0:T(8,128)(2,1)}, u32[]{:S(2)}, u32[]{:S(2)}) collective-permute-start(bf16[4,256,1024]{2,1,0:T(8,128)(2,1)S(1)} %pad_maximum_fusion.refs_8_), channel_id=1, source_target_pairs={{0,2},{2,0},{1,3},{3,1},{4,6},{6,4},{5,7},{7,5},{8,10},{10,8},{9,1... | collective-permute-start | bytes 6291464 | tf_op jit(solution)/shard_map/ppermute | solution.py:48
  125.8 37.9 %collective-permute-start.20 = (bf16[1024,768]{1,0:T(8,128)(2,1)}, bf16[1024,768]{1,0:T(8,128)(2,1)}, u32[]{:S(2)}, u32[]{:S(2)}) collective-permute-start(bf16[1024,768]{1,0:T(8,128)(2,1)} %get-tuple-element.204.refs_0_), channel_id=1, source_target_pairs={{0,8},{24,16},{1,9},{25,17},{2,10},{26,18},{3,11},{27,19},{4,12},{... | collective-permute-start | bytes 4718600 | tf_op jit(solution)/shard_map/ppermute | solution.py:950
  155.5 48.4 %collective-permute-start.22 = (bf16[1024,768]{1,0:T(8,128)(2,1)}, bf16[1024,768]{1,0:T(8,128)(2,1)S(1)}, u32[]{:S(2)}, u32[]{:S(2)}) collective-permute-start(bf16[1024,768]{1,0:T(8,128)(2,1)} %get-tuple-element.216.refs_2_), channel_id=1, source_target_pairs={{0,8},{24,16},{1,9},{25,17},{2,10},{26,18},{3,11},{27,19},{4,12},{... | collective-permute-start | bytes 4718600 | tf_op jit(solution)/shard_map/ppermute | solution.py:950
  167.7 36.4 %collective-permute-start.21 = (bf16[1024,768]{1,0:T(8,128)(2,1)}, bf16[1024,768]{1,0:T(8,128)(2,1)}, u32[]{:S(2)}, u32[]{:S(2)}) collective-permute-start(bf16[1024,768]{1,0:T(8,128)(2,1)} %shard_map.174.refs_0_), channel_id=1, source_target_pairs={{8,16},{16,8},{9,17},{17,9},{10,18},{18,10},{11,19},{19,11},{12,20... | collective-permute-start | bytes 4718600 | tf_op jit(solution)/shard_map/ppermute | solution.py:953
  210.7 38.9 %collective-permute-start.23 = (bf16[1024,768]{1,0:T(8,128)(2,1)}, bf16[1024,768]{1,0:T(8,128)(2,1)S(1)}, u32[]{:S(2)}, u32[]{:S(2)}) collective-permute-start(bf16[1024,768]{1,0:T(8,128)(2,1)} %get-tuple-element.219), channel_id=1, source_target_pairs={{0,8},{8,0},{16,24},{24,16},{1,9},{9,1},{17,25},{25,17},{2,10},{10... | collective-permute-start | bytes 4718600 | tf_op jit(solution)/shard_map/ppermute | solution.py:956
  210.7 38.9 %collective-permute-start.24 = (bf16[1024,768]{1,0:T(8,128)(2,1)}, bf16[1024,768]{1,0:T(8,128)(2,1)S(1)}, u32[]{:S(2)}, u32[]{:S(2)}) collective-permute-start(bf16[1024,768]{1,0:T(8,128)(2,1)} %get-tuple-element.240.refs_3_), channel_id=1, source_target_pairs={{8,16},{16,8},{9,17},{17,9},{10,18},{18,10},{11,19},{19,11},{12,20... | collective-permute-start | bytes 4718600 | tf_op jit(solution)/shard_map/ppermute | solution.py:953
  261.1 40.2 %collective-permute-start.34 = (bf16[256,3200]{1,0:T(8,128)(2,1)}, bf16[256,3200]{1,0:T(8,128)(2,1)S(1)}, u32[]{:S(2)}, u32[]{:S(2)}) collective-permute-start(bf16[256,3200]{1,0:T(8,128)(2,1)} %get-tuple-element.252), channel_id=1, source_target_pairs={{0,1},{1,0},{2,3},{3,2},{4,5},{5,4},{6,7},{7,6},{8,9},{9,8},{10,11... | collective-permute-start | bytes 4915208 | tf_op jit(solution)/shard_map/ppermute | solution.py:48
  263.2 35.5 %collective-permute-start.31 = (bf16[1024,768]{1,0:T(8,128)(2,1)}, bf16[1024,768]{1,0:T(8,128)(2,1)S(1)}, u32[]{:S(2)}, u32[]{:S(2)}) collective-permute-start(bf16[1024,768]{1,0:T(8,128)(2,1)} %get-tuple-element.247), channel_id=1, source_target_pairs={{0,8},{8,0},{16,24},{24,16},{1,9},{9,1},{17,25},{25,17},{2,10},{10... | collective-permute-start | bytes 4718600 | tf_op jit(solution)/shard_map/ppermute | solution.py:956
  263.2 37.4 %collective-permute-start.32 = (bf16[1024,768]{1,0:T(8,128)(2,1)}, bf16[1024,768]{1,0:T(8,128)(2,1)S(1)}, u32[]{:S(2)}, u32[]{:S(2)}) collective-permute-start(bf16[1024,768]{1,0:T(8,128)(2,1)} %get-tuple-element.256.refs_3_), channel_id=1, source_target_pairs={{8,16},{16,8},{9,17},{17,9},{10,18},{18,10},{11,19},{19,11},{12,20... | collective-permute-start | bytes 4718600 | tf_op jit(solution)/shard_map/ppermute | solution.py:953
  266.0 35.2 %collective-permute-start.33 = (bf16[1024,768]{1,0:T(8,128)(2,1)}, bf16[1024,768]{1,0:T(8,128)(2,1)S(1)}, u32[]{:S(2)}, u32[]{:S(2)}) collective-permute-start(bf16[1024,768]{1,0:T(8,128)(2,1)} %get-tuple-element.258.refs_5_), channel_id=1, source_target_pairs={{0,4},{4,0},{1,5},{5,1},{2,6},{6,2},{3,7},{7,3},{8,12},{12,8},{9,1... | collective-permute-start | bytes 4718600 | tf_op jit(solution)/shard_map/ppermute | solution.py:48
  314.1 62.7 %collective-permute-start.44 = (bf16[2,1024,768]{2,1,0:T(8,128)(2,1)}, bf16[2,1024,768]{2,1,0:T(8,128)(2,1)}, u32[]{:S(2)}, u32[]{:S(2)}) collective-permute-start(bf16[2,1024,768]{2,1,0:T(8,128)(2,1)} %get-tuple-element.283.refs_0_), channel_id=1, source_target_pairs={{0,2},{2,0},{1,3},{3,1},{4,6},{6,4},{5,7},{7,5},{8,10},{10,8},{9,1... | collective-permute-start | bytes 9437192 | tf_op jit(solution)/shard_map/ppermute | solution.py:48
  316.0 43.6 %collective-permute-start.39 = (bf16[256,3200]{1,0:T(8,128)(2,1)}, bf16[256,3200]{1,0:T(8,128)(2,1)S(1)}, u32[]{:S(2)}, u32[]{:S(2)}) collective-permute-start(bf16[256,3200]{1,0:T(8,128)(2,1)} %get-tuple-element.277.refs_6_), channel_id=1, source_target_pairs={{0,8},{24,16},{1,9},{25,17},{2,10},{26,18},{3,11},{27,19},{4,12},{... | collective-permute-start | bytes 4915208 | tf_op jit(solution)/shard_map/ppermute | solution.py:950
  317.3 37.9 %collective-permute-start.36 = (bf16[1024,768]{1,0:T(8,128)(2,1)}, bf16[1024,768]{1,0:T(8,128)(2,1)S(1)}, u32[]{:S(2)}, u32[]{:S(2)}) collective-permute-start(bf16[1024,768]{1,0:T(8,128)(2,1)} %get-tuple-element.272.refs_1_), channel_id=1, source_target_pairs={{8,0},{16,24},{9,1},{17,25},{10,2},{18,26},{11,3},{19,27},{12,4},{... | collective-permute-start | bytes 4718600 | tf_op jit(solution)/shard_map/ppermute | solution.py:959
  321.5 37.5 %collective-permute-start.37 = (bf16[1024,768]{1,0:T(8,128)(2,1)}, bf16[1024,768]{1,0:T(8,128)(2,1)S(1)}, u32[]{:S(2)}, u32[]{:S(2)}) collective-permute-start(bf16[1024,768]{1,0:T(8,128)(2,1)} %get-tuple-element.273.refs_2_), channel_id=1, source_target_pairs={{8,16},{16,8},{9,17},{17,9},{10,18},{18,10},{11,19},{19,11},{12,20... | collective-permute-start | bytes 4718600 | tf_op jit(solution)/shard_map/ppermute | solution.py:953
  324.3 35.3 %collective-permute-start.38 = (bf16[1024,768]{1,0:T(8,128)(2,1)}, bf16[1024,768]{1,0:T(8,128)(2,1)S(1)}, u32[]{:S(2)}, u32[]{:S(2)}) collective-permute-start(bf16[1024,768]{1,0:T(8,128)(2,1)} %get-tuple-element.275.refs_4_), channel_id=1, source_target_pairs={{0,4},{4,0},{1,5},{5,1},{2,6},{6,2},{3,7},{7,3},{8,12},{12,8},{9,1... | collective-permute-start | bytes 4718600 | tf_op jit(solution)/shard_map/ppermute | solution.py:48
  369.2 39.4 %collective-permute-start.42 = (bf16[256,3200]{1,0:T(8,128)(2,1)}, bf16[256,3200]{1,0:T(8,128)(2,1)}, u32[]{:S(2)}, u32[]{:S(2)}) collective-permute-start(bf16[256,3200]{1,0:T(8,128)(2,1)} %get-tuple-element.291.refs_4_), channel_id=1, source_target_pairs={{8,16},{16,8},{9,17},{17,9},{10,18},{18,10},{11,19},{19,11},{12,20... | collective-permute-start | bytes 4915208 | tf_op jit(solution)/shard_map/ppermute | solution.py:953
  371.9 33.6 %collective-permute-start.40 = (bf16[1024,768]{1,0:T(8,128)(2,1)}, bf16[1024,768]{1,0:T(8,128)(2,1)}, u32[]{:S(2)}, u32[]{:S(2)}) collective-permute-start(bf16[1024,768]{1,0:T(8,128)(2,1)} %get-tuple-element.288.refs_1_), channel_id=1, source_target_pairs={{8,0},{16,24},{9,1},{17,25},{10,2},{18,26},{11,3},{19,27},{12,4},{... | collective-permute-start | bytes 4718600 | tf_op jit(solution)/shard_map/ppermute | solution.py:959
  374.3 34.3 %collective-permute-start.41 = (bf16[1024,768]{1,0:T(8,128)(2,1)}, bf16[1024,768]{1,0:T(8,128)(2,1)}, u32[]{:S(2)}, u32[]{:S(2)}) collective-permute-start(bf16[1024,768]{1,0:T(8,128)(2,1)} %get-tuple-element.289.refs_2_), channel_id=1, source_target_pairs={{0,4},{4,0},{1,5},{5,1},{2,6},{6,2},{3,7},{7,3},{8,12},{12,8},{9,1... | collective-permute-start | bytes 4718600 | tf_op jit(solution)/shard_map/ppermute | solution.py:48
  374.5 46.8 %collective-permute-start.49 = (bf16[2,1024,768]{2,1,0:T(8,128)(2,1)}, bf16[2,1024,768]{2,1,0:T(8,128)(2,1)S(1)}, u32[]{:S(2)}, u32[]{:S(2)}) collective-permute-start(bf16[2,1024,768]{2,1,0:T(8,128)(2,1)} %get-tuple-element.300.refs_0_), channel_id=1, source_target_pairs={{0,2},{2,0},{1,3},{3,1},{4,6},{6,4},{5,7},{7,5},{8,10},{10,8},{9,1... | collective-permute-start | bytes 9437192 | tf_op jit(solution)/shard_map/ppermute | solution.py:48
  416.0 47.1 %collective-permute-start.46 = (bf16[256,3200]{1,0:T(8,128)(2,1)}, bf16[256,3200]{1,0:T(8,128)(2,1)}, u32[]{:S(2)}, u32[]{:S(2)}) collective-permute-start(bf16[256,3200]{1,0:T(8,128)(2,1)} %get-tuple-element.309.refs_3_), channel_id=1, source_target_pairs={{8,0},{16,24},{9,1},{17,25},{10,2},{18,26},{11,3},{19,27},{12,4},{... | collective-permute-start | bytes 4915208 | tf_op jit(solution)/shard_map/ppermute | solution.py:959
  418.5 44.6 %collective-permute-start.45 = (bf16[1024,768]{1,0:T(8,128)(2,1)}, bf16[1024,768]{1,0:T(8,128)(2,1)S(1)}, u32[]{:S(2)}, u32[]{:S(2)}) collective-permute-start(bf16[1024,768]{1,0:T(8,128)(2,1)} %get-tuple-element.306.refs_0_), channel_id=1, source_target_pairs={{0,4},{4,0},{1,5},{5,1},{2,6},{6,2},{3,7},{7,3},{8,12},{12,8},{9,1... | collective-permute-start | bytes 4718600 | tf_op jit(solution)/shard_map/ppermute | solution.py:48
  419.9 43.2 %collective-permute-start.47 = (bf16[256,1024]{1,0:T(8,128)(2,1)}, bf16[256,1024]{1,0:T(8,128)(2,1)}, u32[]{:S(2)}, u32[]{:S(2)}) collective-permute-start(bf16[256,1024]{1,0:T(8,128)(2,1)} %get-tuple-element.298), channel_id=1, source_target_pairs={{0,4},{4,0},{1,5},{5,1},{2,6},{6,2},{3,7},{7,3},{8,12},{12,8},{9,1... | collective-permute-start | bytes 1572872 | tf_op jit(solution)/shard_map/ppermute | solution.py:48
  421.3 56.8 %collective-permute-start.52 = (bf16[2,1024,768]{2,1,0:T(8,128)(2,1)}, bf16[2,1024,768]{2,1,0:T(8,128)(2,1)S(1)}, u32[]{:S(2)}, u32[]{:S(2)}) collective-permute-start(bf16[2,1024,768]{2,1,0:T(8,128)(2,1)} %get-tuple-element.320.refs_0_), channel_id=1, source_target_pairs={{0,2},{2,0},{1,3},{3,1},{4,6},{6,4},{5,7},{7,5},{8,10},{10,8},{9,1... | collective-permute-start | bytes 9437192 | tf_op jit(solution)/shard_map/ppermute | solution.py:48
  474.9 37.6 %collective-permute-start.50 = (bf16[256,3200]{1,0:T(8,128)(2,1)}, bf16[256,3200]{1,0:T(8,128)(2,1)S(1)}, u32[]{:S(2)}, u32[]{:S(2)}) collective-permute-start(bf16[256,3200]{1,0:T(8,128)(2,1)} %get-tuple-element.332.refs_0_), channel_id=1, source_target_pairs={{0,4},{4,0},{1,5},{5,1},{2,6},{6,2},{3,7},{7,3},{8,12},{12,8},{9,1... | collective-permute-start | bytes 4915208 | tf_op jit(solution)/shard_map/ppermute | solution.py:48
  (68 other events, 751.4 us)

commit v4 on v3

--- a/solution.py
+++ b/solution.py
@@ -27,6 +27,7 @@
 score_scale = HEAD_DIM ** (-0.5)
 bf16, f32 = jnp.bfloat16, jnp.float32
 VMEM = 56 * 1024 * 1024
+POST_VMEM = 18 * 1024 * 1024
 
 
 def dot(left, right, dims=((1,), (0,))):
@@ -61,7 +62,7 @@
 STAY = pl.BlockSpec(memory_space=pl.ANY)
 
 
-def call(kernel, out_shape, in_specs, operands, out_specs=None, scratch=(), grid=None, prefetch=0, aliases=None):
+def call(kernel, out_shape, in_specs, operands, out_specs=None, scratch=(), grid=None, prefetch=0, aliases=None, vmem=VMEM):
     out_specs = [whole(s.shape) for s in out_shape] if out_specs is None else out_specs
     spec = pltpu.PrefetchScalarGridSpec(
         num_scalar_prefetch=prefetch,
@@ -75,7 +76,7 @@
         out_shape=list(out_shape),
         grid_spec=spec,
         input_output_aliases=aliases or {},
-        compiler_params=pltpu.CompilerParams(vmem_limit_bytes=VMEM),
+        compiler_params=pltpu.CompilerParams(vmem_limit_bytes=vmem),
         cost_estimate=pl.CostEstimate(flops=0, transcendentals=0, bytes_accessed=0),
     )(*operands)
 
@@ -249,8 +250,28 @@
 
 def write_chunks(out_refs, at, values):
     part = F // len(out_refs)
-    for c, out_ref in enumerate(out_refs):
-        out_ref[:, at * part : (at + 1) * part] = values[:, c * part : (c + 1) * part].astype(bf16)
+    deep = 128
+
+    def rows(r, carry):
+        for c, out_ref in enumerate(out_refs):
+            piece = values[pl.ds(pl.multiple_of(r * deep, deep), deep), c * part : (c + 1) * part]
+            out_ref[pl.ds(pl.multiple_of(r * deep, deep), deep), at * part : (at + 1) * part] = piece.astype(bf16)
+        return carry
+
+    lax.fori_loop(0, D // deep, rows, 0)
+
+
+def clear(i, accs):
+    deep = 128
+
+    @pl.when(i == 0)
+    def _():
+        def rows(r, carry):
+            for acc in accs:
+                acc[pl.ds(pl.multiple_of(r * deep, deep), deep), :] = jnp.zeros((deep, acc.shape[1]), f32)
+            return carry
+
+        lax.fori_loop(0, D // deep, rows, 0)
 
 
 def expert(rows, grads, w_gate_up, w_down, index, chunks):
@@ -308,20 +329,13 @@
             sum_ref[b] = jnp.broadcast_to(sums[at], (length, 128)).T[:8]
         if not chunks:
             return
+        clear(i, accs)
         for p, (left, right) in enumerate(((both, grad_gate), (both, grad_up), (grad, gated))):
-            term, acc = dot(left, right, ((0,), (0,))), accs[p]
-
-            @pl.when(i == 0)
-            def _():
-                acc[...] = term
-
-            @pl.when((i > 0) & (i < steps - 1))
-            def _():
-                acc[...] += term
+            accs[p][...] += dot(left, right, ((0,), (0,)))
 
             @pl.when(i == steps - 1)
             def _():
-                write_chunks(out_refs, p, acc[...] + term)
+                write_chunks(out_refs, p, accs[p])
 
     def block(*shape):
         return pl.BlockSpec((step,) + shape, lambda i, index: (i,) + (0,) * len(shape))
@@ -494,20 +508,13 @@
         grad_gate = jnp.concatenate([dgu_ref[b, :, :F] for b in range(step)], 0)
         grad_up = jnp.concatenate([dgu_ref[b, :, F:] for b in range(step)], 0)
         gated = jnp.concatenate([hid_ref[b] for b in range(step)], 0)
+        clear(i, accs)
         for p, (left, right) in enumerate(((both, grad_gate), (both, grad_up), (grad, gated))):
-            term, acc = dot(left, right, ((0,), (0,))), accs[p]
-
-            @pl.when(i == 0)
-            def _():
-                acc[...] = term
-
-            @pl.when((i > 0) & (i < steps - 1))
-            def _():
-                acc[...] += term
+            accs[p][...] += dot(left, right, ((0,), (0,)))
 
             @pl.when(i == steps - 1)
             def _():
-                write_chunks(out_refs, p, acc[...] + term)
+                write_chunks(out_refs, p, accs[p])
 
     def block(*shape):
         return pl.BlockSpec((step,) + shape, lambda i, after: (i,) + (0,) * len(shape))
@@ -586,7 +593,7 @@
         out_refs, qkv_refs, rest = rest[:out_count], rest[out_count : out_count + qkv_count], rest[out_count + qkv_count :]
         gres_ref, gown_ref, gprev_ref, own_grad_ref = rest[:4]
         far_refs, rest = rest[4 : 4 + 3 * (cores - 1)], rest[4 + 3 * (cores - 1) :]
-        w_out, w_qkv, gatt_ref, dq_ref, dkv_ref, small_ref, out_sems, qkv_sems = rest
+        w_out, w_qkv, gatt_ref, dq_ref, dkv_ref, small_ref, sum_ref, out_sems, qkv_sems, end_sems = rest
         out_copies = load_rows(out_refs, out_offsets_ref, w_out, out_sems)
         qkv_copies = load_rows(qkv_refs, qkv_offsets_ref, w_qkv, qkv_sems)
         total = term_refs[0][...].astype(f32)
@@ -612,19 +619,7 @@
         gatt_ref[...] = dot(grad_attn, w_out[...], ((1,), (1,))).astype(bf16)
 
         def write(at, values):
-            group = min(at // D, 2)
-            start = at - group * D
-            for p in range(shards * cores):
-                rows_of = values[p * deep : (p + 1) * deep]
-                for j in range(cores):
-
-                    @pl.when((core_ref[0] + j) % cores == p % cores)
-                    def _():
-                        if j == 0:
-                            own_grad_ref[p // cores, :, at : at + values.shape[1]] = rows_of.astype(bf16)
-                        else:
-                            ref = far_refs[3 * (j - 1) + group]
-                            ref[p // cores, :, start : start + values.shape[1]] = rows_of.astype(bf16)
+            sum_ref[:, at : at + values.shape[1]] = values.astype(bf16)
 
         write(width, dot(att_ref[...], grad_attn, ((0,), (0,))))
 
@@ -679,6 +674,18 @@
         gain_grad = jnp.sum(own * normed_own + from_kv[:length] * normed_prev, 0, keepdims=True)
         column = jnp.broadcast_to(gain_grad, (128, D)).T
         write(width + D, jnp.where(lanes((D, 128)) == EXPERTS + 1, column, small_ref[...]))
+        copies = []
+        for s in range(shards):
+            for j in range(cores):
+                at = pl.multiple_of((s * cores + (core_ref[0] + j) % cores) * deep, 16)
+                targets = [(own_grad_ref, 0)] if j == 0 else [(far_refs[3 * (j - 1) + g], g * D) for g in range(3)]
+                for g, (target, start) in enumerate(targets):
+                    source = sum_ref.at[pl.ds(at, deep), start : start + target.shape[2]]
+                    copy = pltpu.make_async_copy(source, target.at[s], end_sems.at[s, j, g])
+                    copy.start()
+                    copies.append(copy)
+        for copy in copies:
+            copy.wait()
 
     operands = (
         *returned, residual, router, routes, cotangent, gain, router_w, query, kv, lse, cosines, sines, inputs,
@@ -695,6 +702,7 @@
         + [array((shards, deep, w), bf16) for w in (D, D, D + 128)] * (cores - 1),
         [SCALARS] * 4 + [whole(v.shape) for v in operands] + [STAY] * (out_count + qkv_count),
         (out_offsets, qkv_offsets, flag, core, *operands, *out_pieces, *qkv_pieces),
+        out_specs=[whole((length, D)), whole((length, D)), whole((length, D))] + [STAY] * (1 + 3 * (cores - 1)),
         scratch=[
             pltpu.VMEM((QW, D), bf16),
             pltpu.VMEM((D, width), bf16),
@@ -702,8 +710,10 @@
             pltpu.VMEM((length, QW), bf16),
             pltpu.VMEM((2 * length, 2 * KVW), bf16),
             pltpu.VMEM((D, 128), f32),
+            pltpu.VMEM((D, width + D + 128), bf16),
             pltpu.SemaphoreType.DMA((out_count,)),
             pltpu.SemaphoreType.DMA((qkv_count,)),
+            pltpu.SemaphoreType.DMA((shards, cores, 3)),
         ],
     )
 
@@ -715,7 +725,7 @@
         out_ref[...] = res_ref[...] + norm_back(normed, inverse, grad)
 
     operands = (grad_sum, grad_residual, hidden_own, gain)
-    return call(kernel, [array(grad_sum.shape, f32)], [whole(v.shape) for v in operands], operands)[0]
+    return call(kernel, [array(grad_sum.shape, f32)], [whole(v.shape) for v in operands], operands, vmem=16 * 1024 * 1024)[0]
 
 
 def place(sources, experts, outs, shapes, chunk, chunks):
@@ -726,9 +736,16 @@
         source_refs = refs[: len(sources)]
         gate_up_ref, down_ref, wide, sems = refs[len(sources) + len(outs) :]
         copies = []
+        deep = 128
         values = [ref.at[i] for ref in source_refs for i in range(ref.shape[0])]
         for i, source in enumerate(values):
-            wide[i] = source[...].astype(f32)
+
+            def rows(r, carry):
+                at = pl.ds(pl.multiple_of(r * deep, deep), deep)
+                wide[i, at, :] = source[at, :].astype(f32)
+                return carry
+
+            lax.fori_loop(0, D // deep, rows, 0)
             for p, target in enumerate(
                 (
                     gate_up_ref.at[experts_ref[i], :, chunk * part : (chunk + 1) * part],
@@ -750,6 +767,7 @@
         out_specs=[STAY, STAY],
         scratch=[pltpu.VMEM((count, D, 3 * part), f32), pltpu.SemaphoreType.DMA((count, 3))],
         aliases={1 + len(sources) + i: i for i in range(len(outs))},
+        vmem=28 * 1024 * 1024,
     )
 
 
@@ -794,31 +812,35 @@
 
 
 def post(function, flags, arrays, outs):
-    parts = 4
-
-    def cut(shape):
-        return shape[:-2] + (shape[-2] // parts, shape[-1])
+    parts = 8
 
     def kernel(flags_ref, *refs):
-        values = function([flags_ref[i] for i in range(flags.shape[0])], *[ref[...] for ref in refs[: len(arrays)]])
-        for ref, value in zip(refs[len(arrays) :], values):
-            if isinstance(value, tuple):
-                for i, v in enumerate(value):
-                    ref[i] = v.astype(ref.dtype)
-            else:
-                ref[...] = value.astype(ref.dtype)
-
-    def spec(shape):
-        return pl.BlockSpec(cut(shape), lambda i: (0,) * (len(shape) - 2) + (i, 0))
-
-    return call(
+        ins, results = refs[: len(arrays)], refs[len(arrays) :]
+        scalars = [flags_ref[i] for i in range(flags.shape[0])]
+
+        def part_of(ref, r):
+            deep = ref.shape[-2] // parts
+            return (slice(None),) * (len(ref.shape) - 2) + (pl.ds(pl.multiple_of(r * deep, deep), deep), slice(None))
+
+        def rows(r, carry):
+            values = function(scalars, *[ref[part_of(ref, r)] for ref in ins])
+            for ref, value in zip(results, values):
+                if isinstance(value, tuple):
+                    value = jnp.stack(value)
+                ref[part_of(ref, r)] = value.astype(ref.dtype)
+            return carry
+
+        lax.fori_loop(0, parts, rows, 0)
+
+    near = pl.BlockSpec(memory_space=pltpu.VMEM)
+    return pl.pallas_call(
         kernel,
-        outs,
-        [SCALARS] + [spec(v.shape) for v in arrays],
-        (flags, *arrays),
-        out_specs=[spec(v.shape) for v in outs],
-        grid=(parts,),
-    )
+        out_shape=list(outs),
+        in_specs=[SCALARS] + [near] * len(arrays),
+        out_specs=[near] * len(outs),
+        compiler_params=pltpu.CompilerParams(vmem_limit_bytes=POST_VMEM),
+        cost_estimate=pl.CostEstimate(flops=0, transcendentals=0, bytes_accessed=0),
+    )(flags, *arrays)
 
 
 def tie(values, after):

time: 541 us -> 503 us (0.930)
  the two profiles are of different devices: /device:TPU:9 before, /device:TPU:0 now
where the time goes in v4:
time: 503 us; the launch traced here: 493 us
  waiting for transfers between devices  219 us (44%)
  Pallas kernels  181 us (36%)
  starting transfers between devices  58.1 us (12%)
  local copies, waits for them, and re-layouts  23.3 us (5%)
  other arithmetic  10.6 us (2%)
    pallas_call x14, Pallas kernels, call(): pl.pallas_call(kernel, out_shape=list(out_shape), grid_spec=spec, input_o...  157 us
    ppermute x39, waiting for transfers between devices, turn(): return lax.ppermute(value, axes, pairs)  123 us
    ppermute x3, waiting for transfers between devices, go_out(): return lax.ppermute(total, 'line', [(1, 0), (2, 3)])  46.4 us
    ppermute x2, waiting for transfers between devices, in_and_out(): return lax.ppermute(sent, 'line', [(0, 1), (1, 0), (2, 3), (3, 2)])  33.7 us
    ppermute x39, starting transfers between devices, turn(): return lax.ppermute(value, axes, pairs)  27.8 us
    pallas_call x8, Pallas kernels, post(): pl.pallas_call(kernel, out_shape=list(outs), in_specs=[SCALARS] + [near]...  23.3 us
    unnamed x74, local copies, waits for them, and re-layouts  17.1 us
    ppermute x3, starting transfers between devices, go_in(): return lax.ppermute(raw, 'line', [(0, 1), (3, 2)])  10.6 us
  transfers between devices with their start and end apart: 54, of which 23 were waited for; matrix products, arithmetic and copies ran while one was open for 3% of the time, Pallas kernels for 29%

profile of v4, /device:TPU:0, one launch (start us, length us, event | category | flops | bytes accessed | tf_op | source)
XLA Modules:
  0.0 493.5 jit_solution(17157443035039277484)
XLA Ops:
  8.3 9.0 %collective-permute-done.1.rest_1_.rest_23_ = bf16[128,2048]{1,0:T(8,128)(2,1)S(1)} collective-permute-done((bf16[128,2048]{1,0:T(8,128)(2,1)S(1)}, bf16[128,2048]{1,0:T(8,128)(2,1)S(1)}, u32[]{:S(2)}, u32[]{:S(2)}) %collective-permute-start.1) | collective-permute-done | bytes 524320 | tf_op jit(solution)/shard_map/ppermute | solution.py:49
  22.1 6.5 %collective-permute-done.prev_ref.rest_16_ = bf16[256,1024]{1,0:T(8,128)(2,1)S(1)} collective-permute-done((bf16[256,1024]{1,0:T(8,128)(2,1)}, bf16[256,1024]{1,0:T(8,128)(2,1)S(1)}, u32[]{:S(2)}, u32[]{:S(2)}) %collective-permute-start) | collective-permute-done | bytes 524320 | tf_op jit(solution)/shard_map/ppermute | solution.py:924
  43.3 6.7 %shard_map.169 = (bf16[256,1024]{1,0:T(8,128)(2,1)}, bf16[512,1024]{1,0:T(8,128)(2,1)}, bf16[512,1024]{1,0:T(8,128)(2,1)}) custom-call(s32[5]{0:T(128)} %stack.111.offsets_ref.qkv_offsets_ref, bf16[256,1024]{1,0:T(8,128)(2,1)} %copy-done.30, bf16[256,1024]{1,0:T(8,128)(2,1)} %hid_ref.1, f32[1,1024]{1,0:T(1,128)} %get-tuple-element.357.gain_ref, ...), custom_call_target="tpu_custom_call" | custom-call | tf_op jit(solution)/shard_map/pallas_call | solution.py:74
  50.4 8.6 %shard_map.170 = (bf16[256,1024]{1,0:T(8,128)(2,1)}, f32[512,128]{1,0:T(8,128)}) custom-call(s32[1]{0:T(128)} %bitcast.15.flag_ref, bf16[256,1024]{1,0:T(8,128)(2,1)} %get-tuple-element.180.q_ref.rest_10_, bf16[512,1024]{1,0:T(8,128)(2,1)} %get-tuple-element.181.kv_ref.rest_11_), custom_call_target="tpu_custom_call" | custom-call | tf_op jit(solution)/shard_map/pallas_call | solution.py:74
  63.9 5.2 %shard_map.171 = (f32[256,1024]{1,0:T(8,128)}, f32[256,128]{1,0:T(8,128)}, bf16[272,1024]{1,0:T(8,128)(2,1)}) custom-call(s32[3]{0:T(128)} %pad_add_fusion.2.offsets_ref.out_offsets_ref, bf16[256,1024]{1,0:T(8,128)(2,1)} %get-tuple-element.188.att_ref.rest_18_, bf16[256,1024]{1,0:T(8,128)(2,1)} %hid_ref.1, f32[1,1024]{1,0:T(1,128)} %get-tuple-element.356.gain_ref.rest_8_, ...), custom_call_target="tpu_custom_call" | custom-call | tf_op jit(solution)/shard_map/pallas_call | solution.py:74
  72.7 12.2 %collective-permute-done.11.refs_1_ = bf16[272,1024]{1,0:T(8,128)(2,1)S(1)} collective-permute-done((bf16[272,1024]{1,0:T(8,128)(2,1)}, bf16[272,1024]{1,0:T(8,128)(2,1)S(1)}, u32[]{:S(2)}, u32[]{:S(2)}) %collective-permute-start.11) | collective-permute-done | bytes 557088 | tf_op jit(solution)/shard_map/ppermute | solution.py:49
  84.9 11.8 %collective-permute-done.12.refs_2_ = bf16[272,1024]{1,0:T(8,128)(2,1)S(1)} collective-permute-done((bf16[272,1024]{1,0:T(8,128)(2,1)}, bf16[272,1024]{1,0:T(8,128)(2,1)S(1)}, u32[]{:S(2)}, u32[]{:S(2)}) %collective-permute-start.12) | collective-permute-done | bytes 557088 | tf_op jit(solution)/shard_map/ppermute | solution.py:49
  99.8 27.0 %shard_map.172 = (bf16[8,256,1024]{2,1,0:T(8,128)(2,1)}, bf16[8,256,512]{2,1,0:T(8,128)(2,1)}, f32[8,8,256]{2,1,0:T(8,128)}, bf16[1024,768]{1,0:T(8,128)(2,1)}, bf16[1024,768]{1,0:T(8,128)(2,1)}) custom-call(s32[2]{0:T(128)} %pad_add_fusion.1.index_ref, bf16[272,1024]{1,0:T(8,128)(2,1)} %get-tuple-element.192.refs_0_, bf16[272,1024]{1,0:T(8,128)(2,1)} %copy-done.23, ...), custom_call_target="tpu_custom_call" | custom-call | tf_op jit(solution)/shard_map/pallas_call | solution.py:74
  131.8 26.9 %shard_map.173 = (bf16[8,256,1024]{2,1,0:T(8,128)(2,1)}, bf16[8,256,512]{2,1,0:T(8,128)(2,1)}, bf16[4,272,1024]{2,1,0:T(8,128)(2,1)}, bf16[4,272,1024]{2,1,0:T(8,128)(2,1)}) custom-call(s32[4]{0:T(128)} %pad_add_fusion.indices_ref.after_ref, bf16[272,1024]{1,0:T(8,128)(2,1)} %get-tuple-element.192.refs_0_, bf16[272,1024]{1,0:T(8,128)(2,1)} %copy-done.23, ...), custom_call_target="tpu_custom_call" | custom-call | tf_op jit(solution)/shard_map/pallas_call | solution.py:74
  160.2 5.7 %collective-permute-done.20.refs_1_ = bf16[1024,768]{1,0:T(8,128)(2,1)S(1)} collective-permute-done((bf16[1024,768]{1,0:T(8,128)(2,1)}, bf16[1024,768]{1,0:T(8,128)(2,1)S(1)}, u32[]{:S(2)}, u32[]{:S(2)}) %collective-permute-start.20) | collective-permute-done | bytes 1572896 | tf_op jit(solution)/shard_map/ppermute | solution.py:972
  167.7 9.7 %shard_map.175 = (bf16[4,256,1024]{2,1,0:T(8,128)(2,1)}, bf16[4,256,1024]{2,1,0:T(8,128)(2,1)}) custom-call(s32[4]{0:T(128)} %pad_add_fusion.indices_ref.after_ref, bf16[8,256,512]{2,1,0:T(8,128)(2,1)} %get-tuple-element.195.refs_0_, bf16[8,256,512]{2,1,0:T(8,128)(2,1)} %get-tuple-element.203.refs_1_.refs_11_, bf16[8,1024,512]{2,1,0:T(8,128)(2,1)} %refs_3_.1, ...), custom_call_target="tpu_custom_call" | custom-call | tf_op jit(solution)/shard_map/pallas_call | solution.py:74
  185.6 16.7 %shard_map.176 = (bf16[1024,768]{1,0:T(8,128)(2,1)}, bf16[1024,768]{1,0:T(8,128)(2,1)}) custom-call(s32[4]{0:T(128)} %pad_add_fusion.indices_ref.after_ref, bf16[272,1024]{1,0:T(8,128)(2,1)} %get-tuple-element.192.refs_0_, bf16[272,1024]{1,0:T(8,128)(2,1)} %copy-done.23, bf16[272,1024]{1,0:T(8,128)(2,1)} %copy-done.24, ...), custom_call_target="tpu_custom_call" | custom-call | tf_op jit(solution)/shard_map/pallas_call | solution.py:74
  216.1 26.3 %shard_map.178 = (f32[256,1024]{1,0:T(8,128)}, f32[256,1024]{1,0:T(8,128)}, bf16[256,1024]{1,0:T(8,128)(2,1)}, bf16[2,256,3200]{2,1,0:T(8,128)(2,1)}, bf16[2,256...) custom-call(s32[3]{0:T(128)} %pad_add_fusion.2.offsets_ref.out_offsets_ref, ...), custom_call_target="tpu_custom_call" | custom-call | tf_op jit(solution)/shard_map/pallas_call | solution.py:74
  258.7 33.7 %collective-permute-done.31.refs_1_ = bf16[1024,768]{1,0:T(8,128)(2,1)S(1)} collective-permute-done((bf16[1024,768]{1,0:T(8,128)(2,1)S(1)}, bf16[1024,768]{1,0:T(8,128)(2,1)S(1)}, u32[]{:S(2)}, u32[]{:S(2)}) %collective-permute-start.31) | collective-permute-done | bytes 1572896 | tf_op jit(solution)/shard_map/ppermute | solution.py:978
  305.5 35.8 %collective-permute-done.36.refs_0_ = bf16[1024,768]{1,0:T(8,128)(2,1)S(1)} collective-permute-done((bf16[1024,768]{1,0:T(8,128)(2,1)S(1)}, bf16[1024,768]{1,0:T(8,128)(2,1)S(1)}, u32[]{:S(2)}, u32[]{:S(2)}) %collective-permute-start.36) | collective-permute-done | bytes 1572896 | tf_op jit(solution)/shard_map/ppermute | solution.py:981
  355.2 5.4 %shard_map.182 = (f32[8,1024,1024]{2,1,0:T(8,128)}, f32[8,1024,512]{2,1,0:T(8,128)}) custom-call(s32[4]{0:T(128)S(1)} %get-tuple-element.351.experts_ref, bf16[2,1024,768]{2,1,0:T(8,128)(2,1)S(1)} %copy-done.8, bf16[2,1024,768]{2,1,0:T(8,128)(2,1)S(1)} %copy-done.10), custom_call_target="tpu_custom_call" | custom-call | tf_op jit(solution)/shard_map/pallas_call | solution.py:74
  360.6 16.1 %collective-permute-done.43.refs_7_ = bf16[2,256,1024]{2,1,0:T(8,128)(2,1)} collective-permute-done((bf16[2,256,1024]{2,1,0:T(8,128)(2,1)}, bf16[2,256,1024]{2,1,0:T(8,128)(2,1)}, u32[]{:S(2)}, u32[]{:S(2)}) %collective-permute-start.43) | collective-permute-done | bytes 1048608 | tf_op jit(solution)/shard_map/ppermute | solution.py:49
  376.7 10.6 %collective-permute-done.40.refs_0_ = bf16[1024,768]{1,0:T(8,128)(2,1)} collective-permute-done((bf16[1024,768]{1,0:T(8,128)(2,1)}, bf16[1024,768]{1,0:T(8,128)(2,1)}, u32[]{:S(2)}, u32[]{:S(2)}) %collective-permute-start.40) | collective-permute-done | bytes 1572896 | tf_op jit(solution)/shard_map/ppermute | solution.py:981
  397.6 7.0 %shard_map.184 = (f32[8,1024,1024]{2,1,0:T(8,128)}, f32[8,1024,512]{2,1,0:T(8,128)}) custom-call(s32[4]{0:T(128)S(1)} %get-tuple-element.351.experts_ref, bf16[2,1024,768]{2,1,0:T(8,128)(2,1)S(1)} %get-tuple-element.300.refs_0_, bf16[2,1024,768]{2,1,0:T(8,128)(2,1)} %collective-permute-done.49.refs_1_, ...), custom_call_target="tpu_custom_call", output_to_operand_aliasing={{0}: (3, {}), {1}: (4, {})} | custom-call | tf_op jit(solution)/shard_map/pallas_call | solution.py:74
  408.0 31.5 %collective-permute-done.47.refs_6_ = bf16[256,1024]{1,0:T(8,128)(2,1)S(1)} collective-permute-done((bf16[256,1024]{1,0:T(8,128)(2,1)S(1)}, bf16[256,1024]{1,0:T(8,128)(2,1)S(1)}, u32[]{:S(2)}, u32[]{:S(2)}) %collective-permute-start.47) | collective-permute-done | bytes 524320 | tf_op jit(solution)/shard_map/ppermute | solution.py:49
  443.8 5.4 %shard_map.187 = (f32[8,1024,1024]{2,1,0:T(8,128)}, f32[8,1024,512]{2,1,0:T(8,128)}) custom-call(s32[4]{0:T(128)S(1)} %get-tuple-element.350.experts_ref, bf16[2,1024,768]{2,1,0:T(8,128)(2,1)S(1)} %get-tuple-element.320.refs_0_, bf16[2,1024,768]{2,1,0:T(8,128)(2,1)S(1)} %collective-permute-done.52.refs_1_, ...), custom_call_target="tpu_custom_call", output_to_operand_aliasing={{0}: (3, {}), {1}: (4, {})} | custom-call | tf_op jit(solution)/shard_map/pallas_call | solution.py:74
  449.3 5.4 %shard_map.188 = (f32[8,1024,1024]{2,1,0:T(8,128)}, f32[8,1024,512]{2,1,0:T(8,128)}) custom-call(s32[4]{0:T(128)S(1)} %get-tuple-element.350.experts_ref, bf16[2,1024,768]{2,1,0:T(8,128)(2,1)S(1)} %get-tuple-element.326.refs_0_, bf16[2,1024,768]{2,1,0:T(8,128)(2,1)S(1)} %collective-permute-done.51.refs_1_, ...), custom_call_target="tpu_custom_call", output_to_operand_aliasing={{0}: (3, {}), {1}: (4, {})} | custom-call | tf_op jit(solution)/shard_map/pallas_call | solution.py:74
  454.7 25.3 %collective-permute-done.50.refs_1_ = bf16[256,3200]{1,0:T(8,128)(2,1)S(1)} collective-permute-done((bf16[256,3200]{1,0:T(8,128)(2,1)S(1)}, bf16[256,3200]{1,0:T(8,128)(2,1)S(1)}, u32[]{:S(2)}, u32[]{:S(2)}) %collective-permute-start.50) | collective-permute-done | bytes 1638432 | tf_op jit(solution)/shard_map/ppermute | solution.py:49
  485.8 5.6 %shard_map.190 = (f32[512,2048]{1,0:T(8,128)}, f32[512,1024]{1,0:T(8,128)}, f32[512,16]{1,0:T(8,128)}, f32[1,512]{1,0:T(1,128)}, f32[1,512]{1,0:T(1,128)}) custom-call(s32[2]{0:T(128)} %add_multiply_fusion.1.offsets_ref, bf16[1,256,3200]{2,1,0:T(8,128)(2,1)} %bitcast.39, bf16[1,256,3200]{2,1,0:T(8,128)(2,1)} %bitcast.41), custom_call_target="tpu_custom_call" | custom-call | tf_op jit(solution)/shard_map/pallas_call | solution.py:74
  (205 shorter events, 137.7 us)
Async XLA Ops:
  61.4 38.4 %collective-permute-start.18 = (bf16[4,256,1024]{2,1,0:T(8,128)(2,1)S(1)}, bf16[4,256,1024]{2,1,0:T(8,128)(2,1)}, u32[]{:S(2)}, u32[]{:S(2)}) collective-permute-start(bf16[4,256,1024]{2,1,0:T(8,128)(2,1)S(1)} %pad_maximum_fusion.refs_8_), channel_id=1, source_target_pairs={{0,2},{2,0},{1,3},{3,1},{4,6},{6,4},{5,7},{7,5},{8,10},{10,8},{9,1... | collective-permute-start | bytes 6291464 | tf_op jit(solution)/shard_map/ppermute | solution.py:49
  126.7 39.2 %collective-permute-start.20 = (bf16[1024,768]{1,0:T(8,128)(2,1)}, bf16[1024,768]{1,0:T(8,128)(2,1)S(1)}, u32[]{:S(2)}, u32[]{:S(2)}) collective-permute-start(bf16[1024,768]{1,0:T(8,128)(2,1)} %get-tuple-element.204.refs_0_), channel_id=1, source_target_pairs={{0,8},{24,16},{1,9},{25,17},{2,10},{26,18},{3,11},{27,19},{4,12},{... | collective-permute-start | bytes 4718600 | tf_op jit(solution)/shard_map/ppermute | solution.py:972
  158.8 43.4 %collective-permute-start.22 = (bf16[1024,768]{1,0:T(8,128)(2,1)}, bf16[1024,768]{1,0:T(8,128)(2,1)S(1)}, u32[]{:S(2)}, u32[]{:S(2)}) collective-permute-start(bf16[1024,768]{1,0:T(8,128)(2,1)} %get-tuple-element.216.refs_2_), channel_id=1, source_target_pairs={{0,8},{24,16},{1,9},{25,17},{2,10},{26,18},{3,11},{27,19},{4,12},{... | collective-permute-start | bytes 4718600 | tf_op jit(solution)/shard_map/ppermute | solution.py:972
  166.9 36.5 %collective-permute-start.21 = (bf16[1024,768]{1,0:T(8,128)(2,1)S(1)}, bf16[1024,768]{1,0:T(8,128)(2,1)S(1)}, u32[]{:S(2)}, u32[]{:S(2)}) collective-permute-start(bf16[1024,768]{1,0:T(8,128)(2,1)S(1)} %shard_map.174.refs_0_), channel_id=1, source_target_pairs={{8,16},{16,8},{9,17},{17,9},{10,18},{18,10},{11,19},{19,11},{12,20... | collective-permute-start | bytes 4718600 | tf_op jit(solution)/shard_map/ppermute | solution.py:975
  208.9 39.6 %collective-permute-start.23 = (bf16[1024,768]{1,0:T(8,128)(2,1)}, bf16[1024,768]{1,0:T(8,128)(2,1)S(1)}, u32[]{:S(2)}, u32[]{:S(2)}) collective-permute-start(bf16[1024,768]{1,0:T(8,128)(2,1)} %get-tuple-element.219), channel_id=1, source_target_pairs={{0,8},{8,0},{16,24},{24,16},{1,9},{9,1},{17,25},{25,17},{2,10},{10... | collective-permute-start | bytes 4718600 | tf_op jit(solution)/shard_map/ppermute | solution.py:978
  214.0 34.6 %collective-permute-start.24 = (bf16[1024,768]{1,0:T(8,128)(2,1)S(1)}, bf16[1024,768]{1,0:T(8,128)(2,1)}, u32[]{:S(2)}, u32[]{:S(2)}) collective-permute-start(bf16[1024,768]{1,0:T(8,128)(2,1)S(1)} %get-tuple-element.240.refs_3_), channel_id=1, source_target_pairs={{8,16},{16,8},{9,17},{17,9},{10,18},{18,10},{11,19},{19,11},{12,20... | collective-permute-start | bytes 4718600 | tf_op jit(solution)/shard_map/ppermute | solution.py:975
  254.5 39.0 %collective-permute-start.34 = (bf16[256,3200]{1,0:T(8,128)(2,1)S(1)}, bf16[256,3200]{1,0:T(8,128)(2,1)S(1)}, u32[]{:S(2)}, u32[]{:S(2)}) collective-permute-start(bf16[256,3200]{1,0:T(8,128)(2,1)S(1)} %get-tuple-element.252), channel_id=1, source_target_pairs={{0,1},{1,0},{2,3},{3,2},{4,5},{5,4},{6,7},{7,6},{8,9},{9,8},{10,11... | collective-permute-start | bytes 4915208 | tf_op jit(solution)/shard_map/ppermute | solution.py:49
  256.2 36.2 %collective-permute-start.31 = (bf16[1024,768]{1,0:T(8,128)(2,1)S(1)}, bf16[1024,768]{1,0:T(8,128)(2,1)S(1)}, u32[]{:S(2)}, u32[]{:S(2)}) collective-permute-start(bf16[1024,768]{1,0:T(8,128)(2,1)S(1)} %get-tuple-element.247), channel_id=1, source_target_pairs={{0,8},{8,0},{16,24},{24,16},{1,9},{9,1},{17,25},{25,17},{2,10},{10... | collective-permute-start | bytes 4718600 | tf_op jit(solution)/shard_map/ppermute | solution.py:978
  257.3 35.1 %collective-permute-start.32 = (bf16[1024,768]{1,0:T(8,128)(2,1)S(1)}, bf16[1024,768]{1,0:T(8,128)(2,1)S(1)}, u32[]{:S(2)}, u32[]{:S(2)}) collective-permute-start(bf16[1024,768]{1,0:T(8,128)(2,1)S(1)} %get-tuple-element.256.refs_3_), channel_id=1, source_target_pairs={{8,16},{16,8},{9,17},{17,9},{10,18},{18,10},{11,19},{19,11},{12,20... | collective-permute-start | bytes 4718600 | tf_op jit(solution)/shard_map/ppermute | solution.py:975
  258.1 35.4 %collective-permute-start.33 = (bf16[1024,768]{1,0:T(8,128)(2,1)S(1)}, bf16[1024,768]{1,0:T(8,128)(2,1)S(1)}, u32[]{:S(2)}, u32[]{:S(2)}) collective-permute-start(bf16[1024,768]{1,0:T(8,128)(2,1)S(1)} %get-tuple-element.258.refs_5_), channel_id=1, source_target_pairs={{0,4},{4,0},{1,5},{5,1},{2,6},{6,2},{3,7},{7,3},{8,12},{12,8},{9,1... | collective-permute-start | bytes 4718600 | tf_op jit(solution)/shard_map/ppermute | solution.py:49
  298.0 51.1 %collective-permute-start.44 = (bf16[2,1024,768]{2,1,0:T(8,128)(2,1)S(1)}, bf16[2,1024,768]{2,1,0:T(8,128)(2,1)S(1)}, u32[]{:S(2)}, u32[]{:S(2)}) collective-permute-start(bf16[2,1024,768]{2,1,0:T(8,128)(2,1)S(1)} %get-tuple-element.283.refs_0_), channel_id=1, source_target_pairs={{0,2},{2,0},{1,3},{3,1},{4,6},{6,4},{5,7},{7,5},{8,10},{10,8},{9,1... | collective-permute-start | bytes 9437192 | tf_op jit(solution)/shard_map/ppermute | solution.py:49
  298.0 43.5 %collective-permute-start.39 = (bf16[256,3200]{1,0:T(8,128)(2,1)S(1)}, bf16[256,3200]{1,0:T(8,128)(2,1)S(1)}, u32[]{:S(2)}, u32[]{:S(2)}) collective-permute-start(bf16[256,3200]{1,0:T(8,128)(2,1)S(1)} %get-tuple-element.277.refs_6_), channel_id=1, source_target_pairs={{0,8},{24,16},{1,9},{25,17},{2,10},{26,18},{3,11},{27,19},{4,12},{... | collective-permute-start | bytes 4915208 | tf_op jit(solution)/shard_map/ppermute | solution.py:972
  302.8 38.4 %collective-permute-start.36 = (bf16[1024,768]{1,0:T(8,128)(2,1)S(1)}, bf16[1024,768]{1,0:T(8,128)(2,1)S(1)}, u32[]{:S(2)}, u32[]{:S(2)}) collective-permute-start(bf16[1024,768]{1,0:T(8,128)(2,1)S(1)} %get-tuple-element.272.refs_1_), channel_id=1, source_target_pairs={{8,0},{16,24},{9,1},{17,25},{10,2},{18,26},{11,3},{19,27},{12,4},{... | collective-permute-start | bytes 4718600 | tf_op jit(solution)/shard_map/ppermute | solution.py:981
  304.1 37.1 %collective-permute-start.37 = (bf16[1024,768]{1,0:T(8,128)(2,1)S(1)}, bf16[1024,768]{1,0:T(8,128)(2,1)S(1)}, u32[]{:S(2)}, u32[]{:S(2)}) collective-permute-start(bf16[1024,768]{1,0:T(8,128)(2,1)S(1)} %get-tuple-element.273.refs_2_), channel_id=1, source_target_pairs={{8,16},{16,8},{9,17},{17,9},{10,18},{18,10},{11,19},{19,11},{12,20... | collective-permute-start | bytes 4718600 | tf_op jit(solution)/shard_map/ppermute | solution.py:975
  304.9 36.6 %collective-permute-start.38 = (bf16[1024,768]{1,0:T(8,128)(2,1)S(1)}, bf16[1024,768]{1,0:T(8,128)(2,1)S(1)}, u32[]{:S(2)}, u32[]{:S(2)}) collective-permute-start(bf16[1024,768]{1,0:T(8,128)(2,1)S(1)} %get-tuple-element.275.refs_4_), channel_id=1, source_target_pairs={{0,4},{4,0},{1,5},{5,1},{2,6},{6,2},{3,7},{7,3},{8,12},{12,8},{9,1... | collective-permute-start | bytes 4718600 | tf_op jit(solution)/shard_map/ppermute | solution.py:49
  345.4 41.9 %collective-permute-start.42 = (bf16[256,3200]{1,0:T(8,128)(2,1)}, bf16[256,3200]{1,0:T(8,128)(2,1)}, u32[]{:S(2)}, u32[]{:S(2)}) collective-permute-start(bf16[256,3200]{1,0:T(8,128)(2,1)} %get-tuple-element.291.refs_4_), channel_id=1, source_target_pairs={{8,16},{16,8},{9,17},{17,9},{10,18},{18,10},{11,19},{19,11},{12,20... | collective-permute-start | bytes 4915208 | tf_op jit(solution)/shard_map/ppermute | solution.py:975
  347.2 40.1 %collective-permute-start.40 = (bf16[1024,768]{1,0:T(8,128)(2,1)}, bf16[1024,768]{1,0:T(8,128)(2,1)}, u32[]{:S(2)}, u32[]{:S(2)}) collective-permute-start(bf16[1024,768]{1,0:T(8,128)(2,1)} %get-tuple-element.288.refs_1_), channel_id=1, source_target_pairs={{8,0},{16,24},{9,1},{17,25},{10,2},{18,26},{11,3},{19,27},{12,4},{... | collective-permute-start | bytes 4718600 | tf_op jit(solution)/shard_map/ppermute | solution.py:981
  348.5 38.8 %collective-permute-start.41 = (bf16[1024,768]{1,0:T(8,128)(2,1)}, bf16[1024,768]{1,0:T(8,128)(2,1)}, u32[]{:S(2)}, u32[]{:S(2)}) collective-permute-start(bf16[1024,768]{1,0:T(8,128)(2,1)} %get-tuple-element.289.refs_2_), channel_id=1, source_target_pairs={{0,4},{4,0},{1,5},{5,1},{2,6},{6,2},{3,7},{7,3},{8,12},{12,8},{9,1... | collective-permute-start | bytes 4718600 | tf_op jit(solution)/shard_map/ppermute | solution.py:49
  349.1 48.4 %collective-permute-start.49 = (bf16[2,1024,768]{2,1,0:T(8,128)(2,1)S(1)}, bf16[2,1024,768]{2,1,0:T(8,128)(2,1)}, u32[]{:S(2)}, u32[]{:S(2)}) collective-permute-start(bf16[2,1024,768]{2,1,0:T(8,128)(2,1)S(1)} %get-tuple-element.300.refs_0_), channel_id=1, source_target_pairs={{0,2},{2,0},{1,3},{3,1},{4,6},{6,4},{5,7},{7,5},{8,10},{10,8},{9,1... | collective-permute-start | bytes 9437192 | tf_op jit(solution)/shard_map/ppermute | solution.py:49
  392.5 47.0 %collective-permute-start.46 = (bf16[256,3200]{1,0:T(8,128)(2,1)S(1)}, bf16[256,3200]{1,0:T(8,128)(2,1)S(1)}, u32[]{:S(2)}, u32[]{:S(2)}) collective-permute-start(bf16[256,3200]{1,0:T(8,128)(2,1)S(1)} %get-tuple-element.309.refs_3_), channel_id=1, source_target_pairs={{8,0},{16,24},{9,1},{17,25},{10,2},{18,26},{11,3},{19,27},{12,4},{... | collective-permute-start | bytes 4915208 | tf_op jit(solution)/shard_map/ppermute | solution.py:981
  394.1 45.5 %collective-permute-start.45 = (bf16[1024,768]{1,0:T(8,128)(2,1)S(1)}, bf16[1024,768]{1,0:T(8,128)(2,1)S(1)}, u32[]{:S(2)}, u32[]{:S(2)}) collective-permute-start(bf16[1024,768]{1,0:T(8,128)(2,1)S(1)} %get-tuple-element.306.refs_0_), channel_id=1, source_target_pairs={{0,4},{4,0},{1,5},{5,1},{2,6},{6,2},{3,7},{7,3},{8,12},{12,8},{9,1... | collective-permute-start | bytes 4718600 | tf_op jit(solution)/shard_map/ppermute | solution.py:49
  396.0 43.6 %collective-permute-start.47 = (bf16[256,1024]{1,0:T(8,128)(2,1)S(1)}, bf16[256,1024]{1,0:T(8,128)(2,1)S(1)}, u32[]{:S(2)}, u32[]{:S(2)}) collective-permute-start(bf16[256,1024]{1,0:T(8,128)(2,1)S(1)} %get-tuple-element.298), channel_id=1, source_target_pairs={{0,4},{4,0},{1,5},{5,1},{2,6},{6,2},{3,7},{7,3},{8,12},{12,8},{9,1... | collective-permute-start | bytes 1572872 | tf_op jit(solution)/shard_map/ppermute | solution.py:49
  397.5 46.3 %collective-permute-start.52 = (bf16[2,1024,768]{2,1,0:T(8,128)(2,1)S(1)}, bf16[2,1024,768]{2,1,0:T(8,128)(2,1)S(1)}, u32[]{:S(2)}, u32[]{:S(2)}) collective-permute-start(bf16[2,1024,768]{2,1,0:T(8,128)(2,1)S(1)} %get-tuple-element.320.refs_0_), channel_id=1, source_target_pairs={{0,2},{2,0},{1,3},{3,1},{4,6},{6,4},{5,7},{7,5},{8,10},{10,8},{9,1... | collective-permute-start | bytes 9437192 | tf_op jit(solution)/shard_map/ppermute | solution.py:49
  441.8 38.2 %collective-permute-start.50 = (bf16[256,3200]{1,0:T(8,128)(2,1)S(1)}, bf16[256,3200]{1,0:T(8,128)(2,1)S(1)}, u32[]{:S(2)}, u32[]{:S(2)}) collective-permute-start(bf16[256,3200]{1,0:T(8,128)(2,1)S(1)} %get-tuple-element.332.refs_0_), channel_id=1, source_target_pairs={{0,4},{4,0},{1,5},{5,1},{2,6},{6,2},{3,7},{7,3},{8,12},{12,8},{9,1... | collective-permute-start | bytes 4915208 | tf_op jit(solution)/shard_map/ppermute | solution.py:49
  (66 other events, 1009.5 us)

commit v5 on v4

--- a/solution.py
+++ b/solution.py
@@ -128,9 +128,16 @@
     def kernel(offsets_ref, prev_ref, own_ref, gain_ref, cos_ref, sin_ref, *rest):
         piece_refs, (q_ref, kv_ref, in_ref, weight, sems) = rest[:count], rest[count:]
         copies = load_rows(piece_refs, offsets_ref, weight, sems)
+        deep = 64
         for i, ref in enumerate((prev_ref, own_ref)):
-            normed, _ = normalize(ref[...].astype(f32))
-            in_ref[i * length : (i + 1) * length, :] = (normed * gain_ref[...]).astype(bf16)
+
+            def rows(r, carry):
+                normed, _ = normalize(ref[pl.ds(pl.multiple_of(r * deep, deep), deep), :].astype(f32))
+                at = pl.ds(pl.multiple_of(i * length + r * deep, deep), deep)
+                in_ref[at, :] = (normed * gain_ref[...]).astype(bf16)
+                return carry
+
+            lax.fori_loop(0, length // deep, rows, 0)
         for copy in copies:
             copy.wait()
         values = dot(in_ref[length:, :], weight[:, :QW])
@@ -187,8 +194,8 @@
             vals = kv_ref[:, pl.ds(KVW + at, PAIR)].astype(f32)
             for t in range(2):
                 place = pl.multiple_of((2 * jj + t) * PAIR, PAIR)
-                both = two_rows(q_ref[:, pl.ds(place, PAIR)].astype(f32)).astype(bf16)
-                scores = dot(both, doubled(keys, t).astype(bf16), ((1,), (1,))) * score_scale + bias
+                both = (two_rows(q_ref[:, pl.ds(place, PAIR)].astype(f32)) * score_scale).astype(bf16)
+                scores = dot(both, doubled(keys, t).astype(bf16), ((1,), (1,))) + bias
                 largest = jnp.max(scores, -1, keepdims=True)
                 exponent = jnp.exp(scores - largest)
                 totals = jnp.sum(exponent, -1, keepdims=True)
@@ -248,17 +255,55 @@
     )
 
 
-def write_chunks(out_refs, at, values):
-    part = F // len(out_refs)
-    deep = 128
-
-    def rows(r, carry):
-        for c, out_ref in enumerate(out_refs):
-            piece = values[pl.ds(pl.multiple_of(r * deep, deep), deep), c * part : (c + 1) * part]
-            out_ref[pl.ds(pl.multiple_of(r * deep, deep), deep), at * part : (at + 1) * part] = piece.astype(bf16)
-        return carry
-
-    lax.fori_loop(0, D // deep, rows, 0)
+def add_weights(i, steps, lefts, rights, which, chunks, accs, out_refs):
+    part = F // chunks
+    clear(i, accs)
+    for c, acc, out_ref in zip(which, accs, out_refs):
+        for p, (left, right) in enumerate(zip(lefts, rights)):
+            at = slice(p * part, (p + 1) * part)
+            acc[:, at] += dot(left, right[:, c * part : (c + 1) * part], ((0,), (0,)))
+
+        @pl.when(i == steps - 1)
+        def _():
+            deep = 128
+
+            def rows(r, carry):
+                at = pl.ds(pl.multiple_of(r * deep, deep), deep)
+                out_ref[at, :] = acc[at, :].astype(bf16)
+                return carry
+
+            lax.fori_loop(0, D // deep, rows, 0)
+
+
+def load_blocks(i, step, row_refs, grad_refs, both_ref, grad_ref, table_ref, sems):
+    length, each = row_refs[0].shape[0] - EXTRA, grad_refs[0].shape[0]
+
+    def copies(j, row_ref, block_ref):
+        at = pl.ds(pl.multiple_of(j * length, length), length)
+        out = [
+            pltpu.make_async_copy(row_ref.at[:length, :], both_ref.at[at, :], sems.at[j, 0]),
+            pltpu.make_async_copy(block_ref, grad_ref.at[at, :], sems.at[j, 1]),
+        ]
+        if table_ref is not None:
+            out.append(pltpu.make_async_copy(row_ref.at[length:, : 2 * length], table_ref.at[j], sems.at[j, 2]))
+        return out
+
+    @pl.when(i == 0)
+    def _():
+        for j, row_ref in enumerate(row_refs):
+            for copy in copies(j, row_ref, grad_refs[j // each].at[j % each]):
+                copy.start()
+
+    for b in range(step):
+        for copy in copies(i * step + b, row_refs[0], grad_refs[0].at[0]):
+            copy.wait()
+    at = pl.ds(pl.multiple_of(i * step * length, step * length), step * length)
+    return both_ref[at, :], grad_ref[at, :]
+
+
+def gate_table(pair):
+    length = pair.shape[1] // 2
+    return pair[:, :length].astype(f32) + pair[:, length:].astype(f32)
 
 
 def clear(i, accs):
@@ -274,7 +319,7 @@
         lax.fori_loop(0, D // deep, rows, 0)
 
 
-def expert(rows, grads, w_gate_up, w_down, index, chunks):
+def expert(rows, grads, w_gate_up, w_down, index, chunks, which):
     sources, blocks, tall = len(grads), len(rows), rows[0].shape[0]
     length = tall - EXTRA
     step = 2
@@ -284,28 +329,12 @@
     def kernel(index_ref, *refs):
         row_refs, grad_refs, refs = refs[:blocks], refs[blocks : blocks + sources], refs[blocks + sources :]
         gate_up_ref, down_ref, dgu_ref, hid_ref, sum_ref = refs[:5]
-        out_refs, (both_ref, grad_ref, table_ref, *accs) = refs[5 : 5 + chunks], refs[5 + chunks :]
+        out_refs, (both_ref, grad_ref, table_ref, sems, *accs) = refs[5 : 5 + len(which)], refs[5 + len(which) :]
         i = pl.program_id(0)
-        for source, source_ref in enumerate(grad_refs):
-
-            @pl.when((i >= source * turns) & (i < (source + 1) * turns))
-            def _():
-                for b in range(step):
-                    grad_ref[b * length : (b + 1) * length, :] = source_ref[b]
-
-        for j, row_ref in enumerate(row_refs):
-            b = j % step
-
-            @pl.when(i == j // step)
-            def _():
-                both_ref[b * length : (b + 1) * length, :] = row_ref[:length, :]
-                high, low = row_ref[length:, :length], row_ref[length:, length : 2 * length]
-                table_ref[b] = high.astype(f32) + low.astype(f32)
-
-        both, grad = both_ref[...], grad_ref[...]
+        both, grad = load_blocks(i, step, row_refs, grad_refs, both_ref, grad_ref, table_ref, sems)
         columns = []
         for b in range(step):
-            table = table_ref[b]
+            table = gate_table(table_ref[i * step + b])
             mine = lax.broadcasted_iota(jnp.int32, table.shape, 0) == index_ref[1]
             row = jnp.sum(jnp.where(mine, table, 0.0), 0, keepdims=True)
             columns.append(jnp.broadcast_to(row, (128, length)).T[:, :1])
@@ -327,15 +356,7 @@
             dgu_ref[b, :, F:] = grad_up[at]
             hid_ref[b] = gated[at]
             sum_ref[b] = jnp.broadcast_to(sums[at], (length, 128)).T[:8]
-        if not chunks:
-            return
-        clear(i, accs)
-        for p, (left, right) in enumerate(((both, grad_gate), (both, grad_up), (grad, gated))):
-            accs[p][...] += dot(left, right, ((0,), (0,)))
-
-            @pl.when(i == steps - 1)
-            def _():
-                write_chunks(out_refs, p, accs[p])
+        add_weights(i, steps, (both, both, grad), (grad_gate, grad_up, gated), which, chunks, accs, out_refs)
 
     def block(*shape):
         return pl.BlockSpec((step,) + shape, lambda i, index: (i,) + (0,) * len(shape))
@@ -351,20 +372,20 @@
 
     shapes = [array((blocks, length, 2 * F), bf16), array((blocks, length, F), bf16), array((blocks, 8, length), f32)]
     scratch = [
-        pltpu.VMEM((step * length, D), bf16),
-        pltpu.VMEM((step * length, D), bf16),
-        pltpu.VMEM((step, EXTRA, length), f32),
+        pltpu.VMEM((blocks * length, D), bf16),
+        pltpu.VMEM((blocks * length, D), bf16),
+        pltpu.VMEM((blocks, EXTRA, 2 * length), bf16),
+        pltpu.SemaphoreType.DMA((blocks, 3)),
     ]
     return call(
         kernel,
-        shapes + [array((D, 3 * F // chunks), bf16)] * chunks if chunks else shapes,
-        [whole((tall, D))] * blocks
-        + [source_block(s, length, D) for s in range(sources)]
+        shapes + [array((D, 3 * F // chunks), bf16)] * len(which),
+        [STAY] * (blocks + sources)
         + [weight(D, 2 * F), weight(D, F)],
         (index, *rows, *grads, w_gate_up, w_down),
         out_specs=[block(length, 2 * F), block(length, F), block(8, length)]
-        + [pl.BlockSpec((D, 3 * F // chunks), lambda i, index: (0, 0)) for _ in range(chunks)],
-        scratch=scratch + ([pltpu.VMEM((D, F), f32)] * 3 if chunks else []),
+        + [pl.BlockSpec((D, 3 * F // chunks), lambda i, index: (0, 0)) for _ in which],
+        scratch=scratch + [pltpu.VMEM((D, 3 * F // chunks), f32)] * len(which),
         grid=(steps,),
         prefetch=1,
     )
@@ -388,26 +409,10 @@
         row_refs, grad_refs, refs = refs[:blocks], refs[blocks : blocks + sources], refs[blocks + sources :]
         gate_up_ref, down_ref, refs = refs[0], refs[1], refs[2:]
         earlier_refs, weight_refs, sum_refs, refs = refs[:others], refs[others : 2 * others], refs[2 * others : 3 * others], refs[3 * others :]
-        dgu_ref, hid_ref, out_refs, (both_ref, grad_ref, table_ref) = refs[0], refs[1], refs[2 : 2 + sources], refs[2 + sources :]
+        dgu_ref, hid_ref, out_refs, (both_ref, grad_ref, table_ref, sems) = refs[0], refs[1], refs[2 : 2 + sources], refs[2 + sources :]
         i = pl.program_id(0)
-        for source, source_ref in enumerate(grad_refs):
-
-            @pl.when((i >= source * turns) & (i < (source + 1) * turns))
-            def _():
-                for b in range(step):
-                    grad_ref[b * length : (b + 1) * length, :] = source_ref[b]
-
-        for j, row_ref in enumerate(row_refs):
-            b = j % step
-
-            @pl.when(i == j // step)
-            def _():
-                both_ref[b * length : (b + 1) * length, :] = row_ref[:length, :]
-                high, low = row_ref[length:, :length], row_ref[length:, length : 2 * length]
-                table_ref[b] = high.astype(f32) + low.astype(f32)
-
-        both, grad = both_ref[...], grad_ref[...]
-        gate = jnp.concatenate([gate_column(table_ref[b], indices_ref[2 * others + 1]) for b in range(step)], 0)
+        both, grad = load_blocks(i, step, row_refs, grad_refs, both_ref, grad_ref, table_ref, sems)
+        gate = jnp.concatenate([gate_column(gate_table(table_ref[i * step + b]), indices_ref[2 * others + 1]) for b in range(step)], 0)
         gate_up = dot(both, gate_up_ref[0])
         gate_part, up_part = gate_up[:, :F], gate_up[:, F:]
         sigmoid_g = jax.nn.sigmoid(gate_part)
@@ -460,8 +465,7 @@
         kernel,
         [array((blocks, length, 2 * F), bf16), array((blocks, length, F), bf16)]
         + [array((blocks // sources, tall, D), bf16)] * sources,
-        [whole((tall, D))] * blocks
-        + [source_block(s, length, D) for s in range(sources)]
+        [STAY] * (blocks + sources)
         + [weight(others, D, 2 * F), weight(others, D, F)]
         + [block(length, 2 * F)] * others
         + [weight(e, D, 2 * F) for e in range(others)]
@@ -469,16 +473,17 @@
         (indices, *rows, *grads, w_gate_up, w_down, *earlier, *[w_gate_up] * others, *sums),
         out_specs=[block(length, 2 * F), block(length, F)] + [source_block(s, tall, D) for s in range(sources)],
         scratch=[
-            pltpu.VMEM((step * length, D), bf16),
-            pltpu.VMEM((step * length, D), bf16),
-            pltpu.VMEM((step, EXTRA, length), f32),
+            pltpu.VMEM((blocks * length, D), bf16),
+            pltpu.VMEM((blocks * length, D), bf16),
+            pltpu.VMEM((blocks, EXTRA, 2 * length), bf16),
+            pltpu.SemaphoreType.DMA((blocks, 3)),
         ],
         grid=(steps,),
         prefetch=1,
     )
 
 
-def weight_grads(rows, grads, grad_gate_up, hidden, chunks, after):
+def weight_grads(rows, grads, grad_gate_up, hidden, chunks, which, after):
     sources, blocks, tall = len(grads), len(rows), rows[0].shape[0]
     length = tall - EXTRA
     step = 2
@@ -487,34 +492,14 @@
 
     def kernel(after_ref, *refs):
         row_refs, grad_refs, refs = refs[:blocks], refs[blocks : blocks + sources], refs[blocks + sources :]
-        dgu_ref, hid_ref, out_refs = refs[0], refs[1], refs[2 : 2 + chunks]
-        both_ref, grad_ref, *accs = refs[2 + chunks :]
+        dgu_ref, hid_ref, out_refs = refs[0], refs[1], refs[2 : 2 + len(which)]
+        both_ref, grad_ref, sems, *accs = refs[2 + len(which) :]
         i = pl.program_id(0)
-        for source, source_ref in enumerate(grad_refs):
-
-            @pl.when((i >= source * turns) & (i < (source + 1) * turns))
-            def _():
-                for b in range(step):
-                    grad_ref[b * length : (b + 1) * length, :] = source_ref[b]
-
-        for j, row_ref in enumerate(row_refs):
-            b = j % step
-
-            @pl.when(i == j // step)
-            def _():
-                both_ref[b * length : (b + 1) * length, :] = row_ref[:length, :]
-
-        both, grad = both_ref[...], grad_ref[...]
+        both, grad = load_blocks(i, step, row_refs, grad_refs, both_ref, grad_ref, None, sems)
         grad_gate = jnp.concatenate([dgu_ref[b, :, :F] for b in range(step)], 0)
         grad_up = jnp.concatenate([dgu_ref[b, :, F:] for b in range(step)], 0)
         gated = jnp.concatenate([hid_ref[b] for b in range(step)], 0)
-        clear(i, accs)
-        for p, (left, right) in enumerate(((both, grad_gate), (both, grad_up), (grad, gated))):
-            accs[p][...] += dot(left, right, ((0,), (0,)))
-
-            @pl.when(i == steps - 1)
-            def _():
-                write_chunks(out_refs, p, accs[p])
+        add_weights(i, steps, (both, both, grad), (grad_gate, grad_up, gated), which, chunks, accs, out_refs)
 
     def block(*shape):
         return pl.BlockSpec((step,) + shape, lambda i, after: (i,) + (0,) * len(shape))
@@ -527,13 +512,14 @@
 
     return call(
         kernel,
-        [array((D, 3 * F // chunks), bf16)] * chunks,
-        [whole((tall, D))] * blocks
-        + [source_block(s, length, D) for s in range(sources)]
+        [array((D, 3 * F // chunks), bf16)] * len(which),
+        [STAY] * (blocks + sources)
         + [block(length, 2 * F), block(length, F)],
         (after, *rows, *grads, grad_gate_up, hidden),
-        out_specs=[pl.BlockSpec((D, 3 * F // chunks), lambda i, after: (0, 0)) for _ in range(chunks)],
-        scratch=[pltpu.VMEM((step * length, D), bf16)] * 2 + [pltpu.VMEM((D, F), f32)] * 3,
+        out_specs=[pl.BlockSpec((D, 3 * F // chunks), lambda i, after: (0, 0)) for _ in which],
+        scratch=[pltpu.VMEM((blocks * length, D), bf16)] * 2
+        + [pltpu.SemaphoreType.DMA((blocks, 3))]
+        + [pltpu.VMEM((D, 3 * F // chunks), f32)] * len(which),
         grid=(steps,),
         prefetch=1,
     )
@@ -636,13 +622,13 @@
             key_grads, val_grads = [], []
             for t in range(2):
                 place = pl.multiple_of((2 * jj + t) * PAIR, PAIR)
-                both = two_rows(q_ref[:, pl.ds(place, PAIR)].astype(f32)).astype(bf16)
+                both = (two_rows(q_ref[:, pl.ds(place, PAIR)].astype(f32)) * score_scale).astype(bf16)
                 outs = two_rows(gatt_ref[:, pl.ds(place, PAIR)].astype(f32)).astype(bf16)
                 key = doubled(keys, t).astype(bf16)
                 val = doubled(vals, t).astype(bf16)
                 own = lanes(lse_ref.shape) == 2 * jj + t
                 log_total = jnp.sum(jnp.where(own, lse_ref[...], 0.0), -1, keepdims=True)
-                scores = dot(both, key, ((1,), (1,))) * score_scale + bias
+                scores = dot(both, key, ((1,), (1,))) + bias
                 probs = jnp.exp(scores - log_total)
                 grad_probs = dot(outs, val, ((1,), (1,)))
                 inner = jnp.sum(probs * grad_probs, -1, keepdims=True)
@@ -651,7 +637,7 @@
                 low = lanes((length, PAIR)) < HEAD_DIM
                 grad_query = jnp.where(low, grad_query[:length], grad_query[length:])
                 dq_ref[:, pl.ds(place, PAIR)] = back(grad_query, cos_own, sin_own)
-                key_grad = dot(grad_scores, both, ((0,), (0,))) * score_scale
+                key_grad = dot(grad_scores, both, ((0,), (0,)))
                 val_grad = dot(probs.astype(bf16), outs, ((0,), (0,)))
                 key_grads.append(key_grad + pltpu.roll(key_grad, HEAD_DIM, 1))
                 val_grads.append(val_grad + pltpu.roll(val_grad, HEAD_DIM, 1))
@@ -720,9 +706,15 @@
 
 def first_back(grad_sum, grad_residual, hidden_own, gain):
     def kernel(sum_ref, res_ref, hid_ref, gain_ref, out_ref):
-        normed, inverse = normalize(hid_ref[...].astype(f32))
-        grad = sum_ref[...] * gain_ref[...]
-        out_ref[...] = res_ref[...] + norm_back(normed, inverse, grad)
+        deep = 32
+
+        def rows(r, carry):
+            at = pl.ds(pl.multiple_of(r * deep, deep), deep)
+            normed, inverse = normalize(hid_ref[at, :].astype(f32))
+            out_ref[at, :] = res_ref[at, :] + norm_back(normed, inverse, sum_ref[at, :] * gain_ref[...])
+            return carry
+
+        lax.fori_loop(0, out_ref.shape[0] // deep, rows, 0)
 
     operands = (grad_sum, grad_residual, hidden_own, gain)
     return call(kernel, [array(grad_sum.shape, f32)], [whole(v.shape) for v in operands], operands, vmem=16 * 1024 * 1024)[0]
@@ -781,7 +773,14 @@
         out_refs, router_ref, ffn_ref, attn_ref, values_ref, rest_ref, sems = refs[:2], *refs[2:]
         copies = []
         for i, source in enumerate([ref.at[i] for ref in source_refs for i in range(ref.shape[0])]):
-            values_ref[i] = source[...].astype(f32)
+            some = 32
+
+            def rows_of(r, carry):
+                place = pl.ds(pl.multiple_of(r * some, some), some)
+                values_ref[i, place, :] = source[place, :].astype(f32)
+                return carry
+
+            lax.fori_loop(0, deep // some, rows_of, 0)
             at = pl.multiple_of(offsets_ref[i], 8)
             start = 0
             for p, (out_ref, width) in enumerate(zip(out_refs, widths)):
@@ -811,9 +810,7 @@
     )
 
 
-def post(function, flags, arrays, outs):
-    parts = 8
-
+def post(function, flags, arrays, outs, parts=8):
     def kernel(flags_ref, *refs):
         ins, results = refs[: len(arrays)], refs[len(arrays) :]
         scalars = [flags_ref[i] for i in range(flags.shape[0])]
@@ -1043,14 +1040,14 @@
     if (line, side, cores, shards, count) != (4, 2, 2, 2, 2):
         grads_gu, hiddens, sums, chunks = [], [], [], []
         for e in range(count - 1):
-            grad_gu, hidden, total, *parts = expert(rows_near, grads_near, w_gate_up, w_down, indices[e], CHUNKS)
+            grad_gu, hidden, total, *parts = expert(rows_near, grads_near, w_gate_up, w_down, indices[e], CHUNKS, range(CHUNKS))
             grads_gu.append(grad_gu)
             hiddens.append(hidden)
             sums.append(total)
             chunks.append(parts)
         grad_gu, hidden, *blocks = last_expert(rows_near, grads_near, w_gate_up, w_down, both, grads_gu, sums)
         hiddens.append(hidden)
-        chunks.append(weight_grads(rows_near, grads_near, grad_gu, hidden, CHUNKS, both))
+        chunks.append(weight_grads(rows_near, grads_near, grad_gu, hidden, CHUNKS, range(CHUNKS), both))
         terms = row_terms(hiddens, w_down, both, cores)
         returned = send_back([v for v in add_up(blocks[0], [other_core(g, -c % cores) for c, g in enumerate(blocks[1:], 1)])])
         mixed = send_back([v for v in add_up(terms[0], [other_core(g, -c % cores) for c, g in enumerate(terms[1:], 1)])])
@@ -1085,20 +1082,30 @@
             layer_out, grad_in, qkv_sum, out_sum, router_sum, attn_sum[0], ffn_sum[0], outs[0], outs[1],
         )
 
-    gu_0, hid_0, sum_0, *parts_0 = run(lambda i: expert(rows_near, grads_near, w_gate_up, w_down, i, CHUNKS), indices[0])
+    gu_0, hid_0, sum_0, *parts_0 = run(lambda i: expert(rows_near, grads_near, w_gate_up, w_down, i, CHUNKS, (0,)), indices[0])
     chunk = parts_0[0].shape
     two = (2,) + chunk
     in_0 = go_in(parts_0[0])
+    parts_0 += run(lambda i: weight_grads(rows_near, grads_near, gu_0, hid_0, CHUNKS, (1,), i), both)
     gu_1, hid_1, first_half, other_half = run(
         lambda i: last_expert(rows_near, grads_near, w_gate_up, w_down, i, [gu_0], [sum_0]), both
     )
     far = [other_core(other_half)]
     (half_0,) = steps(lambda flag, raw, got: (f(raw) + f(got),), [chunk], parts_0[0], in_0)
     middle_0, in_1 = cross(half_0), go_in(parts_0[1])
+    tall = first_half.shape[1]
+
+    def block_sums(flag, first, other):
+        total = f(first) + f(other)
+        return tuple(total[i] for i in range(len(near)))
+
+    blocks = run(
+        lambda first, other: post(lambda *v: block_sums(*v), flags, (first, other), [array((tall, D), bf16)] * len(near), tall // 16),
+        first_half, far[0],
+    )
+    returned = send_back(blocks)
     mixed, mixed_other = run(lambda i: row_terms([hid_0, hid_1], w_down, i, cores), both)
-    blocks = run(near_sums, first_half, far)
-    returned = send_back(blocks)
-    parts_1 = run(lambda i: weight_grads(rows_near, grads_near, gu_1, hid_1, CHUNKS, i), both)
+    parts_1 = run(lambda i: weight_grads(rows_near, grads_near, gu_1, hid_1, CHUNKS, range(CHUNKS), i), both)
 
     def step_1(flag, half, middle, own, got, raw):
         total = f(half) + f(middle)

time: 503 us -> 493 us (0.980); the launches traced: 493 us -> 492 us
  Pallas kernels: 181 us -> 191 us
  waiting for transfers between devices: 219 us -> 213 us
    ppermute x3, waiting for transfers between devices: 5.74 us -> 0.01 us  [go_in(): return lax.ppermute(raw, 'line', [(0, 1), (3, 2)])]
    pallas_call x8 -> x9, Pallas kernels: 23.3 us -> 28.8 us  [post(): pl.pallas_call(kernel, out_shape=list(outs), in_specs=[SCALARS] + [near]...]
    pallas_call x14 -> x15, Pallas kernels: 157 us -> 162 us  [call(): pl.pallas_call(kernel, out_shape=list(out_shape), grid_spec=spec, input_o...]
    unnamed x74 -> x78, local copies, waits for them, and re-layouts: 17.1 us -> 17.9 us
  transfers between devices with their start and end apart: 54 -> 54, of which waited for: 23 -> 23; matrix products, arithmetic and copies ran while one was open for 3% -> 2% of each run, Pallas kernels for 29% -> 33%
where the time goes in v5:
time: 493 us; the launch traced here: 492 us
  waiting for transfers between devices  213 us (43%)
  Pallas kernels  191 us (39%)
  starting transfers between devices  56.7 us (12%)
  local copies, waits for them, and re-layouts  22.8 us (5%)
  other arithmetic  7.27 us (1%)
    pallas_call x15, Pallas kernels, call(): pl.pallas_call(kernel, out_shape=list(out_shape), grid_spec=spec, input_o...  162 us
    ppermute x39, waiting for transfers between devices, turn(): return lax.ppermute(value, axes, pairs)  123 us
    ppermute x3, waiting for transfers between devices, go_out(): return lax.ppermute(total, 'line', [(1, 0), (2, 3)])  46.3 us
    ppermute x2, waiting for transfers between devices, in_and_out(): return lax.ppermute(sent, 'line', [(0, 1), (1, 0), (2, 3), (3, 2)])  33.5 us
    pallas_call x9, Pallas kernels, post(): pl.pallas_call(kernel, out_shape=list(outs), in_specs=[SCALARS] + [near]...  28.8 us
    ppermute x39, starting transfers between devices, turn(): return lax.ppermute(value, axes, pairs)  28.2 us
    unnamed x78, local copies, waits for them, and re-layouts  17.9 us
    ppermute x3, starting transfers between devices, go_in(): return lax.ppermute(raw, 'line', [(0, 1), (3, 2)])  11.6 us
  transfers between devices with their start and end apart: 54, of which 23 were waited for; matrix products, arithmetic and copies ran while one was open for 2% of the time, Pallas kernels for 33%

profile of v5, /device:TPU:0, one launch (start us, length us, event | category | flops | bytes accessed | tf_op | source)
XLA Modules:
  0.0 491.7 jit_solution(8539208176340567182)
XLA Ops:
  8.3 9.0 %collective-permute-done.1.rest_1_.rest_23_ = bf16[128,2048]{1,0:T(8,128)(2,1)S(1)} collective-permute-done((bf16[128,2048]{1,0:T(8,128)(2,1)S(1)}, bf16[128,2048]{1,0:T(8,128)(2,1)S(1)}, u32[]{:S(2)}, u32[]{:S(2)}) %collective-permute-start.1) | collective-permute-done | bytes 524320 | tf_op jit(solution)/shard_map/ppermute | solution.py:49
  22.1 6.5 %collective-permute-done.prev_ref.rest_16_ = bf16[256,1024]{1,0:T(8,128)(2,1)S(1)} collective-permute-done((bf16[256,1024]{1,0:T(8,128)(2,1)}, bf16[256,1024]{1,0:T(8,128)(2,1)S(1)}, u32[]{:S(2)}, u32[]{:S(2)}) %collective-permute-start) | collective-permute-done | bytes 524320 | tf_op jit(solution)/shard_map/ppermute | solution.py:921
  43.3 6.6 %shard_map.169 = (bf16[256,1024]{1,0:T(8,128)(2,1)}, bf16[512,1024]{1,0:T(8,128)(2,1)}, bf16[512,1024]{1,0:T(8,128)(2,1)}) custom-call(s32[5]{0:T(128)} %stack.111.offsets_ref.qkv_offsets_ref, bf16[256,1024]{1,0:T(8,128)(2,1)} %copy-done.32, bf16[256,1024]{1,0:T(8,128)(2,1)} %hid_ref.1, f32[1,1024]{1,0:T(1,128)} %get-tuple-element.361.gain_ref, ...), custom_call_target="tpu_custom_call" | custom-call | tf_op jit(solution)/shard_map/pallas_call | solution.py:74
  50.4 8.6 %shard_map.170 = (bf16[256,1024]{1,0:T(8,128)(2,1)}, f32[512,128]{1,0:T(8,128)}) custom-call(s32[1]{0:T(128)} %bitcast.15.flag_ref, bf16[256,1024]{1,0:T(8,128)(2,1)} %get-tuple-element.184.q_ref.rest_10_, bf16[512,1024]{1,0:T(8,128)(2,1)} %get-tuple-element.185.kv_ref.rest_11_), custom_call_target="tpu_custom_call" | custom-call | tf_op jit(solution)/shard_map/pallas_call | solution.py:74
  63.9 5.2 %shard_map.171 = (f32[256,1024]{1,0:T(8,128)}, f32[256,128]{1,0:T(8,128)}, bf16[272,1024]{1,0:T(8,128)(2,1)}) custom-call(s32[3]{0:T(128)} %pad_add_fusion.2.offsets_ref.out_offsets_ref, bf16[256,1024]{1,0:T(8,128)(2,1)} %get-tuple-element.192.att_ref.rest_18_, bf16[256,1024]{1,0:T(8,128)(2,1)} %hid_ref.1, f32[1,1024]{1,0:T(1,128)} %get-tuple-element.360.gain_ref.rest_8_, ...), custom_call_target="tpu_custom_call" | custom-call | tf_op jit(solution)/shard_map/pallas_call | solution.py:74
  72.7 12.2 %collective-permute-done.11.refs_1_ = bf16[272,1024]{1,0:T(8,128)(2,1)S(1)} collective-permute-done((bf16[272,1024]{1,0:T(8,128)(2,1)}, bf16[272,1024]{1,0:T(8,128)(2,1)S(1)}, u32[]{:S(2)}, u32[]{:S(2)}) %collective-permute-start.11) | collective-permute-done | bytes 557088 | tf_op jit(solution)/shard_map/ppermute | solution.py:49
  84.9 11.8 %collective-permute-done.12.refs_2_ = bf16[272,1024]{1,0:T(8,128)(2,1)S(1)} collective-permute-done((bf16[272,1024]{1,0:T(8,128)(2,1)}, bf16[272,1024]{1,0:T(8,128)(2,1)S(1)}, u32[]{:S(2)}, u32[]{:S(2)}) %collective-permute-start.12) | collective-permute-done | bytes 557088 | tf_op jit(solution)/shard_map/ppermute | solution.py:49
  99.8 20.3 %shard_map.172 = (bf16[8,256,1024]{2,1,0:T(8,128)(2,1)}, bf16[8,256,512]{2,1,0:T(8,128)(2,1)}, f32[8,8,256]{2,1,0:T(8,128)}, bf16[1024,768]{1,0:T(8,128)(2,1)}) custom-call(s32[2]{0:T(128)} %pad_add_fusion.1.index_ref, bf16[272,1024]{1,0:T(8,128)(2,1)} %get-tuple-element.196.refs_0_, bf16[272,1024]{1,0:T(8,128)(2,1)} %copy-done.24, ...), custom_call_target="tpu_custom_call" | custom-call | tf_op jit(solution)/shard_map/pallas_call | solution.py:74
  125.4 10.4 %shard_map.173.refs_2_ = bf16[1024,768]{1,0:T(8,128)(2,1)} custom-call(s32[4]{0:T(128)} %pad_add_fusion.after_ref.indices_ref, bf16[272,1024]{1,0:T(8,128)(2,1)} %get-tuple-element.196.refs_0_, bf16[272,1024]{1,0:T(8,128)(2,1)} %copy-done.24, bf16[272,1024]{1,0:T(8,128)(2,1)} %copy-done.25, bf16[272,1024]{1,0:T(8,128)(2,1)} %collective-permute-done.13.refs_3_, ...), custom_call_target="tpu_custom_call" | custom-call | tf_op jit(solution)/shard_map/pallas_call | solution.py:74
  135.8 26.2 %shard_map.174 = (bf16[8,256,1024]{2,1,0:T(8,128)(2,1)}, bf16[8,256,512]{2,1,0:T(8,128)(2,1)}, bf16[4,272,1024]{2,1,0:T(8,128)(2,1)}, bf16[4,272,1024]{2,1,0:T(8,128)(2,1)}) custom-call(s32[4]{0:T(128)} %pad_add_fusion.after_ref.indices_ref, bf16[272,1024]{1,0:T(8,128)(2,1)} %get-tuple-element.196.refs_0_, bf16[272,1024]{1,0:T(8,128)(2,1)} %copy-done.24, ...), custom_call_target="tpu_custom_call" | custom-call | tf_op jit(solution)/shard_map/pallas_call | solution.py:74
  175.5 9.7 %shard_map.177 = (bf16[4,256,1024]{2,1,0:T(8,128)(2,1)}, bf16[4,256,1024]{2,1,0:T(8,128)(2,1)}) custom-call(s32[4]{0:T(128)} %pad_add_fusion.after_ref.indices_ref, bf16[8,256,512]{2,1,0:T(8,128)(2,1)} %get-tuple-element.199.refs_11_.refs_0_, bf16[8,256,512]{2,1,0:T(8,128)(2,1)} %get-tuple-element.207.refs_1_.refs_11_, bf16[8,1024,512]{2,1,0:T(8,128)(2,1)} %refs_3_.1, ...), custom_call_target="tpu_custom_call" | custom-call | tf_op jit(solution)/shard_map/pallas_call | solution.py:74
  185.2 17.0 %shard_map.178 = (bf16[1024,768]{1,0:T(8,128)(2,1)}, bf16[1024,768]{1,0:T(8,128)(2,1)}) custom-call(s32[4]{0:T(128)} %pad_add_fusion.after_ref.indices_ref, bf16[272,1024]{1,0:T(8,128)(2,1)} %get-tuple-element.196.refs_0_, bf16[272,1024]{1,0:T(8,128)(2,1)} %copy-done.24, bf16[272,1024]{1,0:T(8,128)(2,1)} %copy-done.25, ...), custom_call_target="tpu_custom_call" | custom-call | tf_op jit(solution)/shard_map/pallas_call | solution.py:74
  211.9 26.3 %shard_map.180 = (f32[256,1024]{1,0:T(8,128)}, f32[256,1024]{1,0:T(8,128)}, bf16[256,1024]{1,0:T(8,128)(2,1)}, bf16[2,256,3200]{2,1,0:T(8,128)(2,1)}, bf16[2,256...) custom-call(s32[3]{0:T(128)} %pad_add_fusion.2.offsets_ref.out_offsets_ref, ...), custom_call_target="tpu_custom_call" | custom-call | tf_op jit(solution)/shard_map/pallas_call | solution.py:74
  258.7 31.6 %collective-permute-done.31.refs_1_ = bf16[1024,768]{1,0:T(8,128)(2,1)S(1)} collective-permute-done((bf16[1024,768]{1,0:T(8,128)(2,1)S(1)}, bf16[1024,768]{1,0:T(8,128)(2,1)S(1)}, u32[]{:S(2)}, u32[]{:S(2)}) %collective-permute-start.31) | collective-permute-done | bytes 1572896 | tf_op jit(solution)/shard_map/ppermute | solution.py:975
  304.3 35.7 %collective-permute-done.36.refs_0_ = bf16[1024,768]{1,0:T(8,128)(2,1)S(1)} collective-permute-done((bf16[1024,768]{1,0:T(8,128)(2,1)S(1)}, bf16[1024,768]{1,0:T(8,128)(2,1)S(1)}, u32[]{:S(2)}, u32[]{:S(2)}) %collective-permute-start.36) | collective-permute-done | bytes 1572896 | tf_op jit(solution)/shard_map/ppermute | solution.py:978
  354.1 5.4 %shard_map.184 = (f32[8,1024,1024]{2,1,0:T(8,128)}, f32[8,1024,512]{2,1,0:T(8,128)}) custom-call(s32[4]{0:T(128)S(1)} %get-tuple-element.359.experts_ref, bf16[2,1024,768]{2,1,0:T(8,128)(2,1)S(1)} %copy-done.9, bf16[2,1024,768]{2,1,0:T(8,128)(2,1)S(1)} %copy-done.11), custom_call_target="tpu_custom_call" | custom-call | tf_op jit(solution)/shard_map/pallas_call | solution.py:74
  359.5 16.0 %collective-permute-done.43.refs_7_ = bf16[2,256,1024]{2,1,0:T(8,128)(2,1)} collective-permute-done((bf16[2,256,1024]{2,1,0:T(8,128)(2,1)}, bf16[2,256,1024]{2,1,0:T(8,128)(2,1)}, u32[]{:S(2)}, u32[]{:S(2)}) %collective-permute-start.43) | collective-permute-done | bytes 1048608 | tf_op jit(solution)/shard_map/ppermute | solution.py:49
  375.6 10.6 %collective-permute-done.40.refs_0_ = bf16[1024,768]{1,0:T(8,128)(2,1)} collective-permute-done((bf16[1024,768]{1,0:T(8,128)(2,1)}, bf16[1024,768]{1,0:T(8,128)(2,1)}, u32[]{:S(2)}, u32[]{:S(2)}) %collective-permute-start.40) | collective-permute-done | bytes 1572896 | tf_op jit(solution)/shard_map/ppermute | solution.py:978
  396.2 7.0 %shard_map.186 = (f32[8,1024,1024]{2,1,0:T(8,128)}, f32[8,1024,512]{2,1,0:T(8,128)}) custom-call(s32[4]{0:T(128)S(1)} %get-tuple-element.359.experts_ref, bf16[2,1024,768]{2,1,0:T(8,128)(2,1)S(1)} %get-tuple-element.308.refs_0_, bf16[2,1024,768]{2,1,0:T(8,128)(2,1)} %collective-permute-done.49.refs_1_, ...), custom_call_target="tpu_custom_call", output_to_operand_aliasing={{0}: (3, {}), {1}: (4, {})} | custom-call | tf_op jit(solution)/shard_map/pallas_call | solution.py:74
  406.6 31.6 %collective-permute-done.47.refs_6_ = bf16[256,1024]{1,0:T(8,128)(2,1)S(1)} collective-permute-done((bf16[256,1024]{1,0:T(8,128)(2,1)S(1)}, bf16[256,1024]{1,0:T(8,128)(2,1)S(1)}, u32[]{:S(2)}, u32[]{:S(2)}) %collective-permute-start.47) | collective-permute-done | bytes 524320 | tf_op jit(solution)/shard_map/ppermute | solution.py:49
  443.6 5.4 %shard_map.189 = (f32[8,1024,1024]{2,1,0:T(8,128)}, f32[8,1024,512]{2,1,0:T(8,128)}) custom-call(s32[4]{0:T(128)S(1)} %get-tuple-element.358.experts_ref, bf16[2,1024,768]{2,1,0:T(8,128)(2,1)S(1)} %get-tuple-element.328.refs_0_, bf16[2,1024,768]{2,1,0:T(8,128)(2,1)S(1)} %collective-permute-done.52.refs_1_, ...), custom_call_target="tpu_custom_call", output_to_operand_aliasing={{0}: (3, {}), {1}: (4, {})} | custom-call | tf_op jit(solution)/shard_map/pallas_call | solution.py:74
  449.0 5.4 %shard_map.190 = (f32[8,1024,1024]{2,1,0:T(8,128)}, f32[8,1024,512]{2,1,0:T(8,128)}) custom-call(s32[4]{0:T(128)S(1)} %get-tuple-element.358.experts_ref, bf16[2,1024,768]{2,1,0:T(8,128)(2,1)S(1)} %get-tuple-element.334.refs_0_, bf16[2,1024,768]{2,1,0:T(8,128)(2,1)S(1)} %collective-permute-done.51.refs_1_, ...), custom_call_target="tpu_custom_call", output_to_operand_aliasing={{0}: (3, {}), {1}: (4, {})} | custom-call | tf_op jit(solution)/shard_map/pallas_call | solution.py:74
  454.5 24.2 %collective-permute-done.50.refs_1_ = bf16[256,3200]{1,0:T(8,128)(2,1)S(1)} collective-permute-done((bf16[256,3200]{1,0:T(8,128)(2,1)S(1)}, bf16[256,3200]{1,0:T(8,128)(2,1)S(1)}, u32[]{:S(2)}, u32[]{:S(2)}) %collective-permute-start.50) | collective-permute-done | bytes 1638432 | tf_op jit(solution)/shard_map/ppermute | solution.py:49
  484.4 5.6 %shard_map.192 = (f32[512,2048]{1,0:T(8,128)}, f32[512,1024]{1,0:T(8,128)}, f32[512,16]{1,0:T(8,128)}, f32[1,512]{1,0:T(1,128)}, f32[1,512]{1,0:T(1,128)}) custom-call(s32[2]{0:T(128)} %add_multiply_fusion.1.offsets_ref, bf16[1,256,3200]{2,1,0:T(8,128)(2,1)} %bitcast.31, bf16[1,256,3200]{2,1,0:T(8,128)(2,1)} %bitcast.33), custom_call_target="tpu_custom_call" | custom-call | tf_op jit(solution)/shard_map/pallas_call | solution.py:74
  (209 shorter events, 142.1 us)
Async XLA Ops:
  61.4 38.4 %collective-permute-start.18 = (bf16[4,256,1024]{2,1,0:T(8,128)(2,1)S(1)}, bf16[4,256,1024]{2,1,0:T(8,128)(2,1)}, u32[]{:S(2)}, u32[]{:S(2)}) collective-permute-start(bf16[4,256,1024]{2,1,0:T(8,128)(2,1)S(1)} %pad_maximum_fusion.refs_8_), channel_id=1, source_target_pairs={{0,2},{2,0},{1,3},{3,1},{4,6},{6,4},{5,7},{7,5},{8,10},{10,8},{9,1... | collective-permute-start | bytes 6291464 | tf_op jit(solution)/shard_map/ppermute | solution.py:49
  120.1 44.6 %collective-permute-start.20 = (bf16[1024,768]{1,0:T(8,128)(2,1)}, bf16[1024,768]{1,0:T(8,128)(2,1)}, u32[]{:S(2)}, u32[]{:S(2)}) collective-permute-start(bf16[1024,768]{1,0:T(8,128)(2,1)} %get-tuple-element.208.refs_0_), channel_id=1, source_target_pairs={{0,8},{24,16},{1,9},{25,17},{2,10},{26,18},{3,11},{27,19},{4,12},{... | collective-permute-start | bytes 4718600 | tf_op jit(solution)/shard_map/ppermute | solution.py:969
  162.1 40.1 %collective-permute-start.22 = (bf16[1024,768]{1,0:T(8,128)(2,1)S(1)}, bf16[1024,768]{1,0:T(8,128)(2,1)}, u32[]{:S(2)}, u32[]{:S(2)}) collective-permute-start(bf16[1024,768]{1,0:T(8,128)(2,1)S(1)} %copy-done.4), channel_id=1, source_target_pairs={{0,8},{24,16},{1,9},{25,17},{2,10},{26,18},{3,11},{27,19},{4,12},{... | collective-permute-start | bytes 4718600 | tf_op jit(solution)/shard_map/ppermute | solution.py:969
  171.7 40.3 %collective-permute-start.25 = (bf16[272,1024]{1,0:T(8,128)(2,1)}, bf16[272,1024]{1,0:T(8,128)(2,1)}, u32[]{:S(2)}, u32[]{:S(2)}) collective-permute-start(bf16[272,1024]{1,0:T(8,128)(2,1)} %get-tuple-element.213), channel_id=1, source_target_pairs={{0,4},{1,5},{4,0},{5,1},{2,6},{3,7},{6,2},{7,3},{8,12},{9,13},{12,... | collective-permute-start | bytes 1671176 | tf_op jit(solution)/shard_map/ppermute | solution.py:49
  173.0 38.9 %collective-permute-start.26 = (bf16[272,1024]{1,0:T(8,128)(2,1)}, bf16[272,1024]{1,0:T(8,128)(2,1)}, u32[]{:S(2)}, u32[]{:S(2)}) collective-permute-start(bf16[272,1024]{1,0:T(8,128)(2,1)} %get-tuple-element.214), channel_id=1, source_target_pairs={{0,1},{1,0},{4,5},{5,4},{2,3},{3,2},{6,7},{7,6},{8,9},{9,8},{12,13... | collective-permute-start | bytes 1671176 | tf_op jit(solution)/shard_map/ppermute | solution.py:49
  174.5 37.4 %collective-permute-start.27 = (bf16[272,1024]{1,0:T(8,128)(2,1)}, bf16[272,1024]{1,0:T(8,128)(2,1)}, u32[]{:S(2)}, u32[]{:S(2)}) collective-permute-start(bf16[272,1024]{1,0:T(8,128)(2,1)} %get-tuple-element.215), channel_id=1, source_target_pairs={{0,5},{1,4},{4,1},{5,0},{2,7},{3,6},{6,3},{7,2},{8,13},{9,12},{12,... | collective-permute-start | bytes 1671176 | tf_op jit(solution)/shard_map/ppermute | solution.py:49
  209.8 36.4 %collective-permute-start.23 = (bf16[1024,768]{1,0:T(8,128)(2,1)}, bf16[1024,768]{1,0:T(8,128)(2,1)S(1)}, u32[]{:S(2)}, u32[]{:S(2)}) collective-permute-start(bf16[1024,768]{1,0:T(8,128)(2,1)} %get-tuple-element.227), channel_id=1, source_target_pairs={{0,8},{8,0},{16,24},{24,16},{1,9},{9,1},{17,25},{25,17},{2,10},{10... | collective-permute-start | bytes 4718600 | tf_op jit(solution)/shard_map/ppermute | solution.py:975
  210.1 36.1 %collective-permute-start.24 = (bf16[1024,768]{1,0:T(8,128)(2,1)S(1)}, bf16[1024,768]{1,0:T(8,128)(2,1)}, u32[]{:S(2)}, u32[]{:S(2)}) collective-permute-start(bf16[1024,768]{1,0:T(8,128)(2,1)S(1)} %get-tuple-element.248.refs_3_), channel_id=1, source_target_pairs={{8,16},{16,8},{9,17},{17,9},{10,18},{18,10},{11,19},{19,11},{12,20... | collective-permute-start | bytes 4718600 | tf_op jit(solution)/shard_map/ppermute | solution.py:972
  252.1 40.6 %collective-permute-start.34 = (bf16[256,3200]{1,0:T(8,128)(2,1)S(1)}, bf16[256,3200]{1,0:T(8,128)(2,1)S(1)}, u32[]{:S(2)}, u32[]{:S(2)}) collective-permute-start(bf16[256,3200]{1,0:T(8,128)(2,1)S(1)} %get-tuple-element.260), channel_id=1, source_target_pairs={{0,1},{1,0},{2,3},{3,2},{4,5},{5,4},{6,7},{7,6},{8,9},{9,8},{10,11... | collective-permute-start | bytes 4915208 | tf_op jit(solution)/shard_map/ppermute | solution.py:49
  253.9 36.5 %collective-permute-start.31 = (bf16[1024,768]{1,0:T(8,128)(2,1)S(1)}, bf16[1024,768]{1,0:T(8,128)(2,1)S(1)}, u32[]{:S(2)}, u32[]{:S(2)}) collective-permute-start(bf16[1024,768]{1,0:T(8,128)(2,1)S(1)} %get-tuple-element.255), channel_id=1, source_target_pairs={{0,8},{8,0},{16,24},{24,16},{1,9},{9,1},{17,25},{25,17},{2,10},{10... | collective-permute-start | bytes 4718600 | tf_op jit(solution)/shard_map/ppermute | solution.py:975
  297.2 50.8 %collective-permute-start.44 = (bf16[2,1024,768]{2,1,0:T(8,128)(2,1)S(1)}, bf16[2,1024,768]{2,1,0:T(8,128)(2,1)S(1)}, u32[]{:S(2)}, u32[]{:S(2)}) collective-permute-start(bf16[2,1024,768]{2,1,0:T(8,128)(2,1)S(1)} %get-tuple-element.291.refs_0_), channel_id=1, source_target_pairs={{0,2},{2,0},{1,3},{3,1},{4,6},{6,4},{5,7},{7,5},{8,10},{10,8},{9,1... | collective-permute-start | bytes 9437192 | tf_op jit(solution)/shard_map/ppermute | solution.py:49
  297.2 43.1 %collective-permute-start.39 = (bf16[256,3200]{1,0:T(8,128)(2,1)S(1)}, bf16[256,3200]{1,0:T(8,128)(2,1)S(1)}, u32[]{:S(2)}, u32[]{:S(2)}) collective-permute-start(bf16[256,3200]{1,0:T(8,128)(2,1)S(1)} %get-tuple-element.285.refs_6_), channel_id=1, source_target_pairs={{0,8},{24,16},{1,9},{25,17},{2,10},{26,18},{3,11},{27,19},{4,12},{... | collective-permute-start | bytes 4915208 | tf_op jit(solution)/shard_map/ppermute | solution.py:969
  301.7 38.4 %collective-permute-start.36 = (bf16[1024,768]{1,0:T(8,128)(2,1)S(1)}, bf16[1024,768]{1,0:T(8,128)(2,1)S(1)}, u32[]{:S(2)}, u32[]{:S(2)}) collective-permute-start(bf16[1024,768]{1,0:T(8,128)(2,1)S(1)} %get-tuple-element.280.refs_1_), channel_id=1, source_target_pairs={{8,0},{16,24},{9,1},{17,25},{10,2},{18,26},{11,3},{19,27},{12,4},{... | collective-permute-start | bytes 4718600 | tf_op jit(solution)/shard_map/ppermute | solution.py:978
  303.0 37.1 %collective-permute-start.37 = (bf16[1024,768]{1,0:T(8,128)(2,1)S(1)}, bf16[1024,768]{1,0:T(8,128)(2,1)S(1)}, u32[]{:S(2)}, u32[]{:S(2)}) collective-permute-start(bf16[1024,768]{1,0:T(8,128)(2,1)S(1)} %get-tuple-element.281.refs_2_), channel_id=1, source_target_pairs={{8,16},{16,8},{9,17},{17,9},{10,18},{18,10},{11,19},{19,11},{12,20... | collective-permute-start | bytes 4718600 | tf_op jit(solution)/shard_map/ppermute | solution.py:972
  303.7 36.6 %collective-permute-start.38 = (bf16[1024,768]{1,0:T(8,128)(2,1)S(1)}, bf16[1024,768]{1,0:T(8,128)(2,1)S(1)}, u32[]{:S(2)}, u32[]{:S(2)}) collective-permute-start(bf16[1024,768]{1,0:T(8,128)(2,1)S(1)} %get-tuple-element.283.refs_4_), channel_id=1, source_target_pairs={{0,4},{4,0},{1,5},{5,1},{2,6},{6,2},{3,7},{7,3},{8,12},{12,8},{9,1... | collective-permute-start | bytes 4718600 | tf_op jit(solution)/shard_map/ppermute | solution.py:49
  344.3 41.9 %collective-permute-start.42 = (bf16[256,3200]{1,0:T(8,128)(2,1)}, bf16[256,3200]{1,0:T(8,128)(2,1)}, u32[]{:S(2)}, u32[]{:S(2)}) collective-permute-start(bf16[256,3200]{1,0:T(8,128)(2,1)} %get-tuple-element.299.refs_4_), channel_id=1, source_target_pairs={{8,16},{16,8},{9,17},{17,9},{10,18},{18,10},{11,19},{19,11},{12,20... | collective-permute-start | bytes 4915208 | tf_op jit(solution)/shard_map/ppermute | solution.py:972
  346.1 40.0 %collective-permute-start.40 = (bf16[1024,768]{1,0:T(8,128)(2,1)}, bf16[1024,768]{1,0:T(8,128)(2,1)}, u32[]{:S(2)}, u32[]{:S(2)}) collective-permute-start(bf16[1024,768]{1,0:T(8,128)(2,1)} %get-tuple-element.296.refs_1_), channel_id=1, source_target_pairs={{8,0},{16,24},{9,1},{17,25},{10,2},{18,26},{11,3},{19,27},{12,4},{... | collective-permute-start | bytes 4718600 | tf_op jit(solution)/shard_map/ppermute | solution.py:978
  347.4 38.8 %collective-permute-start.41 = (bf16[1024,768]{1,0:T(8,128)(2,1)}, bf16[1024,768]{1,0:T(8,128)(2,1)}, u32[]{:S(2)}, u32[]{:S(2)}) collective-permute-start(bf16[1024,768]{1,0:T(8,128)(2,1)} %get-tuple-element.297.refs_2_), channel_id=1, source_target_pairs={{0,4},{4,0},{1,5},{5,1},{2,6},{6,2},{3,7},{7,3},{8,12},{12,8},{9,1... | collective-permute-start | bytes 4718600 | tf_op jit(solution)/shard_map/ppermute | solution.py:49
  348.0 48.1 %collective-permute-start.49 = (bf16[2,1024,768]{2,1,0:T(8,128)(2,1)S(1)}, bf16[2,1024,768]{2,1,0:T(8,128)(2,1)}, u32[]{:S(2)}, u32[]{:S(2)}) collective-permute-start(bf16[2,1024,768]{2,1,0:T(8,128)(2,1)S(1)} %get-tuple-element.308.refs_0_), channel_id=1, source_target_pairs={{0,2},{2,0},{1,3},{3,1},{4,6},{6,4},{5,7},{7,5},{8,10},{10,8},{9,1... | collective-permute-start | bytes 9437192 | tf_op jit(solution)/shard_map/ppermute | solution.py:49
  391.4 46.8 %collective-permute-start.46 = (bf16[256,3200]{1,0:T(8,128)(2,1)S(1)}, bf16[256,3200]{1,0:T(8,128)(2,1)S(1)}, u32[]{:S(2)}, u32[]{:S(2)}) collective-permute-start(bf16[256,3200]{1,0:T(8,128)(2,1)S(1)} %get-tuple-element.317.refs_3_), channel_id=1, source_target_pairs={{8,0},{16,24},{9,1},{17,25},{10,2},{18,26},{11,3},{19,27},{12,4},{... | collective-permute-start | bytes 4915208 | tf_op jit(solution)/shard_map/ppermute | solution.py:978
  392.7 45.5 %collective-permute-start.45 = (bf16[1024,768]{1,0:T(8,128)(2,1)S(1)}, bf16[1024,768]{1,0:T(8,128)(2,1)S(1)}, u32[]{:S(2)}, u32[]{:S(2)}) collective-permute-start(bf16[1024,768]{1,0:T(8,128)(2,1)S(1)} %get-tuple-element.314.refs_0_), channel_id=1, source_target_pairs={{0,4},{4,0},{1,5},{5,1},{2,6},{6,2},{3,7},{7,3},{8,12},{12,8},{9,1... | collective-permute-start | bytes 4718600 | tf_op jit(solution)/shard_map/ppermute | solution.py:49
  394.6 43.6 %collective-permute-start.47 = (bf16[256,1024]{1,0:T(8,128)(2,1)S(1)}, bf16[256,1024]{1,0:T(8,128)(2,1)S(1)}, u32[]{:S(2)}, u32[]{:S(2)}) collective-permute-start(bf16[256,1024]{1,0:T(8,128)(2,1)S(1)} %get-tuple-element.306), channel_id=1, source_target_pairs={{0,4},{4,0},{1,5},{5,1},{2,6},{6,2},{3,7},{7,3},{8,12},{12,8},{9,1... | collective-permute-start | bytes 1572872 | tf_op jit(solution)/shard_map/ppermute | solution.py:49
  396.1 47.4 %collective-permute-start.52 = (bf16[2,1024,768]{2,1,0:T(8,128)(2,1)S(1)}, bf16[2,1024,768]{2,1,0:T(8,128)(2,1)S(1)}, u32[]{:S(2)}, u32[]{:S(2)}) collective-permute-start(bf16[2,1024,768]{2,1,0:T(8,128)(2,1)S(1)} %get-tuple-element.328.refs_0_), channel_id=1, source_target_pairs={{0,2},{2,0},{1,3},{3,1},{4,6},{6,4},{5,7},{7,5},{8,10},{10,8},{9,1... | collective-permute-start | bytes 9437192 | tf_op jit(solution)/shard_map/ppermute | solution.py:49
  440.5 38.2 %collective-permute-start.50 = (bf16[256,3200]{1,0:T(8,128)(2,1)S(1)}, bf16[256,3200]{1,0:T(8,128)(2,1)S(1)}, u32[]{:S(2)}, u32[]{:S(2)}) collective-permute-start(bf16[256,3200]{1,0:T(8,128)(2,1)S(1)} %get-tuple-element.340.refs_0_), channel_id=1, source_target_pairs={{0,4},{4,0},{1,5},{5,1},{2,6},{6,2},{3,7},{7,3},{8,12},{12,8},{9,1... | collective-permute-start | bytes 4915208 | tf_op jit(solution)/shard_map/ppermute | solution.py:49
  (68 other events, 1017.1 us)

commit v6 on v5

--- a/solution.py
+++ b/solution.py
@@ -763,13 +763,14 @@
     )
 
 
-def unpack(sources, offsets, rows):
+def unpack(sources, offsets, rows, others=()):
     count = sum(source.shape[0] for source in sources)
     deep, wide = sources[0].shape[1:]
     widths = (QW + 2 * KVW, D)
 
     def kernel(offsets_ref, *refs):
         source_refs, refs = refs[: len(sources)], refs[len(sources) :]
+        other_refs, refs = refs[: len(others)], refs[len(others) :]
         out_refs, router_ref, ffn_ref, attn_ref, values_ref, rest_ref, sems = refs[:2], *refs[2:]
         copies = []
         for i, source in enumerate([ref.at[i] for ref in source_refs for i in range(ref.shape[0])]):
@@ -777,7 +778,8 @@
 
             def rows_of(r, carry):
                 place = pl.ds(pl.multiple_of(r * some, some), some)
-                values_ref[i, place, :] = source[place, :].astype(f32)
+                value = source[place, :].astype(f32)
+                values_ref[i, place, :] = value + other_refs[i][0, place, :].astype(f32) if others else value
                 return carry
 
             lax.fori_loop(0, deep // some, rows_of, 0)
@@ -799,8 +801,8 @@
     return call(
         kernel,
         [array((rows, width), f32) for width in widths] + [array((rows, EXPERTS), f32)] + [array((1, rows), f32)] * 2,
-        [SCALARS] + [whole(v.shape) for v in sources],
-        (offsets, *sources),
+        [SCALARS] + [whole(v.shape) for v in (*sources, *others)],
+        (offsets, *sources, *others),
         out_specs=[STAY] * 2 + [whole((rows, EXPERTS))] + [whole((1, rows))] * 2,
         scratch=[
             pltpu.VMEM((count, deep, wide), f32),
@@ -1173,14 +1175,16 @@
         step_6, [two, (deep, wide), (rows_of, D), array((rows_of, D), f32)],
         full_3, side_3, out_w, total_w, residual, own_m, far_m, grad_own, grad_later,
     )
-    core_3, side_w = other_core(pair_3), other_side(full_w)
+    core_3, side_w, core_w = other_core(pair_3), other_side(full_w), other_core(full_w)
     grad_in = run(lambda grad: first_back(grad, grad_residual, hidden_in, gain_attn), grad_sum)
     outs = run(lambda pair, swap, outs: placed(pair, [swap], outs, 1, 0), pair_2, core_2, outs)
     outs = run(lambda pair, swap, outs: placed(pair, [swap], outs, 1, 1), pair_3, core_3, outs)
-    (sum_w,) = steps(lambda flag, w, far: (f(w) + f(far),), [(deep, wide)], full_w, side_w)
-    core_w = other_core(sum_w)
+    side_w, core_w = run(lambda *v: v, side_w, core_w)
+    both_w = other_core(side_w)
     at_w = jnp.stack([(core_at - core) % cores for core in range(cores)]).astype(jnp.int32) * deep
-    qkv_sum, out_sum, router_sum, ffn_sum, attn_sum = run(lambda *v: unpack([w[None] for w in v], at_w, deep * cores), sum_w, core_w)
+    qkv_sum, out_sum, router_sum, ffn_sum, attn_sum = run(
+        lambda *v: unpack([w[None] for w in v[:2]], at_w, deep * cores, [w[None] for w in v[2:]]), full_w, core_w, side_w, both_w
+    )
     return (
         layer_out,
         grad_in,

time: 493 us -> 493 us (level)
    pallas_call x9 -> x8, Pallas kernels: 28.8 us -> 27.8 us  [post(): pl.pallas_call(kernel, out_shape=list(outs), in_specs=[SCALARS] + [near]...]
    ppermute x39 -> x40, starting transfers between devices: 28.2 us -> 28.5 us  [turn(): return lax.ppermute(value, axes, pairs)]
    ppermute x39 -> x40, waiting for transfers between devices: 123 us -> 123 us  [turn(): return lax.ppermute(value, axes, pairs)]
    unnamed x78 -> x82, local copies, waits for them, and re-layouts: 17.9 us -> 17.9 us
  transfers between devices with their start and end apart: 54 -> 55, of which waited for: 23 -> 23; matrix products, arithmetic and copies ran while one was open for 2% -> 2% of each run, Pallas kernels for 33% -> 33%
where the time goes in v6:
time: 493 us; the launch traced here: 492 us
  waiting for transfers between devices  213 us (43%)
  Pallas kernels  191 us (39%)
  starting transfers between devices  57 us (12%)
  local copies, waits for them, and re-layouts  22.8 us (5%)
  other arithmetic  7.13 us (1%)
    pallas_call x15, Pallas kernels, call(): pl.pallas_call(kernel, out_shape=list(out_shape), grid_spec=spec, input_o...  163 us
    ppermute x40, waiting for transfers between devices, turn(): return lax.ppermute(value, axes, pairs)  123 us
    ppermute x3, waiting for transfers between devices, go_out(): return lax.ppermute(total, 'line', [(1, 0), (2, 3)])  46.3 us
    ppermute x2, waiting for transfers between devices, in_and_out(): return lax.ppermute(sent, 'line', [(0, 1), (1, 0), (2, 3), (3, 2)])  33.4 us
    ppermute x40, starting transfers between devices, turn(): return lax.ppermute(value, axes, pairs)  28.5 us
    pallas_call x8, Pallas kernels, post(): pl.pallas_call(kernel, out_shape=list(outs), in_specs=[SCALARS] + [near]...  27.8 us
    unnamed x82, local copies, waits for them, and re-layouts  17.9 us
    ppermute x3, starting transfers between devices, go_in(): return lax.ppermute(raw, 'line', [(0, 1), (3, 2)])  11.6 us
  transfers between devices with their start and end apart: 55, of which 23 were waited for; matrix products, arithmetic and copies ran while one was open for 2% of the time, Pallas kernels for 33%

profile of v6, /device:TPU:0, one launch (start us, length us, event | category | flops | bytes accessed | tf_op | source)
XLA Modules:
  0.0 491.6 jit_solution(5676216490142964122)
XLA Ops:
  8.3 9.0 %collective-permute-done.1.rest_1_.rest_23_ = bf16[128,2048]{1,0:T(8,128)(2,1)S(1)} collective-permute-done((bf16[128,2048]{1,0:T(8,128)(2,1)S(1)}, bf16[128,2048]{1,0:T(8,128)(2,1)S(1)}, u32[]{:S(2)}, u32[]{:S(2)}) %collective-permute-start.1) | collective-permute-done | bytes 524320 | tf_op jit(solution)/shard_map/ppermute | solution.py:49
  22.1 6.5 %collective-permute-done.prev_ref.rest_16_ = bf16[256,1024]{1,0:T(8,128)(2,1)S(1)} collective-permute-done((bf16[256,1024]{1,0:T(8,128)(2,1)}, bf16[256,1024]{1,0:T(8,128)(2,1)S(1)}, u32[]{:S(2)}, u32[]{:S(2)}) %collective-permute-start) | collective-permute-done | bytes 524320 | tf_op jit(solution)/shard_map/ppermute | solution.py:923
  43.3 6.7 %shard_map.169 = (bf16[256,1024]{1,0:T(8,128)(2,1)}, bf16[512,1024]{1,0:T(8,128)(2,1)}, bf16[512,1024]{1,0:T(8,128)(2,1)}) custom-call(s32[5]{0:T(128)} %stack.111.offsets_ref.qkv_offsets_ref, bf16[256,1024]{1,0:T(8,128)(2,1)} %copy-done.32, bf16[256,1024]{1,0:T(8,128)(2,1)} %hid_ref.1, f32[1,1024]{1,0:T(1,128)} %get-tuple-element.365.gain_ref, ...), custom_call_target="tpu_custom_call" | custom-call | tf_op jit(solution)/shard_map/pallas_call | solution.py:74
  50.4 8.6 %shard_map.170 = (bf16[256,1024]{1,0:T(8,128)(2,1)}, f32[512,128]{1,0:T(8,128)}) custom-call(s32[1]{0:T(128)} %bitcast.15.flag_ref, bf16[256,1024]{1,0:T(8,128)(2,1)} %get-tuple-element.186.q_ref.rest_10_, bf16[512,1024]{1,0:T(8,128)(2,1)} %get-tuple-element.187.kv_ref.rest_11_), custom_call_target="tpu_custom_call" | custom-call | tf_op jit(solution)/shard_map/pallas_call | solution.py:74
  63.8 5.2 %shard_map.171 = (f32[256,1024]{1,0:T(8,128)}, f32[256,128]{1,0:T(8,128)}, bf16[272,1024]{1,0:T(8,128)(2,1)}) custom-call(s32[3]{0:T(128)} %pad_add_fusion.2.offsets_ref.out_offsets_ref, bf16[256,1024]{1,0:T(8,128)(2,1)} %get-tuple-element.194.att_ref.rest_18_, bf16[256,1024]{1,0:T(8,128)(2,1)} %hid_ref.1, f32[1,1024]{1,0:T(1,128)} %get-tuple-element.364.gain_ref.rest_8_, ...), custom_call_target="tpu_custom_call" | custom-call | tf_op jit(solution)/shard_map/pallas_call | solution.py:74
  72.6 12.2 %collective-permute-done.11.refs_1_ = bf16[272,1024]{1,0:T(8,128)(2,1)S(1)} collective-permute-done((bf16[272,1024]{1,0:T(8,128)(2,1)}, bf16[272,1024]{1,0:T(8,128)(2,1)S(1)}, u32[]{:S(2)}, u32[]{:S(2)}) %collective-permute-start.11) | collective-permute-done | bytes 557088 | tf_op jit(solution)/shard_map/ppermute | solution.py:49
  84.8 11.9 %collective-permute-done.12.refs_2_ = bf16[272,1024]{1,0:T(8,128)(2,1)S(1)} collective-permute-done((bf16[272,1024]{1,0:T(8,128)(2,1)}, bf16[272,1024]{1,0:T(8,128)(2,1)S(1)}, u32[]{:S(2)}, u32[]{:S(2)}) %collective-permute-start.12) | collective-permute-done | bytes 557088 | tf_op jit(solution)/shard_map/ppermute | solution.py:49
  99.8 20.2 %shard_map.172 = (bf16[8,256,1024]{2,1,0:T(8,128)(2,1)}, bf16[8,256,512]{2,1,0:T(8,128)(2,1)}, f32[8,8,256]{2,1,0:T(8,128)}, bf16[1024,768]{1,0:T(8,128)(2,1)}) custom-call(s32[2]{0:T(128)} %pad_add_fusion.1.index_ref, bf16[272,1024]{1,0:T(8,128)(2,1)} %get-tuple-element.198.refs_0_, bf16[272,1024]{1,0:T(8,128)(2,1)} %copy-done.24, ...), custom_call_target="tpu_custom_call" | custom-call | tf_op jit(solution)/shard_map/pallas_call | solution.py:74
  125.2 10.3 %shard_map.173.refs_2_ = bf16[1024,768]{1,0:T(8,128)(2,1)} custom-call(s32[4]{0:T(128)} %pad_add_fusion.after_ref.indices_ref, bf16[272,1024]{1,0:T(8,128)(2,1)} %get-tuple-element.198.refs_0_, bf16[272,1024]{1,0:T(8,128)(2,1)} %copy-done.24, bf16[272,1024]{1,0:T(8,128)(2,1)} %copy-done.25, bf16[272,1024]{1,0:T(8,128)(2,1)} %collective-permute-done.13.refs_3_, ...), custom_call_target="tpu_custom_call" | custom-call | tf_op jit(solution)/shard_map/pallas_call | solution.py:74
  135.6 26.2 %shard_map.174 = (bf16[8,256,1024]{2,1,0:T(8,128)(2,1)}, bf16[8,256,512]{2,1,0:T(8,128)(2,1)}, bf16[4,272,1024]{2,1,0:T(8,128)(2,1)}, bf16[4,272,1024]{2,1,0:T(8,128)(2,1)}) custom-call(s32[4]{0:T(128)} %pad_add_fusion.after_ref.indices_ref, bf16[272,1024]{1,0:T(8,128)(2,1)} %get-tuple-element.198.refs_0_, bf16[272,1024]{1,0:T(8,128)(2,1)} %copy-done.24, ...), custom_call_target="tpu_custom_call" | custom-call | tf_op jit(solution)/shard_map/pallas_call | solution.py:74
  175.3 9.7 %shard_map.177 = (bf16[4,256,1024]{2,1,0:T(8,128)(2,1)}, bf16[4,256,1024]{2,1,0:T(8,128)(2,1)}) custom-call(s32[4]{0:T(128)} %pad_add_fusion.after_ref.indices_ref, bf16[8,256,512]{2,1,0:T(8,128)(2,1)} %get-tuple-element.201.refs_11_.refs_0_, bf16[8,256,512]{2,1,0:T(8,128)(2,1)} %get-tuple-element.209.refs_1_.refs_11_, bf16[8,1024,512]{2,1,0:T(8,128)(2,1)} %refs_3_.1, ...), custom_call_target="tpu_custom_call" | custom-call | tf_op jit(solution)/shard_map/pallas_call | solution.py:74
  185.0 17.0 %shard_map.178 = (bf16[1024,768]{1,0:T(8,128)(2,1)}, bf16[1024,768]{1,0:T(8,128)(2,1)}) custom-call(s32[4]{0:T(128)} %pad_add_fusion.after_ref.indices_ref, bf16[272,1024]{1,0:T(8,128)(2,1)} %get-tuple-element.198.refs_0_, bf16[272,1024]{1,0:T(8,128)(2,1)} %copy-done.24, bf16[272,1024]{1,0:T(8,128)(2,1)} %copy-done.25, ...), custom_call_target="tpu_custom_call" | custom-call | tf_op jit(solution)/shard_map/pallas_call | solution.py:74
  211.8 26.3 %shard_map.180 = (f32[256,1024]{1,0:T(8,128)}, f32[256,1024]{1,0:T(8,128)}, bf16[256,1024]{1,0:T(8,128)(2,1)}, bf16[2,256,3200]{2,1,0:T(8,128)(2,1)}, bf16[2,256...) custom-call(s32[3]{0:T(128)} %pad_add_fusion.2.offsets_ref.out_offsets_ref, ...), custom_call_target="tpu_custom_call" | custom-call | tf_op jit(solution)/shard_map/pallas_call | solution.py:74
  258.6 31.6 %collective-permute-done.31.refs_1_ = bf16[1024,768]{1,0:T(8,128)(2,1)S(1)} collective-permute-done((bf16[1024,768]{1,0:T(8,128)(2,1)S(1)}, bf16[1024,768]{1,0:T(8,128)(2,1)S(1)}, u32[]{:S(2)}, u32[]{:S(2)}) %collective-permute-start.31) | collective-permute-done | bytes 1572896 | tf_op jit(solution)/shard_map/ppermute | solution.py:977
  304.2 35.7 %collective-permute-done.36.refs_0_ = bf16[1024,768]{1,0:T(8,128)(2,1)S(1)} collective-permute-done((bf16[1024,768]{1,0:T(8,128)(2,1)S(1)}, bf16[1024,768]{1,0:T(8,128)(2,1)S(1)}, u32[]{:S(2)}, u32[]{:S(2)}) %collective-permute-start.36) | collective-permute-done | bytes 1572896 | tf_op jit(solution)/shard_map/ppermute | solution.py:980
  353.9 5.4 %shard_map.184 = (f32[8,1024,1024]{2,1,0:T(8,128)}, f32[8,1024,512]{2,1,0:T(8,128)}) custom-call(s32[4]{0:T(128)S(1)} %get-tuple-element.363.experts_ref, bf16[2,1024,768]{2,1,0:T(8,128)(2,1)S(1)} %copy-done.8, bf16[2,1024,768]{2,1,0:T(8,128)(2,1)S(1)} %copy-done.10), custom_call_target="tpu_custom_call" | custom-call | tf_op jit(solution)/shard_map/pallas_call | solution.py:74
  359.4 16.1 %collective-permute-done.43.refs_7_ = bf16[2,256,1024]{2,1,0:T(8,128)(2,1)} collective-permute-done((bf16[2,256,1024]{2,1,0:T(8,128)(2,1)}, bf16[2,256,1024]{2,1,0:T(8,128)(2,1)}, u32[]{:S(2)}, u32[]{:S(2)}) %collective-permute-start.43) | collective-permute-done | bytes 1048608 | tf_op jit(solution)/shard_map/ppermute | solution.py:49
  375.4 10.6 %collective-permute-done.40.refs_0_ = bf16[1024,768]{1,0:T(8,128)(2,1)} collective-permute-done((bf16[1024,768]{1,0:T(8,128)(2,1)}, bf16[1024,768]{1,0:T(8,128)(2,1)}, u32[]{:S(2)}, u32[]{:S(2)}) %collective-permute-start.40) | collective-permute-done | bytes 1572896 | tf_op jit(solution)/shard_map/ppermute | solution.py:980
  396.0 7.0 %shard_map.186 = (f32[8,1024,1024]{2,1,0:T(8,128)}, f32[8,1024,512]{2,1,0:T(8,128)}) custom-call(s32[4]{0:T(128)S(1)} %get-tuple-element.363.experts_ref, bf16[2,1024,768]{2,1,0:T(8,128)(2,1)S(1)} %get-tuple-element.310.refs_0_, bf16[2,1024,768]{2,1,0:T(8,128)(2,1)} %collective-permute-done.49.refs_1_, ...), custom_call_target="tpu_custom_call", output_to_operand_aliasing={{0}: (3, {}), {1}: (4, {})} | custom-call | tf_op jit(solution)/shard_map/pallas_call | solution.py:74
  406.4 31.6 %collective-permute-done.47.refs_6_ = bf16[256,1024]{1,0:T(8,128)(2,1)S(1)} collective-permute-done((bf16[256,1024]{1,0:T(8,128)(2,1)S(1)}, bf16[256,1024]{1,0:T(8,128)(2,1)S(1)}, u32[]{:S(2)}, u32[]{:S(2)}) %collective-permute-start.47) | collective-permute-done | bytes 524320 | tf_op jit(solution)/shard_map/ppermute | solution.py:49
  443.6 5.4 %shard_map.189 = (f32[8,1024,1024]{2,1,0:T(8,128)}, f32[8,1024,512]{2,1,0:T(8,128)}) custom-call(s32[4]{0:T(128)S(1)} %get-tuple-element.362.experts_ref, bf16[2,1024,768]{2,1,0:T(8,128)(2,1)S(1)} %get-tuple-element.330.refs_0_, bf16[2,1024,768]{2,1,0:T(8,128)(2,1)S(1)} %collective-permute-done.53.refs_1_, ...), custom_call_target="tpu_custom_call", output_to_operand_aliasing={{0}: (3, {}), {1}: (4, {})} | custom-call | tf_op jit(solution)/shard_map/pallas_call | solution.py:74
  449.1 5.4 %shard_map.190 = (f32[8,1024,1024]{2,1,0:T(8,128)}, f32[8,1024,512]{2,1,0:T(8,128)}) custom-call(s32[4]{0:T(128)S(1)} %get-tuple-element.362.experts_ref, bf16[2,1024,768]{2,1,0:T(8,128)(2,1)S(1)} %get-tuple-element.336.refs_0_, bf16[2,1024,768]{2,1,0:T(8,128)(2,1)S(1)} %collective-permute-done.52.refs_1_, ...), custom_call_target="tpu_custom_call", output_to_operand_aliasing={{0}: (3, {}), {1}: (4, {})} | custom-call | tf_op jit(solution)/shard_map/pallas_call | solution.py:74
  454.5 23.9 %collective-permute-done.50 = bf16[256,3200]{1,0:T(8,128)(2,1)S(1)} collective-permute-done((bf16[256,3200]{1,0:T(8,128)(2,1)S(1)}, bf16[256,3200]{1,0:T(8,128)(2,1)S(1)}, u32[]{:S(2)}, u32[]{:S(2)}) %collective-permute-start.50) | collective-permute-done | bytes 1638432 | tf_op jit(solution)/shard_map/ppermute | solution.py:49
  483.2 6.7 %shard_map.191 = (f32[512,2048]{1,0:T(8,128)}, f32[512,1024]{1,0:T(8,128)}, f32[512,16]{1,0:T(8,128)}, f32[1,512]{1,0:T(1,128)}, f32[1,512]{1,0:T(1,128)}) custom-call(s32[2]{0:T(128)} %add_multiply_fusion.1.offsets_ref, bf16[1,256,3200]{2,1,0:T(8,128)(2,1)} %bitcast.33, bf16[1,256,3200]{2,1,0:T(8,128)(2,1)} %bitcast.36, bf16[1,256,3200]{2,1,0:T(8,128)(2,1)} %bitcast.35, ...), custom_call_target="tpu_custom_call" | custom-call | tf_op jit(solution)/shard_map/pallas_call | solution.py:74
  (214 shorter events, 141.1 us)
Async XLA Ops:
  61.3 38.4 %collective-permute-start.18 = (bf16[4,256,1024]{2,1,0:T(8,128)(2,1)S(1)}, bf16[4,256,1024]{2,1,0:T(8,128)(2,1)}, u32[]{:S(2)}, u32[]{:S(2)}) collective-permute-start(bf16[4,256,1024]{2,1,0:T(8,128)(2,1)S(1)} %pad_maximum_fusion.refs_8_), channel_id=1, source_target_pairs={{0,2},{2,0},{1,3},{3,1},{4,6},{6,4},{5,7},{7,5},{8,10},{10,8},{9,1... | collective-permute-start | bytes 6291464 | tf_op jit(solution)/shard_map/ppermute | solution.py:49
  120.0 44.5 %collective-permute-start.20 = (bf16[1024,768]{1,0:T(8,128)(2,1)}, bf16[1024,768]{1,0:T(8,128)(2,1)}, u32[]{:S(2)}, u32[]{:S(2)}) collective-permute-start(bf16[1024,768]{1,0:T(8,128)(2,1)} %get-tuple-element.210.refs_0_), channel_id=1, source_target_pairs={{0,8},{24,16},{1,9},{25,17},{2,10},{26,18},{3,11},{27,19},{4,12},{... | collective-permute-start | bytes 4718600 | tf_op jit(solution)/shard_map/ppermute | solution.py:971
  162.0 40.0 %collective-permute-start.22 = (bf16[1024,768]{1,0:T(8,128)(2,1)S(1)}, bf16[1024,768]{1,0:T(8,128)(2,1)}, u32[]{:S(2)}, u32[]{:S(2)}) collective-permute-start(bf16[1024,768]{1,0:T(8,128)(2,1)S(1)} %copy-done.3), channel_id=1, source_target_pairs={{0,8},{24,16},{1,9},{25,17},{2,10},{26,18},{3,11},{27,19},{4,12},{... | collective-permute-start | bytes 4718600 | tf_op jit(solution)/shard_map/ppermute | solution.py:971
  171.5 40.3 %collective-permute-start.25 = (bf16[272,1024]{1,0:T(8,128)(2,1)}, bf16[272,1024]{1,0:T(8,128)(2,1)}, u32[]{:S(2)}, u32[]{:S(2)}) collective-permute-start(bf16[272,1024]{1,0:T(8,128)(2,1)} %get-tuple-element.215), channel_id=1, source_target_pairs={{0,4},{1,5},{4,0},{5,1},{2,6},{3,7},{6,2},{7,3},{8,12},{9,13},{12,... | collective-permute-start | bytes 1671176 | tf_op jit(solution)/shard_map/ppermute | solution.py:49
  172.9 38.9 %collective-permute-start.26 = (bf16[272,1024]{1,0:T(8,128)(2,1)}, bf16[272,1024]{1,0:T(8,128)(2,1)}, u32[]{:S(2)}, u32[]{:S(2)}) collective-permute-start(bf16[272,1024]{1,0:T(8,128)(2,1)} %get-tuple-element.216), channel_id=1, source_target_pairs={{0,1},{1,0},{4,5},{5,4},{2,3},{3,2},{6,7},{7,6},{8,9},{9,8},{12,13... | collective-permute-start | bytes 1671176 | tf_op jit(solution)/shard_map/ppermute | solution.py:49
  174.4 37.4 %collective-permute-start.27 = (bf16[272,1024]{1,0:T(8,128)(2,1)}, bf16[272,1024]{1,0:T(8,128)(2,1)}, u32[]{:S(2)}, u32[]{:S(2)}) collective-permute-start(bf16[272,1024]{1,0:T(8,128)(2,1)} %get-tuple-element.217), channel_id=1, source_target_pairs={{0,5},{1,4},{4,1},{5,0},{2,7},{3,6},{6,3},{7,2},{8,13},{9,12},{12,... | collective-permute-start | bytes 1671176 | tf_op jit(solution)/shard_map/ppermute | solution.py:49
  209.6 36.4 %collective-permute-start.23 = (bf16[1024,768]{1,0:T(8,128)(2,1)}, bf16[1024,768]{1,0:T(8,128)(2,1)S(1)}, u32[]{:S(2)}, u32[]{:S(2)}) collective-permute-start(bf16[1024,768]{1,0:T(8,128)(2,1)} %get-tuple-element.229), channel_id=1, source_target_pairs={{0,8},{8,0},{16,24},{24,16},{1,9},{9,1},{17,25},{25,17},{2,10},{10... | collective-permute-start | bytes 4718600 | tf_op jit(solution)/shard_map/ppermute | solution.py:977
  251.9 40.6 %collective-permute-start.34 = (bf16[256,3200]{1,0:T(8,128)(2,1)S(1)}, bf16[256,3200]{1,0:T(8,128)(2,1)S(1)}, u32[]{:S(2)}, u32[]{:S(2)}) collective-permute-start(bf16[256,3200]{1,0:T(8,128)(2,1)S(1)} %get-tuple-element.262), channel_id=1, source_target_pairs={{0,1},{1,0},{2,3},{3,2},{4,5},{5,4},{6,7},{7,6},{8,9},{9,8},{10,11... | collective-permute-start | bytes 4915208 | tf_op jit(solution)/shard_map/ppermute | solution.py:49
  253.7 36.5 %collective-permute-start.31 = (bf16[1024,768]{1,0:T(8,128)(2,1)S(1)}, bf16[1024,768]{1,0:T(8,128)(2,1)S(1)}, u32[]{:S(2)}, u32[]{:S(2)}) collective-permute-start(bf16[1024,768]{1,0:T(8,128)(2,1)S(1)} %get-tuple-element.257), channel_id=1, source_target_pairs={{0,8},{8,0},{16,24},{24,16},{1,9},{9,1},{17,25},{25,17},{2,10},{10... | collective-permute-start | bytes 4718600 | tf_op jit(solution)/shard_map/ppermute | solution.py:977
  297.0 50.9 %collective-permute-start.44 = (bf16[2,1024,768]{2,1,0:T(8,128)(2,1)S(1)}, bf16[2,1024,768]{2,1,0:T(8,128)(2,1)S(1)}, u32[]{:S(2)}, u32[]{:S(2)}) collective-permute-start(bf16[2,1024,768]{2,1,0:T(8,128)(2,1)S(1)} %get-tuple-element.293.refs_0_), channel_id=1, source_target_pairs={{0,2},{2,0},{1,3},{3,1},{4,6},{6,4},{5,7},{7,5},{8,10},{10,8},{9,1... | collective-permute-start | bytes 9437192 | tf_op jit(solution)/shard_map/ppermute | solution.py:49
  297.0 43.1 %collective-permute-start.39 = (bf16[256,3200]{1,0:T(8,128)(2,1)S(1)}, bf16[256,3200]{1,0:T(8,128)(2,1)S(1)}, u32[]{:S(2)}, u32[]{:S(2)}) collective-permute-start(bf16[256,3200]{1,0:T(8,128)(2,1)S(1)} %get-tuple-element.287.refs_6_), channel_id=1, source_target_pairs={{0,8},{24,16},{1,9},{25,17},{2,10},{26,18},{3,11},{27,19},{4,12},{... | collective-permute-start | bytes 4915208 | tf_op jit(solution)/shard_map/ppermute | solution.py:971
  301.5 38.4 %collective-permute-start.36 = (bf16[1024,768]{1,0:T(8,128)(2,1)S(1)}, bf16[1024,768]{1,0:T(8,128)(2,1)S(1)}, u32[]{:S(2)}, u32[]{:S(2)}) collective-permute-start(bf16[1024,768]{1,0:T(8,128)(2,1)S(1)} %get-tuple-element.282.refs_1_), channel_id=1, source_target_pairs={{8,0},{16,24},{9,1},{17,25},{10,2},{18,26},{11,3},{19,27},{12,4},{... | collective-permute-start | bytes 4718600 | tf_op jit(solution)/shard_map/ppermute | solution.py:980
  302.8 37.1 %collective-permute-start.37 = (bf16[1024,768]{1,0:T(8,128)(2,1)S(1)}, bf16[1024,768]{1,0:T(8,128)(2,1)S(1)}, u32[]{:S(2)}, u32[]{:S(2)}) collective-permute-start(bf16[1024,768]{1,0:T(8,128)(2,1)S(1)} %get-tuple-element.283.refs_2_), channel_id=1, source_target_pairs={{8,16},{16,8},{9,17},{17,9},{10,18},{18,10},{11,19},{19,11},{12,20... | collective-permute-start | bytes 4718600 | tf_op jit(solution)/shard_map/ppermute | solution.py:974
  303.6 36.6 %collective-permute-start.38 = (bf16[1024,768]{1,0:T(8,128)(2,1)S(1)}, bf16[1024,768]{1,0:T(8,128)(2,1)S(1)}, u32[]{:S(2)}, u32[]{:S(2)}) collective-permute-start(bf16[1024,768]{1,0:T(8,128)(2,1)S(1)} %get-tuple-element.285.refs_4_), channel_id=1, source_target_pairs={{0,4},{4,0},{1,5},{5,1},{2,6},{6,2},{3,7},{7,3},{8,12},{12,8},{9,1... | collective-permute-start | bytes 4718600 | tf_op jit(solution)/shard_map/ppermute | solution.py:49
  344.1 41.9 %collective-permute-start.42 = (bf16[256,3200]{1,0:T(8,128)(2,1)}, bf16[256,3200]{1,0:T(8,128)(2,1)}, u32[]{:S(2)}, u32[]{:S(2)}) collective-permute-start(bf16[256,3200]{1,0:T(8,128)(2,1)} %get-tuple-element.301.refs_4_), channel_id=1, source_target_pairs={{8,16},{16,8},{9,17},{17,9},{10,18},{18,10},{11,19},{19,11},{12,20... | collective-permute-start | bytes 4915208 | tf_op jit(solution)/shard_map/ppermute | solution.py:974
  346.0 40.0 %collective-permute-start.40 = (bf16[1024,768]{1,0:T(8,128)(2,1)}, bf16[1024,768]{1,0:T(8,128)(2,1)}, u32[]{:S(2)}, u32[]{:S(2)}) collective-permute-start(bf16[1024,768]{1,0:T(8,128)(2,1)} %get-tuple-element.298.refs_1_), channel_id=1, source_target_pairs={{8,0},{16,24},{9,1},{17,25},{10,2},{18,26},{11,3},{19,27},{12,4},{... | collective-permute-start | bytes 4718600 | tf_op jit(solution)/shard_map/ppermute | solution.py:980
  347.3 38.7 %collective-permute-start.41 = (bf16[1024,768]{1,0:T(8,128)(2,1)}, bf16[1024,768]{1,0:T(8,128)(2,1)}, u32[]{:S(2)}, u32[]{:S(2)}) collective-permute-start(bf16[1024,768]{1,0:T(8,128)(2,1)} %get-tuple-element.299.refs_2_), channel_id=1, source_target_pairs={{0,4},{4,0},{1,5},{5,1},{2,6},{6,2},{3,7},{7,3},{8,12},{12,8},{9,1... | collective-permute-start | bytes 4718600 | tf_op jit(solution)/shard_map/ppermute | solution.py:49
  347.9 48.1 %collective-permute-start.49 = (bf16[2,1024,768]{2,1,0:T(8,128)(2,1)S(1)}, bf16[2,1024,768]{2,1,0:T(8,128)(2,1)}, u32[]{:S(2)}, u32[]{:S(2)}) collective-permute-start(bf16[2,1024,768]{2,1,0:T(8,128)(2,1)S(1)} %get-tuple-element.310.refs_0_), channel_id=1, source_target_pairs={{0,2},{2,0},{1,3},{3,1},{4,6},{6,4},{5,7},{7,5},{8,10},{10,8},{9,1... | collective-permute-start | bytes 9437192 | tf_op jit(solution)/shard_map/ppermute | solution.py:49
  391.2 46.8 %collective-permute-start.46 = (bf16[256,3200]{1,0:T(8,128)(2,1)S(1)}, bf16[256,3200]{1,0:T(8,128)(2,1)S(1)}, u32[]{:S(2)}, u32[]{:S(2)}) collective-permute-start(bf16[256,3200]{1,0:T(8,128)(2,1)S(1)} %get-tuple-element.319.refs_3_), channel_id=1, source_target_pairs={{8,0},{16,24},{9,1},{17,25},{10,2},{18,26},{11,3},{19,27},{12,4},{... | collective-permute-start | bytes 4915208 | tf_op jit(solution)/shard_map/ppermute | solution.py:980
  392.5 45.5 %collective-permute-start.45 = (bf16[1024,768]{1,0:T(8,128)(2,1)S(1)}, bf16[1024,768]{1,0:T(8,128)(2,1)S(1)}, u32[]{:S(2)}, u32[]{:S(2)}) collective-permute-start(bf16[1024,768]{1,0:T(8,128)(2,1)S(1)} %get-tuple-element.316.refs_0_), channel_id=1, source_target_pairs={{0,4},{4,0},{1,5},{5,1},{2,6},{6,2},{3,7},{7,3},{8,12},{12,8},{9,1... | collective-permute-start | bytes 4718600 | tf_op jit(solution)/shard_map/ppermute | solution.py:49
  394.4 43.6 %collective-permute-start.47 = (bf16[256,1024]{1,0:T(8,128)(2,1)S(1)}, bf16[256,1024]{1,0:T(8,128)(2,1)S(1)}, u32[]{:S(2)}, u32[]{:S(2)}) collective-permute-start(bf16[256,1024]{1,0:T(8,128)(2,1)S(1)} %get-tuple-element.308), channel_id=1, source_target_pairs={{0,4},{4,0},{1,5},{5,1},{2,6},{6,2},{3,7},{7,3},{8,12},{12,8},{9,1... | collective-permute-start | bytes 1572872 | tf_op jit(solution)/shard_map/ppermute | solution.py:49
  396.0 47.6 %collective-permute-start.53 = (bf16[2,1024,768]{2,1,0:T(8,128)(2,1)S(1)}, bf16[2,1024,768]{2,1,0:T(8,128)(2,1)S(1)}, u32[]{:S(2)}, u32[]{:S(2)}) collective-permute-start(bf16[2,1024,768]{2,1,0:T(8,128)(2,1)S(1)} %get-tuple-element.330.refs_0_), channel_id=1, source_target_pairs={{0,2},{2,0},{1,3},{3,1},{4,6},{6,4},{5,7},{7,5},{8,10},{10,8},{9,1... | collective-permute-start | bytes 9437192 | tf_op jit(solution)/shard_map/ppermute | solution.py:49
  440.2 38.2 %collective-permute-start.50 = (bf16[256,3200]{1,0:T(8,128)(2,1)S(1)}, bf16[256,3200]{1,0:T(8,128)(2,1)S(1)}, u32[]{:S(2)}, u32[]{:S(2)}) collective-permute-start(bf16[256,3200]{1,0:T(8,128)(2,1)S(1)} %get-tuple-element.344), channel_id=1, source_target_pairs={{0,4},{4,0},{1,5},{5,1},{2,6},{6,2},{3,7},{7,3},{8,12},{12,8},{9,1... | collective-permute-start | bytes 4915208 | tf_op jit(solution)/shard_map/ppermute | solution.py:49
  440.8 37.7 %collective-permute-start.51 = (bf16[256,3200]{1,0:T(8,128)(2,1)S(1)}, bf16[256,3200]{1,0:T(8,128)(2,1)S(1)}, u32[]{:S(2)}, u32[]{:S(2)}) collective-permute-start(bf16[256,3200]{1,0:T(8,128)(2,1)S(1)} %get-tuple-element.344), channel_id=1, source_target_pairs={{0,2},{2,0},{1,3},{3,1},{4,6},{6,4},{5,7},{7,5},{8,10},{10,8},{9,1... | collective-permute-start | bytes 4915208 | tf_op jit(solution)/shard_map/ppermute | solution.py:49
  (71 other events, 1060.7 us)
